TPU v7x, 32 devices: a whole 2x2x4 slice. The times are simulated.
32 devices in a mesh: grp: 2 (over y), leaf: 16 (over z, x, core).
Axes of the slice: x: 2, y: 2, z: 4, core: 2. Of those that a mesh axis runs over, the one named last changes fastest.
Arguments:
- vectors: float32 [16, 32768], P(None, ('grp', 'leaf')), may hold values from -6 to 6
- points: float32 [3, 32768], P(None, ('grp', 'leaf')), may hold values from -1 to 2
- near_lists: int32 [64, 6], P(('grp', 'leaf')), may hold values from -1 to 5, as said below
- inter_lists: int32 [64, 16], P(('grp', 'leaf')), may hold values from 0 to 31, as said below
- skeleton: int32 [64, 64], P(('grp', 'leaf')), may hold values from 0 to 511, as said below
- interp: float32 [64, 64, 512], P(('grp', 'leaf')), may hold values from -0.25 to 0.25
- transfer: float32 [64, 64, 128], P(('grp', 'leaf')), may hold values from -0.125 to 0.125
- coarse_points: float32 [2, 3, 128], replicated, may hold values from 0 to 1
Outputs:
- filtered: float32 [16, 32768], P(None, ('grp', 'leaf'))
Inputs may be any that keep to these rules, and one draw needn't show every extreme that they name: `near_lists`: place w of leaf l's window is leaf (l // 2 - 1) * 2 + w. Slot 0 holds the leaf itself (2 + l % 2); the next slots hold distinct places of other leaves of the same subtree; then -1 to the end of the row. `inter_lists`: distinct leaves of the leaf's own subtree, numbered from the subtree's first leaf, none in the leaf's window. `skeleton`: distinct places within the leaf.
All inputs are finite; a program needn't handle non-finite values.
Results may differ from a plain program's by a relative error of at most 0.00013.
Values sent between devices are 32-bit elements; how exact they have to be, the bound alone decides.
No kernel may reach another device: no remote copies, remote signals or barrier semaphores. Data moves between devices by JAX's collectives and lax.ppermute only.
A program may use at most 64 MiB of HBM per device.

v0:
```python
import jax
import jax.numpy as jnp
from jax import lax
from jax.sharding import PartitionSpec as P

kappa_scale = 3.4641016151377544
centre = 0.05
half_width = 0.05
highest = lax.Precision.HIGHEST


def with_halo(x, sides, width):
    for axis, dim in sides:
        devices, length = (lax.axis_size(axis), x.shape[dim])
        up = [(i, (i + 1) % devices) for i in range(devices - 1)]
        down = [(j, i) for i, j in up]
        last = lax.slice_in_dim(x, length - width, length, axis=dim)
        initial = lax.slice_in_dim(x, 0, width, axis=dim)
        before = lax.ppermute(last, axis, up)
        after = lax.ppermute(initial, axis, down)
        x = jnp.concatenate([before, x, after], axis=dim)
    return x


def matern(source, target):
    delta_x = source[..., 0, :, None] - target[..., 0, None, :]
    delta_y = source[..., 1, :, None] - target[..., 1, None, :]
    delta_z = source[..., 2, :, None] - target[..., 2, None, :]
    scaled = kappa_scale * jnp.sqrt(delta_x * delta_x + delta_y * delta_y + delta_z * delta_z)
    return (1.0 + scaled) * jnp.exp(-scaled)


def on_device(vectors, points, near_lists, inter_lists, skeleton, interp, transfer, coarse_points):
    per_dev = near_lists.shape[0]
    slot_count = near_lists.shape[1]
    leaf_size = interp.shape[2]
    vec_count = vectors.shape[0]
    leaf_index = lax.axis_index("leaf")
    group_index = lax.axis_index("grp")
    group_count = lax.axis_size("grp")
    leaf_points = points.reshape(3, per_dev, leaf_size).transpose(1, 0, 2)
    skel_points = jnp.take_along_axis(leaf_points, skeleton[:, None, :], axis=2)
    subtree_skel = lax.all_gather(skel_points, "leaf", axis=0, tiled=True)
    own_coarse = lax.dynamic_index_in_dim(coarse_points, group_index, 0, keepdims=False)
    apart = (jnp.arange(group_count) != group_index).astype(jnp.float32)
    coupling = matern(coarse_points, own_coarse[None]) * apart[:, None, None]
    live_slots = jnp.max(jnp.sum((near_lists >= 0).astype(jnp.int32), axis=1))
    first_leaf = leaf_index * per_dev
    subtree_lists = lax.all_gather(inter_lists, "leaf", axis=0, tiled=True)
    own_ids = first_leaf + jnp.arange(per_dev, dtype=jnp.int32)
    hits = jnp.sum(
        (subtree_lists[:, :, None] == own_ids[None, None, :]).astype(jnp.float32), axis=1
    )
    push_kernel = matern(skel_points[None], subtree_skel[:, None]) * hits[:, :, None, None]

    def operate(field):
        stacked = jnp.concatenate([points, field], axis=0)
        window = with_halo(stacked, (("leaf", 1),), per_dev * leaf_size)
        window_points = window[:3].reshape(3, 3 * per_dev, leaf_size)
        window_vecs = window[3:].reshape(vec_count, 3 * per_dev, leaf_size)

        def near_slot(slot, running):
            chosen = lax.dynamic_index_in_dim(near_lists, slot, 1, keepdims=False)
            present = (chosen >= 0).astype(jnp.float32)
            safe_place = jnp.where(chosen >= 0, chosen, 0)
            source_points = jnp.take(window_points, safe_place, axis=1).transpose(1, 0, 2)
            source_vecs = jnp.take(window_vecs, safe_place, axis=1)
            kernel = matern(source_points, leaf_points)
            product = jnp.einsum("vlp,lpq->lvq", source_vecs, kernel, precision=highest)
            return running + present[:, None, None] * product

        near_part = lax.fori_loop(
            0, live_slots, near_slot, jnp.zeros((per_dev, vec_count, leaf_size), jnp.float32)
        )
        leaf_vecs = field.reshape(vec_count, per_dev, leaf_size)
        coeffs = jnp.einsum("vlp,lrp->lvr", leaf_vecs, interp, precision=highest)
        leaf_far = lax.psum_scatter(
            jnp.einsum("jvr,tjrq->tvq", coeffs, push_kernel, precision=highest),
            "leaf",
            scatter_dimension=0,
            tiled=True,
        )
        upward = jnp.einsum("lvr,lrc->vc", coeffs, transfer, precision=highest)
        subtree_total = lax.psum(upward, "leaf")
        group_coeffs = lax.all_gather(subtree_total[None], "grp", axis=0, tiled=True)
        coarse_field = jnp.einsum("avr,arq->vq", group_coeffs, coupling, precision=highest)
        downward = leaf_far + jnp.einsum("vc,lrc->lvr", coarse_field, transfer, precision=highest)
        far_part = jnp.einsum("lvr,lrp->lvp", downward, interp, precision=highest)
        combined = (near_part + far_part) / (leaf_size * slot_count)
        return combined.transpose(1, 0, 2).reshape(vec_count, per_dev * leaf_size)

    term_one = (operate(vectors) - centre * vectors) / half_width
    term_two = 2.0 * (operate(term_one) - centre * term_one) / half_width - vectors
    term_three = 2.0 * (operate(term_two) - centre * term_two) / half_width - term_one
    squares = lax.psum(jnp.sum(term_three * term_three, axis=1), ("grp", "leaf"))
    total_points = vectors.shape[1] * group_count * lax.axis_size("leaf")
    return term_three / jnp.sqrt(squares / total_points + 1e-06)[:, None]


def solution(mesh):
    placed = (
        P(None, ("grp", "leaf")),
        P(None, ("grp", "leaf")),
        P(("grp", "leaf"), None),
        P(("grp", "leaf"), None),
        P(("grp", "leaf"), None),
        P(("grp", "leaf"), None, None),
        P(("grp", "leaf"), None, None),
        P(),
    )
    return jax.shard_map(
        on_device, mesh=mesh, in_specs=placed, out_specs=P(None, ("grp", "leaf")), check_vma=False
    )
```

profile of v0, /device:TPU:0, one launch (start us, length us, event | category | flops | bytes accessed | tf_op | source)
XLA Modules:
  0.0 311.9 jit_solution(3287674258489741425)
XLA Ops:
  6.5 0.9 pad_maximum_fusion.3
  7.5 1.4 collective-permute-start.1
  8.9 3.0 collective-permute-start
  11.9 0.9 copy.61
  13.0 1.2 gather_fusion.6
  14.4 23.1 %all-gather = s32[16,2,16]{2,1,0:T(2,128)S(1)} all-gather(s32[1,2,16]{2,1,0:T(2,128)S(1)} %bitcast.260), channel_id=1, replica_groups=mesh['grp'=2,'leaf'=16] {'leaf'}, dimensions={0}, use_global_device_ids=true | all-gather | bytes 2176 | tf_op jit(solution)/shard_map/all_gather | solution.py:49
  37.7 17.6 %all_gather.15 = f32[32,3,64]{2,1,0:T(4,128)S(1)} all-gather(f32[2,3,64]{2,1,0:T(4,128)S(1)} %bitcast_select_fusion.1), channel_id=1, replica_groups=mesh['grp'=2,'leaf'=16] {'leaf'}, dimensions={0}, use_global_device_ids=true | all-gather | bytes 26112 | tf_op jit(solution)/shard_map/all_gather | solution.py:43
  55.7 3.5 %convolution_bitcast_fusion.2 = f32[32,16,64]{2,1,0:T(8,128)} fusion(f32[32,2]{1,0:T(8,128)S(1)} %copy.67, f32[32,64]{1,0:T(8,128)S(1)} %bitcast.254, f32[2,64]{1,0:T(2,128)S(1)} %bitcast.264, f32[32,64]{1,0:T(8,128)S(1)} %bitcast.257, f32[2,64]{1,0:T(2,128)S(1)} %bitcast.267, f32[32,64]{1,0:T(8,128)S(1)} %bitcast.251, f32[2,64]{1,0:T(2,128)S(1)} %bitcast.261, ...), kind=kOutput, calls=%fused_computation.145 | convolution fusion | flops 53739520 | bytes 165632 | tf_op jit(solution)/shard_map/jvr,tjrq->tvq/dot_general | solution.py:78
  60.2 31.6 %psum.28 = f32[1,16,128]{2,1,0:T(8,128)S(1)} all-reduce(f32[1,16,128]{2,1,0:T(8,128)S(1)} %convolution_bitcast_fusion.8), channel_id=1, replica_groups=mesh['grp'=2,'leaf'=16] {'leaf'}, use_global_device_ids=true, to_apply=%region_6.9 | all-reduce | flops 2048 | bytes 16384 | tf_op jit(solution)/shard_map/psum | solution.py:84
  91.9 4.4 %all_gather.17 = f32[2,16,128]{2,1,0:T(8,128)S(1)} all-gather(f32[1,16,128]{2,1,0:T(8,128)S(1)} %psum.28), channel_id=1, replica_groups=mesh['grp'=2,'leaf'=16] {'grp'}, dimensions={0}, use_global_device_ids=true | all-gather | bytes 24576 | tf_op jit(solution)/shard_map/all_gather | solution.py:85
  96.7 0.6 reduce_max.9
  97.5 19.3 %while.30 = (s32[]{:T(128)}, f32[2,16,512]{2,1,0:T(8,128)S(1)}, s32[]{:T(128)}, s32[2,6]{0,1:T(8,128)S(1)}, f32[16,6,512]{2,0,1:T(8,128)S(1)}, /*index=5*/f32[3,...) while((s32[]{:T(128)}, f32[2,16,512]{2,1,0:T(8,128)S(1)}, s32[]{:T(128)}, ...), condition=%wide.region_3.0_spmd, body=%wide.region_2.0_spmd.sunk | while | flops 107008024 | bytes 479441 | solution.py:72
  98.1 0.6 gather_fusion
  99.4 2.8 fusion.199
  102.8 0.6 gather_fusion
  104.1 2.8 fusion.199
  107.5 0.6 gather_fusion
  108.7 2.8 fusion.199
  112.1 0.6 gather_fusion
  113.4 2.8 fusion.199
  116.8 0.9 fusion.116
  118.1 1.3 collective-permute-start.3
  119.4 8.9 %collective-permute-start.2 = (f32[19,1024]{1,0:T(8,128)S(1)}, f32[19,1024]{1,0:T(8,128)S(1)}, u32[]{:S(2)}, u32[]{:S(2)}) collective-permute-start(f32[19,1024]{1,0:T(8,128)S(1)} %pad_maximum_fusion.4), channel_id=1, source_target_pairs={{0,1},{1,2},{2,3},{3,4},{4,5},{5,6},{6,7},{7,8},{8,9},{9,10},{10,1... | collective-permute-start | bytes 233480 | tf_op jit(solution)/shard_map/ppermute | solution.py:19
  128.7 3.5 %convolution_bitcast_fusion.1 = f32[32,16,64]{2,1,0:T(8,128)} fusion(f32[32,2]{1,0:T(8,128)S(1)} %copy.67, f32[32,64]{1,0:T(8,128)S(1)} %bitcast.255, f32[2,64]{1,0:T(2,128)S(1)} %bitcast.265, f32[32,64]{1,0:T(8,128)S(1)} %bitcast.258, f32[2,64]{1,0:T(2,128)S(1)} %bitcast.268, f32[32,64]{1,0:T(8,128)S(1)} %bitcast.252, f32[2,64]{1,0:T(2,128)S(1)} %bitcast.262, ...), kind=kOutput, calls=%fused_computation.144 | convolution fusion | flops 53739520 | bytes 165632 | tf_op jit(solution)/shard_map/jvr,tjrq->tvq/dot_general | solution.py:78
  132.4 31.8 %psum.29 = f32[1,16,128]{2,1,0:T(8,128)S(1)} all-reduce(f32[1,16,128]{2,1,0:T(8,128)S(1)} %convolution_bitcast_fusion.7), channel_id=1, replica_groups=mesh['grp'=2,'leaf'=16] {'leaf'}, use_global_device_ids=true, to_apply=%region_10.13 | all-reduce | flops 2048 | bytes 16384 | tf_op jit(solution)/shard_map/psum | solution.py:84
  164.2 4.4 %all_gather.18 = f32[2,16,128]{2,1,0:T(8,128)S(1)} all-gather(f32[1,16,128]{2,1,0:T(8,128)S(1)} %psum.29), channel_id=1, replica_groups=mesh['grp'=2,'leaf'=16] {'grp'}, dimensions={0}, use_global_device_ids=true | all-gather | bytes 24576 | tf_op jit(solution)/shard_map/all_gather | solution.py:85
  169.1 19.4 %while.31 = (s32[]{:T(128)}, f32[2,16,512]{2,1,0:T(8,128)S(1)}, s32[]{:T(128)}, s32[2,6]{0,1:T(8,128)S(1)}, f32[16,6,512]{2,0,1:T(8,128)S(1)}, /*index=5*/f32[3,...) while((s32[]{:T(128)}, f32[2,16,512]{2,1,0:T(8,128)S(1)}, s32[]{:T(128)}, ...), condition=%wide.region_8.11_spmd, body=%wide.region_7.10_spmd.sunk | while | flops 107008024 | bytes 479441 | solution.py:72
  169.9 0.6 gather_fusion.2
  171.1 2.8 fusion.203
  174.6 0.6 gather_fusion.2
  175.8 2.8 fusion.203
  179.2 0.6 gather_fusion.2
  180.5 2.8 fusion.203
  185.2 2.8 fusion.203
  188.6 0.9 fusion.115
  189.9 1.3 collective-permute-start.5
  191.2 9.1 %collective-permute-start.4 = (f32[19,1024]{1,0:T(8,128)S(1)}, f32[19,1024]{1,0:T(8,128)S(1)}, u32[]{:S(2)}, u32[]{:S(2)}) collective-permute-start(f32[19,1024]{1,0:T(8,128)S(1)} %pad_maximum_fusion.5), channel_id=1, source_target_pairs={{0,1},{1,2},{2,3},{3,4},{4,5},{5,6},{6,7},{7,8},{8,9},{9,10},{10,1... | collective-permute-start | bytes 233480 | tf_op jit(solution)/shard_map/ppermute | solution.py:19
  200.6 3.4 %convolution_bitcast_fusion = f32[32,16,64]{2,1,0:T(8,128)} fusion(f32[32,2]{1,0:T(8,128)S(1)} %copy.67, f32[32,64]{1,0:T(8,128)S(1)} %bitcast.256, f32[2,64]{1,0:T(2,128)S(1)} %bitcast.266, f32[32,64]{1,0:T(8,128)S(1)} %bitcast.259, f32[2,64]{1,0:T(2,128)S(1)} %bitcast.269, f32[32,64]{1,0:T(8,128)S(1)} %bitcast.253, f32[2,64]{1,0:T(2,128)S(1)} %bitcast.263, ...), kind=kOutput, calls=%fused_computation.143 | convolution fusion | flops 53739520 | bytes 165632 | tf_op jit(solution)/shard_map/jvr,tjrq->tvq/dot_general | solution.py:78
  204.3 31.8 %psum.30 = f32[1,16,128]{2,1,0:T(8,128)S(1)} all-reduce(f32[1,16,128]{2,1,0:T(8,128)S(1)} %convolution_bitcast_fusion.6), channel_id=1, replica_groups=mesh['grp'=2,'leaf'=16] {'leaf'}, use_global_device_ids=true, to_apply=%region_14.17 | all-reduce | flops 2048 | bytes 16384 | tf_op jit(solution)/shard_map/psum | solution.py:84
  236.2 4.4 %all_gather.19 = f32[2,16,128]{2,1,0:T(8,128)S(1)} all-gather(f32[1,16,128]{2,1,0:T(8,128)S(1)} %psum.30), channel_id=1, replica_groups=mesh['grp'=2,'leaf'=16] {'grp'}, dimensions={0}, use_global_device_ids=true | all-gather | bytes 24576 | tf_op jit(solution)/shard_map/all_gather | solution.py:85
  241.0 19.3 %while.32 = (s32[]{:T(128)}, f32[2,16,512]{2,1,0:T(8,128)S(1)}, s32[]{:T(128)}, s32[2,6]{0,1:T(8,128)S(1)}, f32[16,6,512]{2,0,1:T(8,128)S(1)}, /*index=5*/f32[3,...) while((s32[]{:T(128)}, f32[2,16,512]{2,1,0:T(8,128)S(1)}, s32[]{:T(128)}, ...), condition=%wide.region_12.15_spmd, body=%wide.region_11.14_spmd.sunk | while | flops 107008024 | bytes 479441 | solution.py:72
  242.9 2.8 fusion.207
  247.6 2.8 fusion.207
  252.2 2.8 fusion.207
  256.9 2.8 fusion.207
  260.3 0.9 fusion.114
  261.7 42.9 %psum.31 = f32[16]{0:T(128)S(1)} all-reduce(f32[16]{0:T(128)S(1)} %multiply_reduce_fusion), channel_id=1, replica_groups=mesh['grp'=2,'leaf'=16] {'grp','leaf'}, use_global_device_ids=true, to_apply=%region_16.19 | all-reduce | flops 16 | bytes 128 | tf_op jit(solution)/shard_map/psum | solution.py:95
  304.6 0.7 broadcast_divide_fusion
  (174 shorter events, 16.4 us)
Async XLA Ops:
  6.5 48.8 %copy-start = (f32[2,64,512]{2,1,0:T(8,128)S(1)}, f32[2,64,512]{2,1,0:T(8,128)}, u32[]{:S(2)}) copy-start(f32[2,64,512]{2,1,0:T(8,128)} %param.23) | copy-start | bytes 786436
  6.5 6.4 %copy-start.7 = (s32[2,64]{1,0:T(2,128)S(1)}, s32[2,64]{1,0:T(2,128)}, u32[]{:S(2)}) copy-start(s32[2,64]{1,0:T(2,128)} %param.22) | copy-start | bytes 1540
  6.5 7.8 %copy-start.5 = (s32[2,16]{1,0:T(2,128)S(1)}, s32[2,16]{1,0:T(2,128)}, u32[]{:S(2)}) copy-start(s32[2,16]{1,0:T(2,128)} %param.21) | copy-start | bytes 388
  6.5 110.3 %reduce-scatter.4.cloned.1.call-start = ((), (), s32[]{:S(2)}) async-start(), calls=%async_computation.3 | async-start | bytes 278528 | tf_op jit(solution)/shard_map/reduce_scatter | solution.py:77
  7.5 47.9 %copy-start.2 = (f32[16,1024]{1,0:T(8,128)S(1)}, f32[16,1024]{1,0:T(8,128)}, u32[]{:S(2)}) copy-start(f32[16,1024]{1,0:T(8,128)} %param.18) | copy-start | bytes 196612
  7.5 89.9 %collective-permute-start.1 = (f32[19,1024]{1,0:T(8,128)S(1)}, f32[19,1024]{1,0:T(8,128)S(1)}, u32[]{:S(2)}, u32[]{:S(2)}) collective-permute-start(f32[19,1024]{1,0:T(8,128)S(1)} %pad_maximum_fusion.3), channel_id=1, source_target_pairs={{1,0},{2,1},{3,2},{4,3},{5,4},{6,5},{7,6},{8,7},{9,8},{10,9},{11,1... | collective-permute-start | bytes 233480 | tf_op jit(solution)/shard_map/ppermute | solution.py:20
  8.9 88.5 %collective-permute-start = (f32[19,1024]{1,0:T(8,128)S(1)}, f32[19,1024]{1,0:T(8,128)S(1)}, u32[]{:S(2)}, u32[]{:S(2)}) collective-permute-start(f32[19,1024]{1,0:T(8,128)S(1)} %pad_maximum_fusion.3), channel_id=1, source_target_pairs={{0,1},{1,2},{2,3},{3,4},{4,5},{5,6},{6,7},{7,8},{8,9},{9,10},{10,1... | collective-permute-start | bytes 233480 | tf_op jit(solution)/shard_map/ppermute | solution.py:19
  59.2 0.7 copy-start.6
  59.2 0.9 copy-start.1
  59.2 37.1 %copy-start.4 = (f32[2,3,128]{2,0,1:T(2,128)S(1)}, f32[2,3,128]{2,0,1:T(2,128)}, u32[]{:S(2)}) copy-start(f32[2,3,128]{2,0,1:T(2,128)} %param.25) | copy-start | bytes 9220
  59.2 38.2 %copy-start.3 = (f32[3,1024]{1,0:T(4,128)S(1)}, f32[3,1024]{1,0:T(4,128)}, u32[]{:S(2)}) copy-start(f32[3,1024]{1,0:T(4,128)} %param.19) | copy-start | bytes 36868
  59.2 129.4 %reduce-scatter.6.cloned.1.call-start = ((), (), s32[]{:S(2)}) async-start(), calls=%async_computation.4 | async-start | bytes 278528 | tf_op jit(solution)/shard_map/reduce_scatter | solution.py:77
  118.1 50.8 %collective-permute-start.3 = (f32[19,1024]{1,0:T(8,128)S(1)}, f32[19,1024]{1,0:T(8,128)S(1)}, u32[]{:S(2)}, u32[]{:S(2)}) collective-permute-start(f32[19,1024]{1,0:T(8,128)S(1)} %pad_maximum_fusion.4), channel_id=1, source_target_pairs={{1,0},{2,1},{3,2},{4,3},{5,4},{6,5},{7,6},{8,7},{9,8},{10,9},{11,1... | collective-permute-start | bytes 233480 | tf_op jit(solution)/shard_map/ppermute | solution.py:20
  119.4 49.6 %collective-permute-start.2 = (f32[19,1024]{1,0:T(8,128)S(1)}, f32[19,1024]{1,0:T(8,128)S(1)}, u32[]{:S(2)}, u32[]{:S(2)}) collective-permute-start(f32[19,1024]{1,0:T(8,128)S(1)} %pad_maximum_fusion.4), channel_id=1, source_target_pairs={{0,1},{1,2},{2,3},{3,4},{4,5},{5,6},{6,7},{7,8},{8,9},{9,10},{10,1... | collective-permute-start | bytes 233480 | tf_op jit(solution)/shard_map/ppermute | solution.py:19
  132.4 127.9 %reduce-scatter.8.cloned.1.call-start = ((), (), s32[]{:S(2)}) async-start(), calls=%async_computation.5 | async-start | bytes 278528 | tf_op jit(solution)/shard_map/reduce_scatter | solution.py:77
  189.9 51.0 %collective-permute-start.5 = (f32[19,1024]{1,0:T(8,128)S(1)}, f32[19,1024]{1,0:T(8,128)S(1)}, u32[]{:S(2)}, u32[]{:S(2)}) collective-permute-start(f32[19,1024]{1,0:T(8,128)S(1)} %pad_maximum_fusion.5), channel_id=1, source_target_pairs={{1,0},{2,1},{3,2},{4,3},{5,4},{6,5},{7,6},{8,7},{9,8},{10,9},{11,1... | collective-permute-start | bytes 233480 | tf_op jit(solution)/shard_map/ppermute | solution.py:20
  191.2 49.7 %collective-permute-start.4 = (f32[19,1024]{1,0:T(8,128)S(1)}, f32[19,1024]{1,0:T(8,128)S(1)}, u32[]{:S(2)}, u32[]{:S(2)}) collective-permute-start(f32[19,1024]{1,0:T(8,128)S(1)} %pad_maximum_fusion.5), channel_id=1, source_target_pairs={{0,1},{1,2},{2,3},{3,4},{4,5},{5,6},{6,7},{7,8},{8,9},{9,10},{10,1... | collective-permute-start | bytes 233480 | tf_op jit(solution)/shard_map/ppermute | solution.py:19
Sparse Core Ops, SparseCore 0:
  59.3 54.1 reduce-scatter.3
  132.5 54.3 reduce-scatter.5
  204.5 54.4 reduce-scatter.7
where the time goes:
time: 313 us; the launch traced here: 312 us
  blocking collectives  192 us (61%)
  matrix products  49.9 us (16%)
  starting transfers between devices  25.2 us (8%)
  local copies, waits for them, and re-layouts  17.3 us (6%)
  between operations  13.7 us (4%)
  loops' own time  9.74 us (3%)
  other arithmetic  3.93 us (1%)
    psum x3, blocking collectives, operate(): subtree_total = lax.psum(upward, 'leaf')  95.2 us
    psum x1, blocking collectives, on_device(): lax.psum(jnp.sum(term_three * term_three, axis=1), ('grp', 'leaf'))  42.9 us
    dot_general x12, matrix products, near_slot(): product = jnp.einsum('vlp,lpq->lvq', source_vecs, kernel, precision=highest)  33.3 us
    all_gather x1, blocking collectives, on_device(): subtree_lists = lax.all_gather(inter_lists, 'leaf', axis=0, tiled=True)  23.1 us
    ppermute x3, starting transfers between devices, with_halo(): before = lax.ppermute(last, axis, up)  21.1 us
    all_gather x1, blocking collectives, on_device(): subtree_skel = lax.all_gather(skel_points, 'leaf', axis=0, tiled=True)  17.6 us
    all_gather x3, blocking collectives, operate(): lax.all_gather(subtree_total[None], 'grp', axis=0, tiled=True)  13.1 us
    dot_general x3, matrix products, operate(): jnp.einsum('jvr,tjrq->tvq', coeffs, push_kernel, precision=highest)  10.4 us
  transfers between devices with their start and end apart: 9, of which 0 were waited for; matrix products, arithmetic and copies ran while one was open for 21% of the time, Pallas kernels for 0%

commit v1 on v0

v1 whole, which is shorter than its diff:
```python
import jax
import jax.numpy as jnp
from jax import lax
from jax.experimental import pallas as pl
from jax.experimental.pallas import tpu as pltpu
from jax.sharding import PartitionSpec as P

kappa_scale = 3.4641016151377544
log2_e = 1.4426950408889634
centre = 0.05
half_width = 0.05
highest = lax.Precision.HIGHEST
f32 = jnp.float32
bf16 = jnp.bfloat16

VMEM = pl.BlockSpec(memory_space=pltpu.VMEM)
SMEM = pl.BlockSpec(memory_space=pltpu.SMEM)
POINT_ROWS = 8


def split(x):
    hi = x.astype(bf16)
    return hi, (x - hi.astype(f32)).astype(bf16)


def dot3(left, right_hi, right_lo):
    rows = left.shape[0]
    hi, lo = split(left)
    both = jnp.dot(jnp.concatenate([hi, lo], axis=0), right_hi, preferred_element_type=f32)
    return both[:rows] + both[rows:] + jnp.dot(hi, right_lo, preferred_element_type=f32)


def dot_nt(left, right):
    return lax.dot_general(
        left, right, (((1,), (1,)), ((), ())), precision=highest, preferred_element_type=f32
    )


def matern(columns, rows):
    square = None
    for column, row in zip(columns, rows, strict=True):
        delta = column - row
        square = delta * delta if square is None else square + delta * delta
    scaled = square * lax.rsqrt(jnp.maximum(square, 1e-30))
    return (1.0 + scaled) * jnp.exp2(scaled * -log2_e)


def call(kernel, out_shape, in_specs, scratch=(), flops=0, limit=24, **kw):
    return pl.pallas_call(
        kernel,
        out_shape=out_shape,
        in_specs=in_specs,
        out_specs=jax.tree.map(lambda _: VMEM, out_shape),
        scratch_shapes=scratch,
        compiler_params=pltpu.CompilerParams(vmem_limit_bytes=limit << 20),
        cost_estimate=pl.CostEstimate(flops=flops, bytes_accessed=1 << 20, transcendentals=0),
        **kw,
    )


def base_place(kind, odd, per_dev):
    if kind == "own":
        return per_dev
    right = odd == (0 if kind == "pair" else 1)
    return jnp.where(right, 2 * per_dev, 0)


def near_kernel(kind, first, sizes):
    per_dev, leaf_size, vec, slots = sizes

    def body(*refs):
        refs = list(refs)
        lists, meta = refs[:2]
        own = refs[2]
        source = own if kind == "own" else refs[3]
        refs = refs[3:] if kind == "own" else refs[4:]
        if first:
            if kind != "own":
                acc, out, k_hi, k_lo, cols = refs
            else:
                acc, (out, k_hi, k_lo, cols) = None, refs
        else:
            if kind != "own":
                k_hi, k_lo, acc, out = refs
            else:
                acc, (k_hi, k_lo, out) = None, refs
        base = base_place(kind, lax.rem(meta[0], 2), per_dev)
        out[...] = jnp.zeros_like(out) if acc is None else acc[...]
        for j in range(per_dev):
            here = slice(j * leaf_size, (j + 1) * leaf_size)
            if first:
                cols[...] = (source[vec : vec + POINT_ROWS, here] * kappa_scale).T
            hits = []
            for leaf in range(per_dev):
                hit = lists[leaf, 0] == base + j
                for slot in range(1, slots):
                    hit = jnp.logical_or(hit, lists[leaf, slot] == base + j)
                hits.append(hit)
            for leaf in range(per_dev):
                there = slice(leaf * leaf_size, (leaf + 1) * leaf_size)

                @pl.when(hits[leaf])
                def _():
                    if first:
                        rows = [
                            own[vec + d : vec + d + 1, there] * kappa_scale for d in range(3)
                        ]
                        step = 32

                        def chunk(i, _):
                            at = pl.ds(pl.multiple_of(i * step, step), step)
                            columns = [cols[at, d : d + 1] for d in range(3)]
                            hi, lo = split(matern(columns, rows))
                            k_hi[j, at, there] = hi
                            k_lo[j, at, there] = lo
                            return 0

                        lax.fori_loop(0, leaf_size // step, chunk, 0, unroll=2)
                    out[:, there] += dot3(source[:vec, here], k_hi[j, :, there], k_lo[j, :, there])

    return body


def send_parts(out, coeffs, upward, meta, groups, leaves):
    group = meta[1]
    for i in range(leaves):
        out[group * leaves + i, : coeffs.shape[0]] = coeffs
    for t in range(1, groups):
        other = lax.rem(group + t, groups)
        for i in range(leaves):
            out[other * leaves + i, : upward.shape[0]] = upward


def coefficients(field, interp, transfer):
    per_dev, _, leaf_size = interp.shape
    parts = [
        dot_nt(field[:, j * leaf_size : (j + 1) * leaf_size], interp[j]) for j in range(per_dev)
    ]
    coeffs = jnp.concatenate(parts, axis=1)
    upward = jnp.dot(coeffs, transfer[...], precision=highest, preferred_element_type=f32)
    return coeffs, upward


def on_device(vectors, points, near_lists, inter_lists, skeleton, interp, transfer, coarse_points):
    per_dev, slots = near_lists.shape
    rank, leaf_size = interp.shape[1:]
    coarse = transfer.shape[2]
    vec, width = vectors.shape
    leaves, groups = lax.axis_size("leaf"), lax.axis_size("grp")
    devices = leaves * groups
    cols = per_dev * rank
    assert cols == coarse
    leaf_index, group_index = lax.axis_index("leaf"), lax.axis_index("grp")
    meta = jnp.stack([leaf_index, group_index]).astype(jnp.int32)
    transfer = transfer.reshape(cols, coarse)
    inner = [(i, i ^ 1) for i in range(leaves)]
    outer = [(i, i + 1) for i in range(1, leaves - 1, 2)]
    outer = outer + [(j, i) for i, j in outer]
    exchange = lambda x: lax.all_to_all(x, ("grp", "leaf"), 0, 0, tiled=True)
    sizes = (per_dev, leaf_size, vec, slots)
    shape = jax.ShapeDtypeStruct
    near_shape = shape((vec, width), f32)
    k_shape = shape((per_dev, leaf_size, width), bf16)

    stacked = jnp.concatenate(
        [vectors, points, jnp.zeros((POINT_ROWS - 3, width), f32)], axis=0
    )
    pair_window = lax.ppermute(stacked, "leaf", inner)
    next_window = lax.ppermute(stacked, "leaf", outer)

    def start_body(meta, field, skel, interp, transfer, out):
        coeffs, upward = coefficients(field[:vec], interp, transfer)
        spots = []
        for j in range(per_dev):
            places = lax.broadcasted_iota(jnp.int32, (leaf_size, rank), 0)
            pick = (places == skel[j : j + 1, :]).astype(f32)
            spots.append(
                jnp.dot(
                    field[vec:, j * leaf_size : (j + 1) * leaf_size],
                    pick,
                    precision=highest,
                    preferred_element_type=f32,
                )
            )
        spot = jnp.concatenate(spots, axis=1)
        own = jnp.concatenate([coeffs, spot], axis=0)
        send_parts(out, own, upward, meta, groups, leaves)

    payload = call(
        start_body,
        shape((devices, vec + POINT_ROWS, cols), f32),
        [SMEM, VMEM, VMEM, VMEM, VMEM],
        flops=10**7,
    )(meta, stacked, skeleton, interp, transfer)
    received = exchange(payload)

    near, own_hi, own_lo = call(
        near_kernel("own", True, sizes),
        (near_shape, k_shape, k_shape),
        [SMEM, SMEM, VMEM],
        scratch=[pltpu.VMEM((leaf_size, POINT_ROWS), f32)],
        flops=10**10,
    )(near_lists, meta, stacked)

    def couple_body(meta, coarse_points, transfer, out_hi, out_lo):
        group = meta[1]
        mine = coarse_points[group] * kappa_scale
        rows = [mine[d : d + 1] for d in range(3)]
        for t in range(1, groups):
            far = (coarse_points[lax.rem(group + t, groups)] * kappa_scale).T
            kernel = matern([far[:, d : d + 1] for d in range(3)], rows)
            at = slice((t - 1) * coarse, t * coarse)
            out_hi[at], out_lo[at] = split(dot_nt(kernel, transfer[...]))

    couple_shape = shape(((groups - 1) * coarse, cols), bf16)
    padded_coarse = jnp.pad(coarse_points, ((0, 0), (0, POINT_ROWS - 3), (0, 0)))
    couple_hi, couple_lo = call(
        couple_body, (couple_shape, couple_shape), [SMEM, VMEM, VMEM], flops=10**8
    )(meta, padded_coarse, transfer)

    def near_first(kind, window, acc):
        return call(
            near_kernel(kind, True, sizes),
            (near_shape, k_shape, k_shape),
            [SMEM, SMEM, VMEM, VMEM, VMEM],
            scratch=[pltpu.VMEM((leaf_size, POINT_ROWS), f32)],
            flops=10**10,
        )(near_lists, meta, stacked, window, acc)

    near, pair_hi, pair_lo = near_first("pair", pair_window, near)
    near, next_hi, next_lo = near_first("next", next_window, near)

    def far_body(lists, meta, received, out_hi, out_lo, marks):
        group, leaf = meta[1], meta[0]
        mine = received[group * leaves + leaf][vec:] * kappa_scale
        rows = [mine[d : d + 1] for d in range(3)]
        for m in range(leaves * per_dev):
            for j in range(per_dev):
                marks[m, j] = 0.0
        for j in range(per_dev):
            for s in range(lists.shape[1]):
                marks[lists[j, s], j] = 1.0
        lane_leaf = lax.broadcasted_iota(jnp.int32, (1, cols), 1) // rank

        def block(i, _):
            spots = (received[group * leaves + i][vec:] * kappa_scale).T
            for h in range(per_dev):
                part = spots[h * rank : (h + 1) * rank]
                kernel = matern([part[:, d : d + 1] for d in range(3)], rows)
                mark = jnp.zeros((1, cols), f32)
                for j in range(per_dev):
                    mark = jnp.where(lane_leaf == j, marks[i * per_dev + h, j], mark)
                at = pl.ds(pl.multiple_of((i * per_dev + h) * rank, rank), rank)
                hi, lo = split(kernel * mark)
                out_hi[at] = hi
                out_lo[at] = lo
            return 0

        lax.fori_loop(0, leaves, block, 0)

    far_shape = shape((leaves * cols, cols), bf16)
    far_hi, far_lo = call(
        far_body,
        (far_shape, far_shape),
        [SMEM, SMEM, VMEM],
        scratch=[pltpu.SMEM((leaves * per_dev, per_dev), f32)],
        flops=10**9,
    )(inter_lists, meta, received)

    def post_body(step, meta, received, far_hi, far_lo, couple_hi, couple_lo, near, *rest):
        if step == 1:
            field, interp, transfer, out, send = rest
        elif step == 2:
            field, before, interp, transfer, out, send = rest
        else:
            field, before, interp, out, send = rest
        group = meta[1]
        coeffs = jnp.concatenate(
            [received[group * leaves + i, :vec] for i in range(leaves)], axis=1
        )
        down = dot3(coeffs, far_hi[...], far_lo[...])
        totals = []
        for t in range(1, groups):
            first = lax.rem(group + t, groups) * leaves
            parts = [received[first + i, :vec] for i in range(leaves)]
            while len(parts) > 1:
                parts = [sum(parts[i : i + 2]) for i in range(0, len(parts), 2)]
            totals.append(parts[0])
        if totals:
            down = down + dot3(jnp.concatenate(totals, axis=1), couple_hi[...], couple_lo[...])
        news = []
        for j in range(per_dev):
            here = slice(j * leaf_size, (j + 1) * leaf_size)
            far = jnp.dot(
                down[:, j * rank : (j + 1) * rank],
                interp[j],
                precision=highest,
                preferred_element_type=f32,
            )
            applied = (near[:, here] + far) * (1.0 / (leaf_size * slots))
            term = (applied - centre * field[:vec, here]) * (1.0 / half_width)
            if step > 1:
                term = 2.0 * term - before[:vec, here]
            out[:, here] = term
            news.append(term)
        if step < 3:
            coeffs, upward = coefficients(jnp.concatenate(news, axis=1), interp, transfer)
            send_parts(send, coeffs, upward, meta, groups, leaves)
        else:
            squares = None
            for term in news:
                part = jnp.sum(term * term, axis=1, keepdims=True)
                squares = part if squares is None else squares + part
            diagonal = lax.broadcasted_iota(jnp.int32, (vec, 128), 0) == lax.broadcasted_iota(
                jnp.int32, (vec, 128), 1
            )
            row = jnp.sum(jnp.where(diagonal, squares, 0.0), axis=0, keepdims=True)
            for i in range(devices):
                send[i] = row

    def post(step, received, near, *rest):
        send_shape = (devices, vec, cols) if step < 3 else (devices, 1, 128)
        return call(
            lambda *refs: post_body(step, *refs),
            (near_shape, shape(send_shape, f32)),
            [SMEM] + [VMEM] * (6 + len(rest)),
            flops=10**8,
        )(meta, received, far_hi, far_lo, couple_hi, couple_lo, near, *rest)

    def near_again(field):
        pair_field = lax.ppermute(field, "leaf", inner)
        next_field = lax.ppermute(field, "leaf", outer)
        near = call(
            near_kernel("own", False, sizes), near_shape, [SMEM, SMEM, VMEM, VMEM, VMEM],
            flops=10**9,
        )(near_lists, meta, field, own_hi, own_lo)
        for kind, window, hi, lo in (
            ("pair", pair_field, pair_hi, pair_lo),
            ("next", next_field, next_hi, next_lo),
        ):
            near = call(
                near_kernel(kind, False, sizes),
                near_shape,
                [SMEM, SMEM, VMEM, VMEM, VMEM, VMEM, VMEM],
                flops=10**9,
            )(near_lists, meta, field, window, hi, lo, near)
        return near

    term_one, payload = post(1, received, near, stacked, interp, transfer)
    received = exchange(payload)
    near = near_again(term_one)
    term_two, payload = post(2, received, near, term_one, stacked, interp, transfer)
    received = exchange(payload)
    near = near_again(term_two)
    term_three, payload = post(3, received, near, term_two, term_one, interp)
    received = exchange(payload)
    squares = jnp.sum(received, axis=(0, 1))[:vec]
    total_points = width * devices
    return term_three / jnp.sqrt(squares / total_points + 1e-06)[:, None]


def solution(mesh):
    placed = (
        P(None, ("grp", "leaf")),
        P(None, ("grp", "leaf")),
        P(("grp", "leaf"), None),
        P(("grp", "leaf"), None),
        P(("grp", "leaf"), None),
        P(("grp", "leaf"), None, None),
        P(("grp", "leaf"), None, None),
        P(),
    )
    return jax.shard_map(
        on_device, mesh=mesh, in_specs=placed, out_specs=P(None, ("grp", "leaf")), check_vma=False
    )
```

time: 313 us -> 111 us (0.35)
  blocking collectives: 192 us -> 12.4 us
  matrix products: 49.9 us -> 0 us
  Pallas kernels: 0 us -> 25.2 us
  between operations: 13.7 us -> 0.35 us
  starting transfers between devices: 25.2 us -> 37.9 us
  local copies, waits for them, and re-layouts: 17.3 us -> 27.6 us
  loops' own time: 9.74 us -> 0 us
  waiting for transfers between devices: 0.16 us -> 5.48 us
    psum x4 -> x0, blocking collectives: 138 us -> none  [the longest x3 95.2 us: operate(): subtree_total = lax.psum(upward, 'leaf')]
    all_gather x5 -> x0, blocking collectives: 53.8 us -> none  [the longest x1 23.1 us: on_device(): subtree_lists = lax.all_gather(inter_lists, 'leaf', axis=0, tiled=True)]
    dot_general x30 -> x0, matrix products: 49.9 us -> none  [the longest x12 33.3 us: near_slot(): product = jnp.einsum('vlp,lpq->lvq', source_vecs, kernel, precision=highest)]
    all_to_all x0 -> x3, starting transfers between devices: none -> 34.9 us  [on_device(): exchange = lambda x: lax.all_to_all(x, ('grp', 'leaf'), 0, 0, tiled=True)]
    unnamed x18 -> x91, local copies, waits for them, and re-layouts: 1.51 us -> 27.5 us
    pallas_call x0 -> x15, Pallas kernels: none -> 25.2 us  [the longest x1 5.34 us: on_device(): call(near_kernel('own', True, sizes), (near_shape, k_shape, k_shape), [SM...]
    ppermute x6, starting transfers between devices: 25.1 us -> 3 us  [the longest x2 1.31 us: near_again(): next_field = lax.ppermute(field, 'leaf', outer)]
    gather x27 -> x0, local copies, waits for them, and re-layouts: 14.9 us -> none  [the longest x12 6.87 us: near_slot(): jnp.take(window_points, safe_place, axis=1).transpose(1, 0, 2)]
  transfers between devices with their start and end apart: 9 -> 9, of which waited for: 0 -> 2; matrix products, arithmetic and copies ran while one was open for 21% -> 0% of each run, Pallas kernels for 0% -> 14%
where the time goes in v1:
time: 111 us
  starting transfers between devices  37.9 us (34%)
  local copies, waits for them, and re-layouts  27.6 us (25%)
  Pallas kernels  25.2 us (23%)
  blocking collectives  12.4 us (11%)
  waiting for transfers between devices  5.48 us (5%)
  other arithmetic  1.78 us (2%)
    all_to_all x3, starting transfers between devices, on_device(): exchange = lambda x: lax.all_to_all(x, ('grp', 'leaf'), 0, 0, tiled=True)  34.9 us
    unnamed x91, local copies, waits for them, and re-layouts  27.5 us
    all_to_all x1, blocking collectives, on_device(): exchange = lambda x: lax.all_to_all(x, ('grp', 'leaf'), 0, 0, tiled=True)  12.4 us
    all_to_all x3, waiting for transfers between devices, on_device(): exchange = lambda x: lax.all_to_all(x, ('grp', 'leaf'), 0, 0, tiled=True)  5.45 us
    pallas_call x1, Pallas kernels, on_device(): call(near_kernel('own', True, sizes), (near_shape, k_shape, k_shape), [SM...  5.34 us
    pallas_call x3, Pallas kernels, post(): call(lambda *refs: post_body(step, *refs), (near_shape, shape(send_shape,...  5.31 us
    pallas_call x1, Pallas kernels, on_device(): call(far_body, (far_shape, far_shape), [SMEM, SMEM, VMEM], scratch=[pltpu...  4.75 us
    pallas_call x2, Pallas kernels, near_again(): call(near_kernel('own', False, sizes), near_shape, [SMEM, SMEM, VMEM, VME...  2.71 us
  transfers between devices with their start and end apart: 9, of which 2 were waited for; matrix products, arithmetic and copies ran while one was open for 0% of the time, Pallas kernels for 14%

profile of v1, /device:TPU:0, one launch (start us, length us, event | category | flops | bytes accessed | tf_op | source)
XLA Modules:
  0.0 110.7 jit_solution(11637982461267091740)
XLA Ops:
  0.1 0.9 maximum_maximum_fusion.field.refs_2_.refs_7_.refs_8_
  1.6 0.7 collective-permute-start
  2.3 0.9 copy-done.15
  3.3 0.8 copy-done.23
  4.1 0.7 copy-done.42
  4.8 2.2 %shard_map.82 = f32[32,24,128]{2,1,0:T(8,128)} custom-call(s32[2]{0:T(128)S(1)} %pad_add_fusion.meta.refs_1_.refs_0_, f32[24,1024]{1,0:T(8,128)S(1)} %maximum_maximum_fusion.field.refs_2_.refs_7_.refs_8_, s32[2,64]{1,0:T(2,128)S(1)} %copy-done.42, f32[2,64,512]{2,1,0:T(8,128)S(1)} %copy-done.15, f32[128,128]{1,0:T(8,128)S(1)} %bitcast.3), custom_call_target="tpu_custom_call" | custom-call | flops 10000000 | bytes 1048576 | tf_op jit(solution)/shard_map/pallas_call | solution.py:189
  6.9 8.7 %all-to-all-start = ((f32[32,24,128]{2,1,0:T(8,128)}), f32[32,24,128]{2,1,0:T(8,128)S(1)}, u32[]{:S(2)}, u32[]{:S(2)}) async-start(f32[32,24,128]{2,1,0:T(8,128)} %shard_map.82), calls=%async_computation | async-start | bytes 786432 | tf_op jit(solution)/shard_map/all_to_all | solution.py:159
  15.7 0.7 copy-done.40
  16.4 5.3 %shard_map.85 = (f32[16,1024]{1,0:T(8,128)S(1)}, bf16[2,512,1024]{2,1,0:T(8,128)(2,1)S(1)}, bf16[2,512,1024]{2,1,0:T(8,128)(2,1)S(1)}) custom-call(s32[2,6]{1,0:T(2,128)S(1)} %copy-done.40, s32[2]{0:T(128)S(1)} %pad_add_fusion.meta.refs_1_.refs_0_, f32[24,1024]{1,0:T(8,128)S(1)} %maximum_maximum_fusion.field.refs_2_.refs_7_.refs_8_), custom_call_target="tpu_custom_call" | custom-call | flops 10000000000 | bytes 1048576 | tf_op jit(solution)/shard_map/pallas_call | solution.py:197
  21.7 1.4 %copy-done = bf16[2,512,1024]{2,1,0:T(8,128)(2,1)} copy-done((bf16[2,512,1024]{2,1,0:T(8,128)(2,1)}, bf16[2,512,1024]{2,1,0:T(8,128)(2,1)S(1)}, u32[]{:S(2)}) %copy-start) | copy-done | bytes 2097176
  23.1 1.0 shard_map.84
  24.7 0.8 shard_map.86
  25.6 1.4 %copy-done.3 = bf16[2,512,1024]{2,1,0:T(8,128)(2,1)} copy-done((bf16[2,512,1024]{2,1,0:T(8,128)(2,1)}, bf16[2,512,1024]{2,1,0:T(8,128)(2,1)S(1)}, u32[]{:S(2)}) %copy-start.3) | copy-done | bytes 2097176
  26.9 1.3 %copy-done.6 = bf16[2,512,1024]{2,1,0:T(8,128)(2,1)} copy-done((bf16[2,512,1024]{2,1,0:T(8,128)(2,1)}, bf16[2,512,1024]{2,1,0:T(8,128)(2,1)S(1)}, u32[]{:S(2)}) %copy-start.6) | copy-done | bytes 2097176
  28.3 0.8 shard_map.87
  29.1 1.4 %copy-done.9 = bf16[2,512,1024]{2,1,0:T(8,128)(2,1)} copy-done((bf16[2,512,1024]{2,1,0:T(8,128)(2,1)}, bf16[2,512,1024]{2,1,0:T(8,128)(2,1)S(1)}, u32[]{:S(2)}) %copy-start.9) | copy-done | bytes 2097176
  30.5 1.4 %copy-done.12 = bf16[2,512,1024]{2,1,0:T(8,128)(2,1)} copy-done((bf16[2,512,1024]{2,1,0:T(8,128)(2,1)}, bf16[2,512,1024]{2,1,0:T(8,128)(2,1)S(1)}, u32[]{:S(2)}) %copy-start.12) | copy-done | bytes 2097176
  31.8 0.6 copy-done.38
  32.5 0.8 copy-done.20
  33.2 1.0 copy-done.21
  34.2 4.8 %shard_map.83 = (bf16[2048,128]{1,0:T(8,128)(2,1)S(1)}, bf16[2048,128]{1,0:T(8,128)(2,1)S(1)}) custom-call(s32[2,16]{1,0:T(2,128)S(1)} %copy-done.43, s32[2]{0:T(128)S(1)} %pad_add_fusion.meta.refs_1_.refs_0_, f32[32,24,128]{2,1,0:T(8,128)S(1)} %copy-done.21), custom_call_target="tpu_custom_call" | custom-call | flops 1000000000 | bytes 1048576 | tf_op jit(solution)/shard_map/pallas_call | solution.py:262
  39.1 1.0 copy-done.22
  40.0 1.6 %shard_map.88 = (f32[16,1024]{1,0:T(8,128)S(1)}, f32[32,16,128]{2,1,0:T(8,128)S(1)}) custom-call(s32[2]{0:T(128)S(1)} %pad_add_fusion.meta.refs_1_.refs_0_, f32[32,24,128]{2,1,0:T(8,128)S(1)} %copy-done.22, bf16[2048,128]{1,0:T(8,128)(2,1)S(1)} %get-tuple-element.24.refs_2_, bf16[2048,128]{1,0:T(8,128)(2,1)S(1)} %get-tuple-element.25.refs_3_, ...), custom_call_target="tpu_custom_call" | custom-call | flops 100000000 | bytes 1048576 | tf_op jit(solution)/shard_map/pallas_call | solution.py:323
  41.7 0.7 copy-done.35
  42.4 19.5 %all-to-all-start.1 = ((f32[32,16,128]{2,1,0:T(8,128)}), f32[32,16,128]{2,1,0:T(8,128)}, u32[]{:S(2)}, u32[]{:S(2)}) async-start(f32[32,16,128]{2,1,0:T(8,128)} %copy-done.35), calls=%async_computation.1 | async-start | bytes 524288 | tf_op jit(solution)/shard_map/all_to_all | solution.py:159
  62.2 0.7 collective-permute-start.2
  62.9 1.6 %copy-done.1 = bf16[2,512,1024]{2,1,0:T(8,128)(2,1)S(1)} copy-done((bf16[2,512,1024]{2,1,0:T(8,128)(2,1)S(1)}, bf16[2,512,1024]{2,1,0:T(8,128)(2,1)}, u32[]{:S(2)}) %copy-start.1) | copy-done | bytes 2097176
  64.5 1.4 %shard_map.89.refs_6_ = f32[16,1024]{1,0:T(8,128)S(1)} custom-call(s32[2,6]{1,0:T(2,128)S(1)} %copy-done.41, s32[2]{0:T(128)S(1)} %pad_add_fusion.meta.refs_1_.refs_0_, f32[16,1024]{1,0:T(8,128)S(1)} %get-tuple-element.32.refs_2_.refs_7_.refs_8_, bf16[2,512,1024]{2,1,0:T(8,128)(2,1)S(1)} %get-tuple-element.37.refs_3_, bf16[2,512,1024]{2,1,0:T(8,128)(2,1)S(1)} %copy-done.1), custom_call_target="tpu_custom_call" | custom-call | flops 1000000000 | bytes 1048576 | tf_op jit(solution)/shard_map/pallas_call | solution.py:333
  66.0 0.6 copy-done.7
  67.3 1.0 copy-done.10
  68.3 0.6 copy-done.13
  70.1 2.1 %all-to-all-done.1.refs_1_ = f32[32,16,128]{2,1,0:T(8,128)} async-done(((f32[32,16,128]{2,1,0:T(8,128)}), f32[32,16,128]{2,1,0:T(8,128)}, u32[]{:S(2)}, u32[]{:S(2)}) %all-to-all-start.1) | async-done | bytes 262176 | tf_op jit(solution)/shard_map/all_to_all | solution.py:159
  72.2 0.9 copy-done.19
  73.1 0.8 copy-done.25
  73.9 0.8 copy-done.28
  74.7 0.8 copy-done.32
  75.5 0.8 copy-done.37
  76.3 2.1 %shard_map.92 = (f32[16,1024]{1,0:T(8,128)S(1)}, f32[32,16,128]{2,1,0:T(8,128)S(1)}) custom-call(s32[2]{0:T(128)S(1)} %pad_add_fusion.meta.refs_1_.refs_0_, f32[32,16,128]{2,1,0:T(8,128)} %all-to-all-done.1.refs_1_, bf16[2048,128]{1,0:T(8,128)(2,1)S(1)} %get-tuple-element.24.refs_2_, bf16[2048,128]{1,0:T(8,128)(2,1)S(1)} %get-tuple-element.25.refs_3_, ...), custom_call_target="tpu_custom_call" | custom-call | flops 100000000 | bytes 1048576 | tf_op jit(solution)/shard_map/pallas_call | solution.py:323
  78.4 0.7 copy-done.34
  79.1 6.6 %all-to-all-start.2 = ((f32[32,16,128]{2,1,0:T(8,128)}), f32[32,16,128]{2,1,0:T(8,128)}, u32[]{:S(2)}, u32[]{:S(2)}) async-start(f32[32,16,128]{2,1,0:T(8,128)} %copy-done.34), calls=%async_computation.2 | async-start | bytes 524288 | tf_op jit(solution)/shard_map/all_to_all | solution.py:159
  85.9 0.7 collective-permute-start.4
  86.6 1.6 %copy-done.2 = bf16[2,512,1024]{2,1,0:T(8,128)(2,1)S(1)} copy-done((bf16[2,512,1024]{2,1,0:T(8,128)(2,1)S(1)}, bf16[2,512,1024]{2,1,0:T(8,128)(2,1)}, u32[]{:S(2)}) %copy-start.2) | copy-done | bytes 2097176
  88.2 1.4 %shard_map.93.refs_6_ = f32[16,1024]{1,0:T(8,128)S(1)} custom-call(s32[2,6]{1,0:T(2,128)S(1)} %copy-done.41, s32[2]{0:T(128)S(1)} %pad_add_fusion.meta.refs_1_.refs_0_, f32[16,1024]{1,0:T(8,128)S(1)} %get-tuple-element.40.refs_2_.refs_7_, bf16[2,512,1024]{2,1,0:T(8,128)(2,1)S(1)} %get-tuple-element.37.refs_3_, bf16[2,512,1024]{2,1,0:T(8,128)(2,1)S(1)} %copy-done.2), custom_call_target="tpu_custom_call" | custom-call | flops 1000000000 | bytes 1048576 | tf_op jit(solution)/shard_map/pallas_call | solution.py:333
  89.8 0.6 copy-done.8
  92.5 3.4 %all-to-all-done.2.refs_1_ = f32[32,16,128]{2,1,0:T(8,128)} async-done(((f32[32,16,128]{2,1,0:T(8,128)}), f32[32,16,128]{2,1,0:T(8,128)}, u32[]{:S(2)}, u32[]{:S(2)}) %all-to-all-start.2) | async-done | bytes 262176 | tf_op jit(solution)/shard_map/all_to_all | solution.py:159
  95.9 1.6 %shard_map.96 = (f32[16,1024]{1,0:T(8,128)S(1)}, f32[32,1,128]{2,1,0:T(1,128)S(1)}) custom-call(s32[2]{0:T(128)S(1)} %pad_add_fusion.meta.refs_1_.refs_0_, f32[32,16,128]{2,1,0:T(8,128)} %all-to-all-done.2.refs_1_, bf16[2048,128]{1,0:T(8,128)(2,1)S(1)} %get-tuple-element.24.refs_2_, bf16[2048,128]{1,0:T(8,128)(2,1)S(1)} %get-tuple-element.25.refs_3_, ...), custom_call_target="tpu_custom_call" | custom-call | flops 100000000 | bytes 1048576 | tf_op jit(solution)/shard_map/pallas_call | solution.py:323
  97.5 12.4 %all_to_all.20 = f32[32,1,128]{2,1,0:T(1,128)S(1)} all-to-all(f32[32,1,128]{2,1,0:T(1,128)S(1)} %get-tuple-element.42), channel_id=1, replica_groups=mesh['grp'=2,'leaf'=16] {'grp','leaf'}, dimensions={0} | all-to-all | bytes 32768 | tf_op jit(solution)/shard_map/all_to_all | solution.py:159
  110.0 0.7 broadcast_divide_fusion
  (85 shorter events, 6.4 us)
Async XLA Ops:
  1.0 27.3 %copy-start.17 = (f32[24,1024]{1,0:T(8,128)}, f32[24,1024]{1,0:T(8,128)S(1)}, u32[]{:S(2)}) copy-start(f32[24,1024]{1,0:T(8,128)S(1)} %maximum_maximum_fusion.field.refs_2_.refs_7_.refs_8_) | copy-start | bytes 294916
  1.0 23.7 %collective-permute-start.1 = (f32[24,1024]{1,0:T(8,128)S(1)}, f32[24,1024]{1,0:T(8,128)S(1)}, u32[]{:S(2)}, u32[]{:S(2)}) collective-permute-start(f32[24,1024]{1,0:T(8,128)S(1)} %maximum_maximum_fusion.field.refs_2_.refs_7_.refs_8_), channel_id=1, source_target_pairs={{0,1},{1,0},{2,3},{3,2},{4,5},{5,4},{6,7},{7,6},{8,9},{9,8},{10,11... | collective-permute-start | bytes 294920 | tf_op jit(solution)/shard_map/ppermute | solution.py:168
  1.6 26.7 %collective-permute-start = (f32[24,1024]{1,0:T(8,128)S(1)}, f32[24,1024]{1,0:T(8,128)S(1)}, u32[]{:S(2)}, u32[]{:S(2)}) collective-permute-start(f32[24,1024]{1,0:T(8,128)S(1)} %maximum_maximum_fusion.field.refs_2_.refs_7_.refs_8_), channel_id=1, source_target_pairs={{1,2},{3,4},{5,6},{7,8},{9,10},{11,12},{13,14},{2,1},{4,3},{6,5},{... | collective-permute-start | bytes 294920 | tf_op jit(solution)/shard_map/ppermute | solution.py:169
  2.3 1.0 copy-start.15
  3.3 0.8 copy-start.23
  6.9 25.5 %all-to-all-start = ((f32[32,24,128]{2,1,0:T(8,128)}), f32[32,24,128]{2,1,0:T(8,128)S(1)}, u32[]{:S(2)}, u32[]{:S(2)}) async-start(f32[32,24,128]{2,1,0:T(8,128)} %shard_map.82), calls=%async_computation | async-start | bytes 786432 | tf_op jit(solution)/shard_map/all_to_all | solution.py:159
  16.4 6.7 %copy-start.44 = (f32[2,3,128]{2,0,1:T(2,128)S(1)}, f32[2,3,128]{2,0,1:T(2,128)}, u32[]{:S(2)}) copy-start(f32[2,3,128]{2,0,1:T(2,128)} %param.15) | copy-start | bytes 9220
  16.4 6.7 %copy-start.24 = (f32[2,64,128]{2,1,0:T(8,128)S(1)}, f32[2,64,128]{2,1,0:T(8,128)}, u32[]{:S(2)}) copy-start(f32[2,64,128]{2,1,0:T(8,128)} %param.14) | copy-start | bytes 196612
  16.4 8.4 %copy-start.41 = (s32[2,6]{1,0:T(2,128)S(1)}, s32[2,6]{1,0:T(2,128)}, u32[]{:S(2)}) copy-start(s32[2,6]{1,0:T(2,128)} %refs_0_.17) | copy-start | bytes 148
  21.7 1.4 %copy-start = (bf16[2,512,1024]{2,1,0:T(8,128)(2,1)}, bf16[2,512,1024]{2,1,0:T(8,128)(2,1)S(1)}, u32[]{:S(2)}) copy-start(bf16[2,512,1024]{2,1,0:T(8,128)(2,1)S(1)} %get-tuple-element.38.refs_4_) | copy-start | bytes 6291460
  24.7 0.8 copy-start.30
  25.6 1.4 %copy-start.3 = (bf16[2,512,1024]{2,1,0:T(8,128)(2,1)}, bf16[2,512,1024]{2,1,0:T(8,128)(2,1)S(1)}, u32[]{:S(2)}) copy-start(bf16[2,512,1024]{2,1,0:T(8,128)(2,1)S(1)} %get-tuple-element.35.refs_4_) | copy-start | bytes 6291460
  26.9 1.3 %copy-start.6 = (bf16[2,512,1024]{2,1,0:T(8,128)(2,1)}, bf16[2,512,1024]{2,1,0:T(8,128)(2,1)S(1)}, u32[]{:S(2)}) copy-start(bf16[2,512,1024]{2,1,0:T(8,128)(2,1)S(1)} %get-tuple-element.36.refs_5_) | copy-start | bytes 6291460
  28.3 5.0 %copy-start.43 = (s32[2,16]{1,0:T(2,128)S(1)}, s32[2,16]{1,0:T(2,128)}, u32[]{:S(2)}) copy-start(s32[2,16]{1,0:T(2,128)} %lists.1) | copy-start | bytes 388
  29.1 1.4 %copy-start.9 = (bf16[2,512,1024]{2,1,0:T(8,128)(2,1)}, bf16[2,512,1024]{2,1,0:T(8,128)(2,1)S(1)}, u32[]{:S(2)}) copy-start(bf16[2,512,1024]{2,1,0:T(8,128)(2,1)S(1)} %get-tuple-element.33.refs_4_) | copy-start | bytes 6291460
  30.5 1.4 %copy-start.12 = (bf16[2,512,1024]{2,1,0:T(8,128)(2,1)}, bf16[2,512,1024]{2,1,0:T(8,128)(2,1)S(1)}, u32[]{:S(2)}) copy-start(bf16[2,512,1024]{2,1,0:T(8,128)(2,1)S(1)} %get-tuple-element.34.refs_5_) | copy-start | bytes 6291460
  32.5 6.5 %copy-start.16 = (f32[2,64,512]{2,1,0:T(8,128)S(1)}, f32[2,64,512]{2,1,0:T(8,128)}, u32[]{:S(2)}) copy-start(f32[2,64,512]{2,1,0:T(8,128)} %refs_9_.3) | copy-start | bytes 786436
  32.5 0.8 copy-start.20
  33.2 1.0 copy-start.21
  34.2 4.8 %copy-start.18 = (f32[24,1024]{1,0:T(8,128)S(1)}, f32[24,1024]{1,0:T(8,128)}, u32[]{:S(2)}) copy-start(f32[24,1024]{1,0:T(8,128)} %copy-done.17) | copy-start | bytes 294916
  34.2 4.8 %copy-start.27 = (bf16[128,128]{1,0:T(8,128)(2,1)S(1)}, bf16[128,128]{1,0:T(8,128)(2,1)}, u32[]{:S(2)}) copy-start(bf16[128,128]{1,0:T(8,128)(2,1)} %copy-done.26) | copy-start | bytes 98308
  34.2 4.8 %copy-start.31 = (bf16[128,128]{1,0:T(8,128)(2,1)S(1)}, bf16[128,128]{1,0:T(8,128)(2,1)}, u32[]{:S(2)}) copy-start(bf16[128,128]{1,0:T(8,128)(2,1)} %copy-done.30) | copy-start | bytes 98308
  34.2 4.8 %copy-start.39 = (f32[16,1024]{1,0:T(8,128)S(1)}, f32[16,1024]{1,0:T(8,128)}, u32[]{:S(2)}) copy-start(f32[16,1024]{1,0:T(8,128)} %copy-done.38) | copy-start | bytes 196612
  39.0 1.0 copy-start.22
  41.7 0.7 copy-start.35
  42.4 29.8 %all-to-all-start.1 = ((f32[32,16,128]{2,1,0:T(8,128)}), f32[32,16,128]{2,1,0:T(8,128)}, u32[]{:S(2)}, u32[]{:S(2)}) async-start(f32[32,16,128]{2,1,0:T(8,128)} %copy-done.35), calls=%async_computation.1 | async-start | bytes 524288 | tf_op jit(solution)/shard_map/all_to_all | solution.py:159
  62.0 3.9 %collective-permute-start.3 = (f32[16,1024]{1,0:T(8,128)S(1)}, f32[16,1024]{1,0:T(8,128)S(1)}, u32[]{:S(2)}, u32[]{:S(2)}) collective-permute-start(f32[16,1024]{1,0:T(8,128)S(1)} %get-tuple-element.32.refs_2_.refs_7_.refs_8_), channel_id=1, source_target_pairs={{0,1},{1,0},{2,3},{3,2},{4,5},{5,4},{6,7},{7,6},{8,9},{9,8},{10,11... | collective-permute-start | bytes 196616 | tf_op jit(solution)/shard_map/ppermute | solution.py:331
  62.2 5.1 %collective-permute-start.2 = (f32[16,1024]{1,0:T(8,128)S(1)}, f32[16,1024]{1,0:T(8,128)S(1)}, u32[]{:S(2)}, u32[]{:S(2)}) collective-permute-start(f32[16,1024]{1,0:T(8,128)S(1)} %get-tuple-element.32.refs_2_.refs_7_.refs_8_), channel_id=1, source_target_pairs={{1,2},{3,4},{5,6},{7,8},{9,10},{11,12},{13,14},{2,1},{4,3},{6,5},{... | collective-permute-start | bytes 196616 | tf_op jit(solution)/shard_map/ppermute | solution.py:332
  62.9 1.6 %copy-start.1 = (bf16[2,512,1024]{2,1,0:T(8,128)(2,1)S(1)}, bf16[2,512,1024]{2,1,0:T(8,128)(2,1)}, u32[]{:S(2)}) copy-start(bf16[2,512,1024]{2,1,0:T(8,128)(2,1)} %copy-done) | copy-start | bytes 6291460
  64.5 1.6 %copy-start.4 = (bf16[2,512,1024]{2,1,0:T(8,128)(2,1)S(1)}, bf16[2,512,1024]{2,1,0:T(8,128)(2,1)}, u32[]{:S(2)}) copy-start(bf16[2,512,1024]{2,1,0:T(8,128)(2,1)} %copy-done.3) | copy-start | bytes 6291460
  64.5 2.2 %copy-start.7 = (bf16[2,512,1024]{2,1,0:T(8,128)(2,1)S(1)}, bf16[2,512,1024]{2,1,0:T(8,128)(2,1)}, u32[]{:S(2)}) copy-start(bf16[2,512,1024]{2,1,0:T(8,128)(2,1)} %copy-done.6) | copy-start | bytes 6291460
  66.7 1.6 %copy-start.10 = (bf16[2,512,1024]{2,1,0:T(8,128)(2,1)S(1)}, bf16[2,512,1024]{2,1,0:T(8,128)(2,1)}, u32[]{:S(2)}) copy-start(bf16[2,512,1024]{2,1,0:T(8,128)(2,1)} %copy-done.9) | copy-start | bytes 6291460
  66.7 2.2 %copy-start.13 = (bf16[2,512,1024]{2,1,0:T(8,128)(2,1)S(1)}, bf16[2,512,1024]{2,1,0:T(8,128)(2,1)}, u32[]{:S(2)}) copy-start(bf16[2,512,1024]{2,1,0:T(8,128)(2,1)} %copy-done.12) | copy-start | bytes 6291460
  72.2 0.9 copy-start.19
  73.1 0.8 copy-start.25
  73.9 0.8 copy-start.28
  74.7 0.8 copy-start.32
  75.5 0.8 copy-start.37
  79.1 16.8 %all-to-all-start.2 = ((f32[32,16,128]{2,1,0:T(8,128)}), f32[32,16,128]{2,1,0:T(8,128)}, u32[]{:S(2)}, u32[]{:S(2)}) async-start(f32[32,16,128]{2,1,0:T(8,128)} %copy-done.34), calls=%async_computation.2 | async-start | bytes 524288 | tf_op jit(solution)/shard_map/all_to_all | solution.py:159
  85.7 3.9 %collective-permute-start.5 = (f32[16,1024]{1,0:T(8,128)S(1)}, f32[16,1024]{1,0:T(8,128)S(1)}, u32[]{:S(2)}, u32[]{:S(2)}) collective-permute-start(f32[16,1024]{1,0:T(8,128)S(1)} %get-tuple-element.40.refs_2_.refs_7_), channel_id=1, source_target_pairs={{0,1},{1,0},{2,3},{3,2},{4,5},{5,4},{6,7},{7,6},{8,9},{9,8},{10,11... | collective-permute-start | bytes 196616 | tf_op jit(solution)/shard_map/ppermute | solution.py:331
  85.9 5.1 %collective-permute-start.4 = (f32[16,1024]{1,0:T(8,128)S(1)}, f32[16,1024]{1,0:T(8,128)S(1)}, u32[]{:S(2)}, u32[]{:S(2)}) collective-permute-start(f32[16,1024]{1,0:T(8,128)S(1)} %get-tuple-element.40.refs_2_.refs_7_), channel_id=1, source_target_pairs={{1,2},{3,4},{5,6},{7,8},{9,10},{11,12},{13,14},{2,1},{4,3},{6,5},{... | collective-permute-start | bytes 196616 | tf_op jit(solution)/shard_map/ppermute | solution.py:332
  86.6 1.6 %copy-start.2 = (bf16[2,512,1024]{2,1,0:T(8,128)(2,1)S(1)}, bf16[2,512,1024]{2,1,0:T(8,128)(2,1)}, u32[]{:S(2)}) copy-start(bf16[2,512,1024]{2,1,0:T(8,128)(2,1)} %copy-done) | copy-start | bytes 6291460
  88.2 1.6 %copy-start.5 = (bf16[2,512,1024]{2,1,0:T(8,128)(2,1)S(1)}, bf16[2,512,1024]{2,1,0:T(8,128)(2,1)}, u32[]{:S(2)}) copy-start(bf16[2,512,1024]{2,1,0:T(8,128)(2,1)} %copy-done.3) | copy-start | bytes 6291460
  88.2 2.2 %copy-start.8 = (bf16[2,512,1024]{2,1,0:T(8,128)(2,1)S(1)}, bf16[2,512,1024]{2,1,0:T(8,128)(2,1)}, u32[]{:S(2)}) copy-start(bf16[2,512,1024]{2,1,0:T(8,128)(2,1)} %copy-done.6) | copy-start | bytes 6291460
  89.5 1.8 %copy-start.11 = (bf16[2,512,1024]{2,1,0:T(8,128)(2,1)S(1)}, bf16[2,512,1024]{2,1,0:T(8,128)(2,1)}, u32[]{:S(2)}) copy-start(bf16[2,512,1024]{2,1,0:T(8,128)(2,1)} %copy-done.9) | copy-start | bytes 6291460
  89.5 2.4 %copy-start.14 = (bf16[2,512,1024]{2,1,0:T(8,128)(2,1)S(1)}, bf16[2,512,1024]{2,1,0:T(8,128)(2,1)}, u32[]{:S(2)}) copy-start(bf16[2,512,1024]{2,1,0:T(8,128)(2,1)} %copy-done.12) | copy-start | bytes 6291460
  91.0 4.9 %copy-start.29 = (bf16[128,128]{1,0:T(8,128)(2,1)S(1)}, bf16[128,128]{1,0:T(8,128)(2,1)}, u32[]{:S(2)}) copy-start(bf16[128,128]{1,0:T(8,128)(2,1)} %copy-done.26) | copy-start | bytes 98308
  91.0 4.9 %copy-start.33 = (bf16[128,128]{1,0:T(8,128)(2,1)S(1)}, bf16[128,128]{1,0:T(8,128)(2,1)}, u32[]{:S(2)}) copy-start(bf16[128,128]{1,0:T(8,128)(2,1)} %copy-done.30) | copy-start | bytes 98308
  (6 other events, 3.9 us)

commit v2 on v0

v2 whole, which is shorter than its diff:
```python
import jax
import jax.numpy as jnp
from jax import lax
from jax.experimental import pallas as pl
from jax.experimental.pallas import tpu as pltpu
from jax.sharding import PartitionSpec as P

kappa_scale = 3.4641016151377544
log2_e = 1.4426950408889634
centre = 0.05
half_width = 0.05
highest = lax.Precision.HIGHEST
f32 = jnp.float32
bf16 = jnp.bfloat16

HBM = pl.BlockSpec(memory_space=pltpu.HBM)
VMEM = pl.BlockSpec(memory_space=pltpu.VMEM)
SMEM = pl.BlockSpec(memory_space=pltpu.SMEM)
SUB = 8
NEAR_LIMIT = 54000
START_LIMIT = 6000


def split(x):
    hi = x.astype(bf16)
    return hi, (x - hi.astype(f32)).astype(bf16)


def dot3(left, right_hi, right_lo):
    rows = left.shape[0]
    hi, lo = split(left)
    both = jnp.dot(jnp.concatenate([hi, lo], axis=0), right_hi, preferred_element_type=f32)
    return both[:rows] + both[rows:] + jnp.dot(hi, right_lo, preferred_element_type=f32)


def dot_nt(left, right):
    return lax.dot_general(
        left, right, (((1,), (1,)), ((), ())), precision=highest, preferred_element_type=f32
    )


def dot_full(left, right):
    return jnp.dot(left, right, precision=highest, preferred_element_type=f32)


def three_parts(x):
    first = x.astype(bf16).astype(f32)
    second = (x - first).astype(bf16).astype(f32)
    return first, second, x - first - second


def distance_factors(points):
    x, y, z = points
    n = x.shape[1]
    norm = x * x + y * y + z * z
    at = lax.broadcasted_iota(jnp.int32, (SUB, n), 0)

    def rows(values):
        out = jnp.zeros((SUB, n), f32)
        for i, value in enumerate(values):
            out = jnp.where(at == i, value, out)
        return three_parts(out)

    s1, s2, s3 = rows([x, y, z, norm, 1.0])
    t1, t2, t3 = rows([-2.0 * x, -2.0 * y, -2.0 * z, 1.0, norm])
    source = jnp.concatenate([s1, s1, s2, s1, s3, s2], axis=0)
    target = jnp.concatenate([t1, t2, t1, t3, t1, t2], axis=0)
    return source, target


def source_factors(points):
    return distance_factors(points)[0].T.astype(bf16)


def target_factors(points):
    return distance_factors(points)[1].astype(bf16)


def matern(source, target):
    square = jnp.maximum(jnp.dot(source, target, preferred_element_type=f32), 1e-30)
    scaled = square * lax.rsqrt(square)
    return (1.0 + scaled) * jnp.exp2(scaled * -log2_e)


def coordinates(points, origin):
    return [(points[d : d + 1] - origin[d : d + 1, :1]) * kappa_scale for d in range(3)]


class Copies:
    def __init__(self, sems):
        self.sems, self.used, self.open = sems, 0, {}

    def start(self, name, source, target):
        copy = pltpu.make_async_copy(source, target, self.sems.at[self.used])
        self.used += 1
        copy.start()
        self.open[name] = copy

    def wait(self, *names):
        for name in names:
            self.open.pop(name).wait()

    def finish(self):
        self.wait(*list(self.open))


def call(kernel, out_shape, in_specs, out_specs, scratch=(), flops=0, limit=60 * 1024):
    return pl.pallas_call(
        kernel,
        out_shape=out_shape,
        in_specs=in_specs,
        out_specs=out_specs,
        scratch_shapes=scratch,
        compiler_params=pltpu.CompilerParams(vmem_limit_bytes=limit << 10),
        cost_estimate=pl.CostEstimate(flops=flops, bytes_accessed=1 << 20, transcendentals=0),
    )


def on_device(vectors, points, near_lists, inter_lists, skeleton, interp, transfer, coarse_points):
    per_dev, slots = near_lists.shape
    listed = inter_lists.shape[1]
    rank, leaf_size = interp.shape[1:]
    coarse = transfer.shape[2]
    vec, width = vectors.shape
    leaves, groups = lax.axis_size("leaf"), lax.axis_size("grp")
    devices = leaves * groups
    cols = per_dev * rank
    assert cols == coarse
    transfer = transfer.reshape(cols, coarse)
    inner = [(i, i ^ 1) for i in range(leaves)]
    outer = [(i, i + 1) for i in range(1, leaves - 1, 2)]
    outer = outer + [(j, i) for i, j in outer]
    exchange = lambda x: lax.all_to_all(x, ("grp", "leaf"), 0, 0, tiled=True)
    shape = jax.ShapeDtypeStruct
    field_shape = shape((vec, width), f32)
    field_scratch = pltpu.VMEM((vec, width), f32)
    couple_rows = (groups - 1) * coarse
    far_rows = leaves * cols
    limit = max(6000, far_rows * 3 // 2)
    leaf_slice = lambda j: slice(j * leaf_size, (j + 1) * leaf_size)

    def whereabouts():
        return lax.axis_index("leaf"), lax.axis_index("grp")

    def hit(place, lists, kind, j, leaf):
        odd = lax.rem(place[0], 2)
        if kind == 0:
            spot = per_dev + j
        else:
            spot = jnp.where(odd == kind - 1, 2 * per_dev, 0) + j
        found = lists[leaf, 0] == spot
        for slot in range(1, slots):
            found = jnp.logical_or(found, lists[leaf, slot] == spot)
        return found

    def coefficients(field, interp, transfer):
        coeffs = jnp.concatenate(
            [dot_nt(field[:, leaf_slice(j)], interp[j]) for j in range(per_dev)], axis=1
        )
        return coeffs, dot_full(coeffs, transfer[...])

    def send_parts(copies, out, own, upward, group):
        for i in range(leaves):
            copies.start(("own", i), own, out.at[group * leaves + i])
        for t in range(1, groups):
            first = lax.rem(group + t, groups) * leaves
            for i in range(leaves):
                copies.start(("up", t, i), upward, out.at[first + i])

    stacked = jnp.concatenate([vectors, points, jnp.zeros((SUB - 3, width), f32)], axis=0)
    pair_window = lax.ppermute(stacked, "leaf", inner)
    next_window = lax.ppermute(stacked, "leaf", outer)

    def start_body(
        field_in, points_in, skel_in, interp_in, transfer_in, coarse_in, near_lists_in, inter_lists_in,
        out, interp, transfer, coarse_points, near_lists, inter_lists,
        field, points, skel, own, up, sems,
    ):
        copies = Copies(sems)
        copies.start("points", points_in, points)
        copies.start("skel", skel_in, skel)
        copies.start("field", field_in, field)
        copies.start("interp", interp_in, interp)
        copies.start("transfer", transfer_in, transfer)
        copies.start("coarse", coarse_in, coarse_points)
        copies.start("near_lists", near_lists_in, near_lists)
        copies.start("inter_lists", inter_lists_in, inter_lists)
        own[vec:] = jnp.zeros((SUB, cols), f32)
        up[vec:] = jnp.zeros((SUB, cols), f32)
        copies.wait("points", "skel")
        for j in range(per_dev):
            places = lax.broadcasted_iota(jnp.int32, (leaf_size, rank), 0)
            pick = (places == skel[j : j + 1, :]).astype(f32)
            own[vec : vec + 3, j * rank : (j + 1) * rank] = dot_full(points[:, leaf_slice(j)], pick)
        copies.wait("field", "interp", "transfer")
        coeffs, upward = coefficients(field, interp, transfer)
        own[:vec] = coeffs
        up[:vec] = upward
        send_parts(copies, out, own, up, whereabouts()[1])
        copies.finish()

    payload, interp, transfer, coarse_points, near_lists, inter_lists = call(
        start_body,
        (
            shape((devices, vec + SUB, cols), f32),
            shape(interp.shape, f32),
            shape(transfer.shape, f32),
            shape((3, groups, coarse), f32),
            shape(near_lists.shape, jnp.int32),
            shape(inter_lists.shape, jnp.int32),
        ),
        [HBM] * 8,
        (HBM,) + (VMEM,) * 5,
        scratch=[
            field_scratch,
            pltpu.VMEM((3, width), f32),
            pltpu.VMEM((per_dev, rank), jnp.int32),
            pltpu.VMEM((vec + SUB, cols), f32),
            pltpu.VMEM((vec + SUB, cols), f32),
            pltpu.SemaphoreType.DMA((8 + devices,)),
        ],
        flops=10**7,
        limit=START_LIMIT,
    )(
        *[
            pltpu.with_memory_space_constraint(x, pltpu.HBM)
            for x in (
                vectors, points, skeleton, interp, transfer, coarse_points.transpose(1, 0, 2),
                near_lists, inter_lists,
            )
        ]
    )
    entries = [
        (kind, j, leaf) for kind in range(3) for j in range(per_dev) for leaf in range(per_dev)
    ]
    blocks_shape = (3 * per_dev, per_dev, 2, leaf_size, leaf_size)
    couple_shape = (2, couple_rows, cols)

    def near_first_body(
        lists, own, pair, other, coarse_points, transfer,
        near, couple, blocks_out, blocks, sems,
    ):
        def out_copy(block, leaf):
            return pltpu.make_async_copy(
                blocks.at[block, leaf], blocks_out.at[block, leaf], sems.at[block * per_dev + leaf]
            )

        place = whereabouts()
        group = place[1]
        mine = coarse_points[:, group]
        coarse_origin = mine[:, :1]
        target = target_factors(coordinates(mine, coarse_origin))
        for t in range(1, groups):
            far = coarse_points[:, lax.rem(group + t, groups)]
            kernel = matern(source_factors(coordinates(far, coarse_origin)), target)
            at = slice((t - 1) * coarse, t * coarse)
            couple[0, at], couple[1, at] = split(dot_nt(kernel, transfer[...]))
        windows = (own, pair, other)
        origin = own[vec : vec + 3][:, :1]
        targets = [
            target_factors(coordinates(own[vec : vec + 3, leaf_slice(leaf)], origin))
            for leaf in range(per_dev)
        ]
        near[...] = jnp.zeros_like(near)
        hits = [hit(place, lists, *entry) for entry in entries]
        for (kind, j, leaf), found in zip(entries, hits, strict=True):
            window = windows[kind]
            if leaf == 0:
                factors = source_factors(
                    coordinates(window[vec : vec + 3, leaf_slice(j)], origin)
                )
            block = kind * per_dev + j

            @pl.when(found)
            def _():
                step = 64
                for i in range(leaf_size // step):
                    at = slice(i * step, (i + 1) * step)
                    hi, lo = split(matern(factors[at], targets[leaf]))
                    blocks[block, leaf, 0, at] = hi
                    blocks[block, leaf, 1, at] = lo
                out_copy(block, leaf).start()
                near[:, leaf_slice(leaf)] += dot3(
                    window[:vec, leaf_slice(j)], blocks[block, leaf, 0], blocks[block, leaf, 1]
                )

        for (kind, j, leaf), found in zip(entries, hits, strict=True):

            @pl.when(found)
            def _():
                out_copy(kind * per_dev + j, leaf).wait()

    def near_again(kinds, windows, blocks, before=()):
        chosen = [entry for entry in entries if entry[0] in kinds]
        base = kinds[0] * per_dev
        shape_here = (len(kinds) * per_dev, *blocks_shape[1:])

        def body(lists, *refs):
            windows = refs[: len(kinds)]
            acc = refs[len(kinds) : len(kinds) + len(before)]
            blocks_in, near, blocks, sems = refs[len(kinds) + len(before) :]

            def in_copy(block, leaf):
                return pltpu.make_async_copy(
                    blocks_in.at[base + block, leaf], blocks.at[block, leaf],
                    sems.at[block * per_dev + leaf],
                )

            place = whereabouts()
            hits = [hit(place, lists, *entry) for entry in chosen]
            for (kind, j, leaf), found in zip(chosen, hits, strict=True):

                @pl.when(found)
                def _():
                    in_copy(kind * per_dev + j - base, leaf).start()

            near[...] = acc[0][...] if acc else jnp.zeros_like(near)
            for (kind, j, leaf), found in zip(chosen, hits, strict=True):
                block = kind * per_dev + j - base

                @pl.when(found)
                def _():
                    in_copy(block, leaf).wait()
                    near[:, leaf_slice(leaf)] += dot3(
                        windows[kind - kinds[0]][:, leaf_slice(j)],
                        blocks[block, leaf, 0],
                        blocks[block, leaf, 1],
                    )

        return call(
            body,
            field_shape,
            [SMEM] + [VMEM] * (len(kinds) + len(before)) + [HBM],
            VMEM,
            scratch=[pltpu.VMEM(shape_here, bf16), pltpu.SemaphoreType.DMA((len(chosen),))],
            flops=10**8,
            limit=NEAR_LIMIT,
        )(near_lists, *windows, *before, blocks)

    near_scratch = [
        pltpu.VMEM(blocks_shape, bf16),
        pltpu.SemaphoreType.DMA((len(entries),)),
    ]

    def halo(field):
        pair = lax.ppermute(field, "leaf", inner)
        other = lax.ppermute(field, "leaf", outer)
        return pair, other

    def build_far(place, lists, received, origin, far):
        group, leaf = place[1], place[0]
        target = target_factors(coordinates(received[group * leaves + leaf, vec : vec + 3], origin))
        lane_leaf = lax.broadcasted_iota(jnp.int32, (leaves * per_dev, cols), 1) // rank
        row_leaf = lax.broadcasted_iota(jnp.int32, (leaves * per_dev, cols), 0)
        mark = jnp.zeros((leaves * per_dev, cols), f32)
        for j in range(per_dev):
            for s in range(listed):
                here = jnp.logical_and(row_leaf == lists[j, s], lane_leaf == j)
                mark = jnp.where(here, 1.0, mark)
        for i in range(leaves):
            spots = received[group * leaves + i, vec : vec + 3]
            kernel = matern(source_factors(coordinates(spots, origin)), target)
            for h in range(per_dev):
                m = i * per_dev + h
                at = slice(m * rank, (m + 1) * rank)
                hi, lo = split(kernel[h * rank : (h + 1) * rank] * mark[m : m + 1])
                far[0, at] = hi
                far[1, at] = lo

    far_shape = (2, far_rows, cols)

    def post_body(step, lists, received, couple, interp, near, field, *rest):
        rest = list(rest)
        far, before = (None, None) if step == 1 else rest[:2]
        rest = rest if step == 1 else rest[2:]
        transfer = rest.pop(0) if step < 3 else None
        out, send = rest[:2]
        place = whereabouts()
        group = place[1]
        if step == 1:
            far = rest[2]
            origin = received[group * leaves + place[0], vec : vec + 3][:, :1]
            build_far(place, lists, received, origin, far)
        coeffs = jnp.concatenate(
            [received[group * leaves + i, :vec] for i in range(leaves)], axis=1
        )
        totals = []
        for t in range(1, groups):
            first = lax.rem(group + t, groups) * leaves
            parts = [received[first + i, :vec] for i in range(leaves)]
            while len(parts) > 1:
                parts = [sum(parts[i : i + 2]) for i in range(0, len(parts), 2)]
            totals.append(parts[0])
        down = dot3(coeffs, far[0], far[1])
        if totals:
            down = down + dot3(jnp.concatenate(totals, axis=1), couple[0], couple[1])
        news = []
        for j in range(per_dev):
            here = leaf_slice(j)
            far_part = dot_full(down[:, j * rank : (j + 1) * rank], interp[j])
            applied = (near[:, here] + far_part) * (1.0 / (leaf_size * slots))
            term = (applied - centre * field[:vec, here]) * (1.0 / half_width)
            if step > 1:
                term = 2.0 * term - before[:vec, here]
            news.append(term)
            out[:, here] = term
        if step < 3:
            coeffs, upward = coefficients(jnp.concatenate(news, axis=1), interp, transfer)
            for i in range(leaves):
                send[group * leaves + i] = coeffs
            for t in range(1, groups):
                first = lax.rem(group + t, groups) * leaves
                for i in range(leaves):
                    send[first + i] = upward
        else:
            squares = None
            for term in news:
                part = jnp.sum(term * term, axis=1, keepdims=True)
                squares = part if squares is None else squares + part
            diagonal = lax.broadcasted_iota(jnp.int32, (vec, 128), 0) == lax.broadcasted_iota(
                jnp.int32, (vec, 128), 1
            )
            row = jnp.sum(jnp.where(diagonal, squares, 0.0), axis=0, keepdims=True)
            for i in range(devices):
                send[i] = row

    def post(step, received, near, field, *rest):
        send_shape = (devices, vec, cols) if step < 3 else (devices, 1, 128)
        outs = [field_shape, shape(send_shape, f32)]
        if step == 1:
            outs.append(shape(far_shape, bf16))
        args = [received, couple, interp, near, field, *rest]
        if step < 3:
            args.append(transfer)
        return call(
            lambda *refs: post_body(step, *refs),
            tuple(outs),
            [SMEM] + [VMEM] * len(args),
            (VMEM,) * len(outs),
            flops=10**7,
            limit=limit,
        )(inter_lists, *args)

    def again(field):
        pair, other = halo(field)
        near = near_again((0, 1), (field, pair), blocks)
        return near_again((2,), (other,), blocks, (near,))

    received = exchange(payload)
    near, couple, blocks = call(
        near_first_body,
        (field_shape, shape(couple_shape, bf16), shape(blocks_shape, bf16)),
        [SMEM] + [VMEM] * 5,
        (VMEM, VMEM, HBM),
        scratch=near_scratch,
        flops=10**9,
        limit=NEAR_LIMIT,
    )(near_lists, stacked, pair_window, next_window, coarse_points, transfer)
    term_one, payload, far = post(1, received, near, stacked)
    received = exchange(payload)
    near = again(term_one)
    term_two, payload = post(2, received, near, term_one, far, stacked)
    received = exchange(payload)
    near = again(term_two)
    term_three, payload = post(3, received, near, term_two, far, term_one)
    received = exchange(payload)
    squares = jnp.sum(received, axis=(0, 1))[:vec]
    total_points = width * devices
    return term_three / jnp.sqrt(squares / total_points + 1e-06)[:, None]


def solution(mesh):
    placed = (
        P(None, ("grp", "leaf")),
        P(None, ("grp", "leaf")),
        P(("grp", "leaf"), None),
        P(("grp", "leaf"), None),
        P(("grp", "leaf"), None),
        P(("grp", "leaf"), None, None),
        P(("grp", "leaf"), None, None),
        P(),
    )

    return jax.shard_map(
        on_device, mesh=mesh, in_specs=placed, out_specs=P(None, ("grp", "leaf")), check_vma=False
    )
```

time: 313 us -> 84.3 us (0.27)
  blocking collectives: 192 us -> 12.5 us
  matrix products: 49.9 us -> 0 us
  Pallas kernels: 0 us -> 27 us
  local copies, waits for them, and re-layouts: 17.3 us -> 0.08 us
  between operations: 13.7 us -> 0.14 us
  waiting for transfers between devices: 0.16 us -> 10 us
  loops' own time: 9.74 us -> 0 us
  starting transfers between devices: 25.2 us -> 32.2 us
    psum x4 -> x0, blocking collectives: 138 us -> none  [the longest x3 95.2 us: operate(): subtree_total = lax.psum(upward, 'leaf')]
    all_gather x5 -> x0, blocking collectives: 53.8 us -> none  [the longest x1 23.1 us: on_device(): subtree_lists = lax.all_gather(inter_lists, 'leaf', axis=0, tiled=True)]
    dot_general x30 -> x0, matrix products: 49.9 us -> none  [the longest x12 33.3 us: near_slot(): product = jnp.einsum('vlp,lpq->lvq', source_vecs, kernel, precision=highest)]
    pallas_call x0 -> x9, Pallas kernels: none -> 27 us  [the longest x4 9.45 us: near_again(): call(body, field_shape, [SMEM] + [VMEM] * (len(kinds) + len(before)) + [H...]
    all_to_all x0 -> x3, starting transfers between devices: none -> 26.4 us  [on_device(): exchange = lambda x: lax.all_to_all(x, ('grp', 'leaf'), 0, 0, tiled=True)]
    ppermute x6, starting transfers between devices: 25.1 us -> 5.78 us  [the longest x1 3.19 us: on_device(): pair_window = lax.ppermute(stacked, 'leaf', inner)]
    gather x27 -> x0, local copies, waits for them, and re-layouts: 14.9 us -> none  [the longest x12 6.87 us: near_slot(): jnp.take(window_points, safe_place, axis=1).transpose(1, 0, 2)]
    all_to_all x0 -> x1, blocking collectives: none -> 12.5 us  [on_device(): exchange = lambda x: lax.all_to_all(x, ('grp', 'leaf'), 0, 0, tiled=True)]
  transfers between devices with their start and end apart: 9 -> 9, of which waited for: 0 -> 5; matrix products, arithmetic and copies ran while one was open for 21% -> 1% of each run, Pallas kernels for 0% -> 21%
where the time goes in v2:
time: 84.3 us; the launch traced here: 83.7 us
  starting transfers between devices  32.2 us (38%)
  Pallas kernels  27 us (32%)
  blocking collectives  12.5 us (15%)
  waiting for transfers between devices  10 us (12%)
  other arithmetic  1.71 us (2%)
    all_to_all x3, starting transfers between devices, on_device(): exchange = lambda x: lax.all_to_all(x, ('grp', 'leaf'), 0, 0, tiled=True)  26.4 us
    all_to_all x1, blocking collectives, on_device(): exchange = lambda x: lax.all_to_all(x, ('grp', 'leaf'), 0, 0, tiled=True)  12.5 us
    pallas_call x4, Pallas kernels, near_again(): call(body, field_shape, [SMEM] + [VMEM] * (len(kinds) + len(before)) + [H...  9.45 us
    all_to_all x3, waiting for transfers between devices, on_device(): exchange = lambda x: lax.all_to_all(x, ('grp', 'leaf'), 0, 0, tiled=True)  8.4 us
    pallas_call x1, Pallas kernels, on_device(): call(near_first_body, (field_shape, shape(couple_shape, bf16), shape(bloc...  8.08 us
    pallas_call x3, Pallas kernels, post(): call(lambda *refs: post_body(step, *refs), tuple(outs), [SMEM] + [VMEM] *...  6.66 us
    ppermute x1, starting transfers between devices, on_device(): pair_window = lax.ppermute(stacked, 'leaf', inner)  3.19 us
    pallas_call x1, Pallas kernels, on_device(): call(start_body, (shape((devices, vec + SUB, cols), f32), shape(interp.sh...  2.8 us
  transfers between devices with their start and end apart: 9, of which 5 were waited for; matrix products, arithmetic and copies ran while one was open for 1% of the time, Pallas kernels for 21%

profile of v2, /device:TPU:0, one launch (start us, length us, event | category | flops | bytes accessed | tf_op | source)
XLA Modules:
  0.0 83.7 jit_solution(12198879674988432485)
XLA Ops:
  0.0 2.8 %shard_map.82 = (f32[32,24,128]{2,1,0:T(8,128)}, f32[2,64,512]{2,1,0:T(8,128)S(1)}, f32[128,128]{1,0:T(8,128)S(1)}, f32[3,2,128]{2,1,0:T(2,128)S(1)}, s32[2,6]{1,0:T(2,128)S(1)}, /*index=5*/s32[2,16]{1,0:T(2,128)S(1)}) custom-call(f32[16,1024]{1,0:T(8,128)} %field_in.1, f32[3,1024]{1,0:T(4,128)} %points_in.1, s32[2,64]{1,0:T(2,128)} %skel_in.1, ...), custom_call_target="tpu_custom_call" | custom-call | flops 10000000 | bytes 1048576 | tf_op jit(solution)/shard_map/pallas_call | solution.py:202
  2.8 7.3 %all-to-all-start = ((f32[32,24,128]{2,1,0:T(8,128)}), f32[32,24,128]{2,1,0:T(8,128)S(1)}, u32[]{:S(2)}, u32[]{:S(2)}) async-start(f32[32,24,128]{2,1,0:T(8,128)} %get-tuple-element.22), calls=%async_computation | async-start | bytes 786432 | tf_op jit(solution)/shard_map/all_to_all | solution.py:133
  10.1 0.1 pad.2.clone
  10.2 0.9 %maximum_maximum_fusion.own.refs_5_.refs_7_ = f32[24,1024]{1,0:T(8,128)S(1)} fusion(f32[3,1024]{1,0:T(4,128)} %points_in.1, f32[16,1024]{1,0:T(8,128)} %field_in.1, f32[24]{0:T(128)S(1)} %pad.2.clone), kind=kLoop, calls=%fused_computation | loop fusion | flops 49152 | bytes 176224 | tf_op jit(solution)/shard_map/concatenate | solution.py:170
  11.1 0.7 collective-permute-start.1
  11.8 3.2 %collective-permute-start = (f32[24,1024]{1,0:T(8,128)S(1)}, f32[24,1024]{1,0:T(8,128)S(1)}, u32[]{:S(2)}, u32[]{:S(2)}) collective-permute-start(f32[24,1024]{1,0:T(8,128)S(1)} %maximum_maximum_fusion.own.refs_5_.refs_7_), channel_id=1, source_target_pairs={{0,1},{1,0},{2,3},{3,2},{4,5},{5,4},{6,7},{7,6},{8,9},{9,8},{10,11... | collective-permute-start | bytes 294920 | tf_op jit(solution)/shard_map/ppermute | solution.py:171
  15.0 0.0 collective-permute-done.1.other
  15.0 0.9 %collective-permute-done.pair = f32[24,1024]{1,0:T(8,128)S(1)} collective-permute-done((f32[24,1024]{1,0:T(8,128)S(1)}, f32[24,1024]{1,0:T(8,128)S(1)}, u32[]{:S(2)}, u32[]{:S(2)}) %collective-permute-start) | collective-permute-done | bytes 98336 | tf_op jit(solution)/shard_map/ppermute | solution.py:171
  15.9 8.1 %shard_map.83 = (f32[16,1024]{1,0:T(8,128)S(1)}, bf16[2,128,128]{2,1,0:T(8,128)(2,1)S(1)}, bf16[6,2,2,512,512]{4,3,2,1,0:T(8,128)(2,1)}) custom-call(s32[2,6]{1,0:T(2,128)S(1)} %get-tuple-element.23.lists, f32[24,1024]{1,0:T(8,128)S(1)} %maximum_maximum_fusion.own.refs_5_.refs_7_, f32[24,1024]{1,0:T(8,128)S(1)} %collective-permute-done.pair, ...), custom_call_target="tpu_custom_call" | custom-call | flops 1000000000 | bytes 1048576 | tf_op jit(solution)/shard_map/pallas_call | solution.py:450
  24.0 0.0 all-to-all-done.refs_1_
  24.0 3.1 %shard_map.84 = (f32[16,1024]{1,0:T(8,128)S(1)}, f32[32,16,128]{2,1,0:T(8,128)}, bf16[2,2048,128]{2,1,0:T(8,128)(2,1)S(1)}) custom-call(s32[2,16]{1,0:T(2,128)S(1)} %get-tuple-element.21.refs_0_, f32[32,24,128]{2,1,0:T(8,128)S(1)} %all-to-all-done.refs_1_, bf16[2,128,128]{2,1,0:T(8,128)(2,1)S(1)} %get-tuple-element.26.refs_2_, ...), custom_call_target="tpu_custom_call" | custom-call | flops 10000000 | bytes 1048576 | tf_op jit(solution)/shard_map/pallas_call | solution.py:435
  27.2 13.5 %all-to-all-start.1 = ((f32[32,16,128]{2,1,0:T(8,128)}), f32[32,16,128]{2,1,0:T(8,128)S(1)}, u32[]{:S(2)}, u32[]{:S(2)}) async-start(f32[32,16,128]{2,1,0:T(8,128)} %get-tuple-element.29), calls=%async_computation.1 | async-start | bytes 524288 | tf_op jit(solution)/shard_map/all_to_all | solution.py:133
  40.7 0.3 collective-permute-start.3
  41.0 0.7 collective-permute-start.2
  41.7 0.3 collective-permute-done.3.refs_1_
  42.0 4.0 %shard_map.85.refs_1_ = f32[16,1024]{1,0:T(8,128)S(1)} custom-call(s32[2,6]{1,0:T(2,128)S(1)} %get-tuple-element.23.lists, f32[16,1024]{1,0:T(8,128)S(1)} %get-tuple-element.30.refs_0_.refs_5_.refs_7_, f32[16,1024]{1,0:T(8,128)S(1)} %collective-permute-done.3.refs_1_, bf16[6,2,2,512,512]{4,3,2,1,0:T(8,128)(2,1)} %get-tuple-element.31.refs_2_), custom_call_target="tpu_custom_call" | custom-call | flops 100000000 | bytes 1048576 | tf_op jit(solution)/shard_map/pallas_call | solution.py:330
  46.0 0.0 collective-permute-done.2.refs_0_
  46.0 0.8 shard_map.86.refs_4_
  46.9 4.1 %all-to-all-done.1.refs_1_ = f32[32,16,128]{2,1,0:T(8,128)S(1)} async-done(((f32[32,16,128]{2,1,0:T(8,128)}), f32[32,16,128]{2,1,0:T(8,128)S(1)}, u32[]{:S(2)}, u32[]{:S(2)}) %all-to-all-start.1) | async-done | bytes 262176 | tf_op jit(solution)/shard_map/all_to_all | solution.py:133
  51.0 2.4 %shard_map.87 = (f32[16,1024]{1,0:T(8,128)S(1)}, f32[32,16,128]{2,1,0:T(8,128)}) custom-call(s32[2,16]{1,0:T(2,128)S(1)} %get-tuple-element.21.refs_0_, f32[32,16,128]{2,1,0:T(8,128)S(1)} %all-to-all-done.1.refs_1_, bf16[2,128,128]{2,1,0:T(8,128)(2,1)S(1)} %get-tuple-element.26.refs_2_, f32[2,64,512]{2,1,0:T(8,128)S(1)} %get-tuple-element.27.refs_3_, ...), custom_call_target="tpu_custom_call" | custom-call | flops 10000000 | bytes 1048576 | tf_op jit(solution)/shard_map/pallas_call | solution.py:435
  53.3 5.6 %all-to-all-start.2 = ((f32[32,16,128]{2,1,0:T(8,128)}), f32[32,16,128]{2,1,0:T(8,128)S(1)}, u32[]{:S(2)}, u32[]{:S(2)}) async-start(f32[32,16,128]{2,1,0:T(8,128)} %get-tuple-element.33), calls=%async_computation.2 | async-start | bytes 524288 | tf_op jit(solution)/shard_map/all_to_all | solution.py:133
  58.9 0.3 collective-permute-start.5
  59.3 0.7 collective-permute-start.4
  59.9 0.3 collective-permute-done.5.refs_1_
  60.3 4.0 %shard_map.88.refs_1_ = f32[16,1024]{1,0:T(8,128)S(1)} custom-call(s32[2,6]{1,0:T(2,128)S(1)} %get-tuple-element.23.lists, f32[16,1024]{1,0:T(8,128)S(1)} %get-tuple-element.34.refs_0_.refs_5_, f32[16,1024]{1,0:T(8,128)S(1)} %collective-permute-done.5.refs_1_, bf16[6,2,2,512,512]{4,3,2,1,0:T(8,128)(2,1)} %get-tuple-element.31.refs_2_), custom_call_target="tpu_custom_call" | custom-call | flops 100000000 | bytes 1048576 | tf_op jit(solution)/shard_map/pallas_call | solution.py:330
  64.3 0.0 collective-permute-done.4.refs_0_
  64.3 0.6 shard_map.89.refs_4_
  64.9 4.3 %all-to-all-done.2.refs_1_ = f32[32,16,128]{2,1,0:T(8,128)S(1)} async-done(((f32[32,16,128]{2,1,0:T(8,128)}), f32[32,16,128]{2,1,0:T(8,128)S(1)}, u32[]{:S(2)}, u32[]{:S(2)}) %all-to-all-start.2) | async-done | bytes 262176 | tf_op jit(solution)/shard_map/all_to_all | solution.py:133
  69.2 1.2 %shard_map.90 = (f32[16,1024]{1,0:T(8,128)S(1)}, f32[32,1,128]{2,1,0:T(1,128)S(1)}) custom-call(s32[2,16]{1,0:T(2,128)S(1)} %get-tuple-element.21.refs_0_, f32[32,16,128]{2,1,0:T(8,128)S(1)} %all-to-all-done.2.refs_1_, bf16[2,128,128]{2,1,0:T(8,128)(2,1)S(1)} %get-tuple-element.26.refs_2_, f32[2,64,512]{2,1,0:T(8,128)S(1)} %get-tuple-element.27.refs_3_, ...), custom_call_target="tpu_custom_call" | custom-call | flops 10000000 | bytes 1048576 | tf_op jit(solution)/shard_map/pallas_call | solution.py:435
  70.4 12.5 %all_to_all.20 = f32[32,1,128]{2,1,0:T(1,128)S(1)} all-to-all(f32[32,1,128]{2,1,0:T(1,128)S(1)} %get-tuple-element.36), channel_id=1, replica_groups=mesh['grp'=2,'leaf'=16] {'grp','leaf'}, dimensions={0} | all-to-all | bytes 32768 | tf_op jit(solution)/shard_map/all_to_all | solution.py:133
  82.9 0.1 reduce_sum.9
  83.0 0.7 broadcast_divide_fusion
  (2 shorter events, 0.0 us)
Async XLA Ops:
  2.8 21.2 %all-to-all-start = ((f32[32,24,128]{2,1,0:T(8,128)}), f32[32,24,128]{2,1,0:T(8,128)S(1)}, u32[]{:S(2)}, u32[]{:S(2)}) async-start(f32[32,24,128]{2,1,0:T(8,128)} %get-tuple-element.22), calls=%async_computation | async-start | bytes 786432 | tf_op jit(solution)/shard_map/all_to_all | solution.py:133
  11.1 3.9 %collective-permute-start.1 = (f32[24,1024]{1,0:T(8,128)S(1)}, f32[24,1024]{1,0:T(8,128)S(1)}, u32[]{:S(2)}, u32[]{:S(2)}) collective-permute-start(f32[24,1024]{1,0:T(8,128)S(1)} %maximum_maximum_fusion.own.refs_5_.refs_7_), channel_id=1, source_target_pairs={{1,2},{3,4},{5,6},{7,8},{9,10},{11,12},{13,14},{2,1},{4,3},{6,5},{... | collective-permute-start | bytes 294920 | tf_op jit(solution)/shard_map/ppermute | solution.py:172
  11.8 4.1 %collective-permute-start = (f32[24,1024]{1,0:T(8,128)S(1)}, f32[24,1024]{1,0:T(8,128)S(1)}, u32[]{:S(2)}, u32[]{:S(2)}) collective-permute-start(f32[24,1024]{1,0:T(8,128)S(1)} %maximum_maximum_fusion.own.refs_5_.refs_7_), channel_id=1, source_target_pairs={{0,1},{1,0},{2,3},{3,2},{4,5},{5,4},{6,7},{7,6},{8,9},{9,8},{10,11... | collective-permute-start | bytes 294920 | tf_op jit(solution)/shard_map/ppermute | solution.py:171
  27.2 23.8 %all-to-all-start.1 = ((f32[32,16,128]{2,1,0:T(8,128)}), f32[32,16,128]{2,1,0:T(8,128)S(1)}, u32[]{:S(2)}, u32[]{:S(2)}) async-start(f32[32,16,128]{2,1,0:T(8,128)} %get-tuple-element.29), calls=%async_computation.1 | async-start | bytes 524288 | tf_op jit(solution)/shard_map/all_to_all | solution.py:133
  40.7 1.3 %collective-permute-start.3 = (f32[16,1024]{1,0:T(8,128)S(1)}, f32[16,1024]{1,0:T(8,128)S(1)}, u32[]{:S(2)}, u32[]{:S(2)}) collective-permute-start(f32[16,1024]{1,0:T(8,128)S(1)} %get-tuple-element.30.refs_0_.refs_5_.refs_7_), channel_id=1, source_target_pairs={{0,1},{1,0},{2,3},{3,2},{4,5},{5,4},{6,7},{7,6},{8,9},{9,8},{10,11... | collective-permute-start | bytes 196616 | tf_op jit(solution)/shard_map/ppermute | solution.py:346
  41.0 5.0 %collective-permute-start.2 = (f32[16,1024]{1,0:T(8,128)S(1)}, f32[16,1024]{1,0:T(8,128)S(1)}, u32[]{:S(2)}, u32[]{:S(2)}) collective-permute-start(f32[16,1024]{1,0:T(8,128)S(1)} %get-tuple-element.30.refs_0_.refs_5_.refs_7_), channel_id=1, source_target_pairs={{1,2},{3,4},{5,6},{7,8},{9,10},{11,12},{13,14},{2,1},{4,3},{6,5},{... | collective-permute-start | bytes 196616 | tf_op jit(solution)/shard_map/ppermute | solution.py:347
  53.3 15.9 %all-to-all-start.2 = ((f32[32,16,128]{2,1,0:T(8,128)}), f32[32,16,128]{2,1,0:T(8,128)S(1)}, u32[]{:S(2)}, u32[]{:S(2)}) async-start(f32[32,16,128]{2,1,0:T(8,128)} %get-tuple-element.33), calls=%async_computation.2 | async-start | bytes 524288 | tf_op jit(solution)/shard_map/all_to_all | solution.py:133
  58.9 1.3 %collective-permute-start.5 = (f32[16,1024]{1,0:T(8,128)S(1)}, f32[16,1024]{1,0:T(8,128)S(1)}, u32[]{:S(2)}, u32[]{:S(2)}) collective-permute-start(f32[16,1024]{1,0:T(8,128)S(1)} %get-tuple-element.34.refs_0_.refs_5_), channel_id=1, source_target_pairs={{0,1},{1,0},{2,3},{3,2},{4,5},{5,4},{6,7},{7,6},{8,9},{9,8},{10,11... | collective-permute-start | bytes 196616 | tf_op jit(solution)/shard_map/ppermute | solution.py:346
  59.3 5.0 %collective-permute-start.4 = (f32[16,1024]{1,0:T(8,128)S(1)}, f32[16,1024]{1,0:T(8,128)S(1)}, u32[]{:S(2)}, u32[]{:S(2)}) collective-permute-start(f32[16,1024]{1,0:T(8,128)S(1)} %get-tuple-element.34.refs_0_.refs_5_), channel_id=1, source_target_pairs={{1,2},{3,4},{5,6},{7,8},{9,10},{11,12},{13,14},{2,1},{4,3},{6,5},{... | collective-permute-start | bytes 196616 | tf_op jit(solution)/shard_map/ppermute | solution.py:347

commit v3 on v2

--- a/solution.py
+++ b/solution.py
@@ -133,7 +133,6 @@
     exchange = lambda x: lax.all_to_all(x, ("grp", "leaf"), 0, 0, tiled=True)
     shape = jax.ShapeDtypeStruct
     field_shape = shape((vec, width), f32)
-    field_scratch = pltpu.VMEM((vec, width), f32)
     couple_rows = (groups - 1) * coarse
     far_rows = leaves * cols
     limit = max(6000, far_rows * 3 // 2)
@@ -167,15 +166,12 @@
             for i in range(leaves):
                 copies.start(("up", t, i), upward, out.at[first + i])
 
-    stacked = jnp.concatenate([vectors, points, jnp.zeros((SUB - 3, width), f32)], axis=0)
-    pair_window = lax.ppermute(stacked, "leaf", inner)
-    next_window = lax.ppermute(stacked, "leaf", outer)
-
     def start_body(
         field_in, points_in, skel_in, interp_in, transfer_in, coarse_in, near_lists_in, inter_lists_in,
-        out, interp, transfer, coarse_points, near_lists, inter_lists,
-        field, points, skel, own, up, sems,
+        out, stacked, interp, transfer, coarse_points, near_lists, inter_lists,
+        points, skel, own, up, sems,
     ):
+        field = stacked.at[pl.ds(0, vec)]
         copies = Copies(sems)
         copies.start("points", points_in, points)
         copies.start("skel", skel_in, skel)
@@ -188,6 +184,8 @@
         own[vec:] = jnp.zeros((SUB, cols), f32)
         up[vec:] = jnp.zeros((SUB, cols), f32)
         copies.wait("points", "skel")
+        stacked[vec:] = jnp.zeros((SUB, width), f32)
+        stacked[vec : vec + 3] = points[...]
         for j in range(per_dev):
             places = lax.broadcasted_iota(jnp.int32, (leaf_size, rank), 0)
             pick = (places == skel[j : j + 1, :]).astype(f32)
@@ -199,10 +197,11 @@
         send_parts(copies, out, own, up, whereabouts()[1])
         copies.finish()
 
-    payload, interp, transfer, coarse_points, near_lists, inter_lists = call(
+    payload, stacked, interp, transfer, coarse_points, near_lists, inter_lists = call(
         start_body,
         (
             shape((devices, vec + SUB, cols), f32),
+            shape((vec + SUB, width), f32),
             shape(interp.shape, f32),
             shape(transfer.shape, f32),
             shape((3, groups, coarse), f32),
@@ -210,9 +209,8 @@
             shape(inter_lists.shape, jnp.int32),
         ),
         [HBM] * 8,
-        (HBM,) + (VMEM,) * 5,
+        (HBM,) + (VMEM,) * 6,
         scratch=[
-            field_scratch,
             pltpu.VMEM((3, width), f32),
             pltpu.VMEM((per_dev, rank), jnp.int32),
             pltpu.VMEM((vec + SUB, cols), f32),
@@ -238,14 +236,82 @@
 
     def near_first_body(
         lists, own, pair, other, coarse_points, transfer,
-        near, couple, blocks_out, blocks, sems,
+        near, blocks_out, couple,
+        even, odd, factors, targets, fields, total, order, sems,
     ):
-        def out_copy(block, leaf):
+        place = whereabouts()
+        origin = own[vec : vec + 3][:, :1]
+        for leaf in range(per_dev):
+            targets[leaf] = target_factors(coordinates(own[vec : vec + 3, leaf_slice(leaf)], origin))
+            total[leaf] = jnp.zeros((vec, leaf_size), f32)
+        count = jnp.int32(0)
+        for i, (kind, j, leaf) in enumerate(entries):
+            window = (own, pair, other)[kind]
+            if leaf == 0:
+                source = kind * per_dev + j
+                factors[source] = source_factors(
+                    coordinates(window[vec : vec + 3, leaf_slice(j)], origin)
+                )
+                fields[source] = jnp.concatenate(split(window[:vec, leaf_slice(j)]), axis=0)
+            order[count] = i
+            count = count + hit(place, lists, kind, j, leaf).astype(jnp.int32)
+
+        def out_copy(i, buffer, side):
+            entry = order[i]
             return pltpu.make_async_copy(
-                blocks.at[block, leaf], blocks_out.at[block, leaf], sems.at[block * per_dev + leaf]
+                buffer, blocks_out.at[entry // per_dev, lax.rem(entry, per_dev)], sems.at[side]
             )
 
-        place = whereabouts()
+        def make(i, buffer):
+            entry = order[i]
+            source, leaf = entry // per_dev, lax.rem(entry, per_dev)
+            step = 64
+            for c in range(leaf_size // step):
+                at = slice(c * step, (c + 1) * step)
+                hi, lo = split(matern(factors[source, at], targets[leaf]))
+                buffer[0, at] = hi
+                buffer[1, at] = lo
+
+        def use(i, buffer):
+            entry = order[i]
+            source, leaf = entry // per_dev, lax.rem(entry, per_dev)
+            field = fields[source]
+            both = jnp.dot(field, buffer[0], preferred_element_type=f32)
+            rest = jnp.dot(field[:vec], buffer[1], preferred_element_type=f32)
+            total[leaf] += both[:vec] + both[vec:] + rest
+
+        make(0, even)
+        out_copy(0, even, 0).start()
+
+        def turn(i, buffer, side, last):
+            @pl.when(i >= 2)
+            def _():
+                out_copy(i - 2, buffer, side).wait()
+
+            make(i, buffer)
+            use(i - 1, last)
+            out_copy(i, buffer, side).start()
+
+        def two(t, _):
+            turn(2 * t + 1, odd, 1, even)
+
+            @pl.when(2 * t + 2 < count)
+            def _():
+                turn(2 * t + 2, even, 0, odd)
+
+            return 0
+
+        lax.fori_loop(0, count // 2, two, 0)
+        ends_even = lax.rem(count, 2) == 1
+
+        @pl.when(ends_even)
+        def _():
+            use(count - 1, even)
+
+        @pl.when(jnp.logical_not(ends_even))
+        def _():
+            use(count - 1, odd)
+
         group = place[1]
         mine = coarse_points[:, group]
         coarse_origin = mine[:, :1]
@@ -255,40 +321,35 @@
             kernel = matern(source_factors(coordinates(far, coarse_origin)), target)
             at = slice((t - 1) * coarse, t * coarse)
             couple[0, at], couple[1, at] = split(dot_nt(kernel, transfer[...]))
-        windows = (own, pair, other)
-        origin = own[vec : vec + 3][:, :1]
-        targets = [
-            target_factors(coordinates(own[vec : vec + 3, leaf_slice(leaf)], origin))
-            for leaf in range(per_dev)
-        ]
-        near[...] = jnp.zeros_like(near)
-        hits = [hit(place, lists, *entry) for entry in entries]
-        for (kind, j, leaf), found in zip(entries, hits, strict=True):
-            window = windows[kind]
-            if leaf == 0:
-                factors = source_factors(
-                    coordinates(window[vec : vec + 3, leaf_slice(j)], origin)
-                )
-            block = kind * per_dev + j
-
-            @pl.when(found)
-            def _():
-                step = 64
-                for i in range(leaf_size // step):
-                    at = slice(i * step, (i + 1) * step)
-                    hi, lo = split(matern(factors[at], targets[leaf]))
-                    blocks[block, leaf, 0, at] = hi
-                    blocks[block, leaf, 1, at] = lo
-                out_copy(block, leaf).start()
-                near[:, leaf_slice(leaf)] += dot3(
-                    window[:vec, leaf_slice(j)], blocks[block, leaf, 0], blocks[block, leaf, 1]
-                )
-
-        for (kind, j, leaf), found in zip(entries, hits, strict=True):
-
-            @pl.when(found)
-            def _():
-                out_copy(kind * per_dev + j, leaf).wait()
+        for leaf in range(per_dev):
+            near[:, leaf_slice(leaf)] = total[leaf]
+        last_even = jnp.where(ends_even, count - 1, count - 2)
+        out_copy(last_even, even, 0).wait()
+
+        @pl.when(count >= 2)
+        def _():
+            out_copy(jnp.where(ends_even, count - 2, count - 1), odd, 1).wait()
+
+    def near_first(pair, other):
+        block_shape = (2, leaf_size, leaf_size)
+        return call(
+            near_first_body,
+            (field_shape, shape(blocks_shape, bf16), shape(couple_shape, bf16)),
+            [SMEM] + [VMEM] * 5,
+            (VMEM, HBM, VMEM),
+            scratch=[
+                pltpu.VMEM(block_shape, bf16),
+                pltpu.VMEM(block_shape, bf16),
+                pltpu.VMEM((3 * per_dev, leaf_size, 6 * SUB), bf16),
+                pltpu.VMEM((per_dev, 6 * SUB, leaf_size), bf16),
+                pltpu.VMEM((3 * per_dev, 2 * vec, leaf_size), bf16),
+                pltpu.VMEM((per_dev, vec, leaf_size), f32),
+                pltpu.SMEM((len(entries) + 1,), jnp.int32),
+                pltpu.SemaphoreType.DMA((2,)),
+            ],
+            flops=10**9,
+            limit=NEAR_LIMIT,
+        )(near_lists, stacked, pair, other, coarse_points, transfer)
 
     def near_again(kinds, windows, blocks, before=()):
         chosen = [entry for entry in entries if entry[0] in kinds]
@@ -335,12 +396,7 @@
             scratch=[pltpu.VMEM(shape_here, bf16), pltpu.SemaphoreType.DMA((len(chosen),))],
             flops=10**8,
             limit=NEAR_LIMIT,
-        )(near_lists, *windows, *before, blocks)
-
-    near_scratch = [
-        pltpu.VMEM(blocks_shape, bf16),
-        pltpu.SemaphoreType.DMA((len(entries),)),
-    ]
+        )(near_lists, *windows, *before, pltpu.with_memory_space_constraint(blocks, pltpu.HBM))
 
     def halo(field):
         pair = lax.ppermute(field, "leaf", inner)
@@ -441,21 +497,15 @@
             limit=limit,
         )(inter_lists, *args)
 
+    received = exchange(payload)
+    pair, other = halo(stacked)
+    near, blocks, couple = near_first(pair, other)
+
     def again(field):
         pair, other = halo(field)
         near = near_again((0, 1), (field, pair), blocks)
         return near_again((2,), (other,), blocks, (near,))
 
-    received = exchange(payload)
-    near, couple, blocks = call(
-        near_first_body,
-        (field_shape, shape(couple_shape, bf16), shape(blocks_shape, bf16)),
-        [SMEM] + [VMEM] * 5,
-        (VMEM, VMEM, HBM),
-        scratch=near_scratch,
-        flops=10**9,
-        limit=NEAR_LIMIT,
-    )(near_lists, stacked, pair_window, next_window, coarse_points, transfer)
     term_one, payload, far = post(1, received, near, stacked)
     received = exchange(payload)
     near = again(term_one)

time: 84.3 us -> 82.9 us (0.983)
  waiting for transfers between devices: 10 us -> 11.3 us
  Pallas kernels: 27 us -> 26 us
  other arithmetic: 1.71 us -> 0.78 us
    ppermute x2 -> x0, starting transfers between devices: 3.84 us -> none  [the longest x1 3.19 us: on_device(): pair_window = lax.ppermute(stacked, 'leaf', inner)]
    ppermute x2 -> x3, starting transfers between devices: 0.63 us -> 3.82 us  [halo(): pair = lax.ppermute(field, 'leaf', inner)]
    all_to_all x3, waiting for transfers between devices: 8.4 us -> 9.62 us  [on_device(): exchange = lambda x: lax.all_to_all(x, ('grp', 'leaf'), 0, 0, tiled=True)]
    ppermute x2 -> x0, waiting for transfers between devices: 0.94 us -> none  [the longest x1 0.94 us: on_device(): pair_window = lax.ppermute(stacked, 'leaf', inner)]
    ppermute x2 -> x3, waiting for transfers between devices: 0.69 us -> 1.63 us  [halo(): pair = lax.ppermute(field, 'leaf', inner)]
    concatenate x1 -> x0, other arithmetic: 0.93 us -> none  [on_device(): jnp.concatenate([vectors, points, jnp.zeros((SUB - 3, width), f32)], axis=0)]
    pallas_call x2, Pallas kernels: 10.9 us -> 10 us  [the longest x1 7.23 us: near_first(): call(near_first_body, (field_shape, shape(blocks_shape, bf16), shape(coup...]
    ppermute x2 -> x3, starting transfers between devices: 1.31 us -> 1.97 us  [halo(): other = lax.ppermute(field, 'leaf', outer)]
  transfers between devices with their start and end apart: 9 -> 9, of which waited for: 5 -> 6; matrix products, arithmetic and copies ran while one was open for 1% -> 0% of each run, Pallas kernels for 21% -> 20%
where the time goes in v3:
time: 82.9 us; the launch traced here: 82.3 us
  starting transfers between devices  31.7 us (38%)
  Pallas kernels  26 us (31%)
  blocking collectives  12.5 us (15%)
  waiting for transfers between devices  11.3 us (14%)
    all_to_all x3, starting transfers between devices, on_device(): exchange = lambda x: lax.all_to_all(x, ('grp', 'leaf'), 0, 0, tiled=True)  25.9 us
    all_to_all x1, blocking collectives, on_device(): exchange = lambda x: lax.all_to_all(x, ('grp', 'leaf'), 0, 0, tiled=True)  12.5 us
    all_to_all x3, waiting for transfers between devices, on_device(): exchange = lambda x: lax.all_to_all(x, ('grp', 'leaf'), 0, 0, tiled=True)  9.62 us
    pallas_call x4, Pallas kernels, near_again(): call(body, field_shape, [SMEM] + [VMEM] * (len(kinds) + len(before)) + [H...  9.27 us
    pallas_call x1, Pallas kernels, near_first(): call(near_first_body, (field_shape, shape(blocks_shape, bf16), shape(coup...  7.23 us
    pallas_call x3, Pallas kernels, post(): call(lambda *refs: post_body(step, *refs), tuple(outs), [SMEM] + [VMEM] *...  6.66 us
    ppermute x3, starting transfers between devices, halo(): pair = lax.ppermute(field, 'leaf', inner)  3.82 us
    pallas_call x1, Pallas kernels, on_device(): call(start_body, (shape((devices, vec + SUB, cols), f32), shape((vec + SU...  2.79 us
  transfers between devices with their start and end apart: 9, of which 6 were waited for; matrix products, arithmetic and copies ran while one was open for 0% of the time, Pallas kernels for 20%

profile of v3, /device:TPU:0, one launch (start us, length us, event | category | flops | bytes accessed | tf_op | source)
XLA Modules:
  0.0 82.3 jit_solution(11284805235704243786)
XLA Ops:
  0.0 2.8 %shard_map.82 = (f32[32,24,128]{2,1,0:T(8,128)}, f32[24,1024]{1,0:T(8,128)S(1)}, f32[2,64,512]{2,1,0:T(8,128)S(1)}, f32[128,128]{1,0:T(8,128)S(1)}, f32[3,2,128]...) custom-call(f32[16,1024]{1,0:T(8,128)} %field_in.1, f32[3,1024]{1,0:T(4,128)} %points_in.1, ...), custom_call_target="tpu_custom_call" | custom-call | flops 10000000 | bytes 1048576 | tf_op jit(solution)/shard_map/pallas_call | solution.py:200
  2.8 7.3 %all-to-all-start = ((f32[32,24,128]{2,1,0:T(8,128)}), f32[32,24,128]{2,1,0:T(8,128)S(1)}, u32[]{:S(2)}, u32[]{:S(2)}) async-start(f32[32,24,128]{2,1,0:T(8,128)} %get-tuple-element.23), calls=%async_computation | async-start | bytes 786432 | tf_op jit(solution)/shard_map/all_to_all | solution.py:133
  10.1 0.7 collective-permute-start.1
  10.8 3.2 %collective-permute-start = (f32[24,1024]{1,0:T(8,128)S(1)}, f32[24,1024]{1,0:T(8,128)S(1)}, u32[]{:S(2)}, u32[]{:S(2)}) collective-permute-start(f32[24,1024]{1,0:T(8,128)S(1)} %get-tuple-element.25.own.refs_5_.refs_7_), channel_id=1, source_target_pairs={{0,1},{1,0},{2,3},{3,2},{4,5},{5,4},{6,7},{7,6},{8,9},{9,8},{10,11... | collective-permute-start | bytes 294920 | tf_op jit(solution)/shard_map/ppermute | solution.py:402
  14.0 0.0 collective-permute-done.1.other
  14.0 0.9 %collective-permute-done.pair = f32[24,1024]{1,0:T(8,128)S(1)} collective-permute-done((f32[24,1024]{1,0:T(8,128)S(1)}, f32[24,1024]{1,0:T(8,128)S(1)}, u32[]{:S(2)}, u32[]{:S(2)}) %collective-permute-start) | collective-permute-done | bytes 98336 | tf_op jit(solution)/shard_map/ppermute | solution.py:402
  14.9 7.2 %shard_map.83 = (f32[16,1024]{1,0:T(8,128)S(1)}, bf16[6,2,2,512,512]{4,3,2,1,0:T(8,128)(2,1)}, bf16[2,128,128]{2,1,0:T(8,128)(2,1)S(1)}) custom-call(s32[2,6]{1,0:T(2,128)S(1)} %get-tuple-element.24.lists, f32[24,1024]{1,0:T(8,128)S(1)} %get-tuple-element.25.own.refs_5_.refs_7_, f32[24,1024]{1,0:T(8,128)S(1)} %collective-permute-done.pair, ...), custom_call_target="tpu_custom_call" | custom-call | flops 1000000000 | bytes 1048576 | tf_op jit(solution)/shard_map/pallas_call | solution.py:335
  22.2 1.0 %all-to-all-done.refs_1_ = f32[32,24,128]{2,1,0:T(8,128)S(1)} async-done(((f32[32,24,128]{2,1,0:T(8,128)}), f32[32,24,128]{2,1,0:T(8,128)S(1)}, u32[]{:S(2)}, u32[]{:S(2)}) %all-to-all-start) | async-done | bytes 393248 | tf_op jit(solution)/shard_map/all_to_all | solution.py:133
  23.2 3.1 %shard_map.84 = (f32[16,1024]{1,0:T(8,128)S(1)}, f32[32,16,128]{2,1,0:T(8,128)}, bf16[2,2048,128]{2,1,0:T(8,128)(2,1)S(1)}) custom-call(s32[2,16]{1,0:T(2,128)S(1)} %get-tuple-element.22.refs_0_, f32[32,24,128]{2,1,0:T(8,128)S(1)} %all-to-all-done.refs_1_, bf16[2,128,128]{2,1,0:T(8,128)(2,1)S(1)} %get-tuple-element.28.refs_2_, ...), custom_call_target="tpu_custom_call" | custom-call | flops 10000000 | bytes 1048576 | tf_op jit(solution)/shard_map/pallas_call | solution.py:491
  26.3 13.0 %all-to-all-start.1 = ((f32[32,16,128]{2,1,0:T(8,128)}), f32[32,16,128]{2,1,0:T(8,128)S(1)}, u32[]{:S(2)}, u32[]{:S(2)}) async-start(f32[32,16,128]{2,1,0:T(8,128)} %get-tuple-element.31), calls=%async_computation.1 | async-start | bytes 524288 | tf_op jit(solution)/shard_map/all_to_all | solution.py:133
  39.4 0.3 collective-permute-start.3
  39.7 0.7 collective-permute-start.2
  40.4 0.3 collective-permute-done.3.refs_1_
  40.7 4.0 %shard_map.85.refs_1_ = f32[16,1024]{1,0:T(8,128)S(1)} custom-call(s32[2,6]{1,0:T(2,128)S(1)} %get-tuple-element.24.lists, f32[16,1024]{1,0:T(8,128)S(1)} %get-tuple-element.32.refs_0_.refs_5_.refs_7_, f32[16,1024]{1,0:T(8,128)S(1)} %collective-permute-done.3.refs_1_, bf16[6,2,2,512,512]{4,3,2,1,0:T(8,128)(2,1)} %get-tuple-element.33.refs_2_), custom_call_target="tpu_custom_call" | custom-call | flops 100000000 | bytes 1048576 | tf_op jit(solution)/shard_map/pallas_call | solution.py:391
  44.7 0.0 collective-permute-done.2.refs_0_
  44.7 0.6 shard_map.86.refs_4_
  45.4 4.3 %all-to-all-done.1.refs_1_ = f32[32,16,128]{2,1,0:T(8,128)S(1)} async-done(((f32[32,16,128]{2,1,0:T(8,128)}), f32[32,16,128]{2,1,0:T(8,128)S(1)}, u32[]{:S(2)}, u32[]{:S(2)}) %all-to-all-start.1) | async-done | bytes 262176 | tf_op jit(solution)/shard_map/all_to_all | solution.py:133
  49.6 2.4 %shard_map.87 = (f32[16,1024]{1,0:T(8,128)S(1)}, f32[32,16,128]{2,1,0:T(8,128)}) custom-call(s32[2,16]{1,0:T(2,128)S(1)} %get-tuple-element.22.refs_0_, f32[32,16,128]{2,1,0:T(8,128)S(1)} %all-to-all-done.1.refs_1_, bf16[2,128,128]{2,1,0:T(8,128)(2,1)S(1)} %get-tuple-element.28.refs_2_, f32[2,64,512]{2,1,0:T(8,128)S(1)} %get-tuple-element.29.refs_3_, ...), custom_call_target="tpu_custom_call" | custom-call | flops 10000000 | bytes 1048576 | tf_op jit(solution)/shard_map/pallas_call | solution.py:491
  52.0 5.5 %all-to-all-start.2 = ((f32[32,16,128]{2,1,0:T(8,128)}), f32[32,16,128]{2,1,0:T(8,128)S(1)}, u32[]{:S(2)}, u32[]{:S(2)}) async-start(f32[32,16,128]{2,1,0:T(8,128)} %get-tuple-element.35), calls=%async_computation.2 | async-start | bytes 524288 | tf_op jit(solution)/shard_map/all_to_all | solution.py:133
  57.6 0.3 collective-permute-start.5
  57.9 0.7 collective-permute-start.4
  58.6 0.3 collective-permute-done.5.refs_1_
  58.9 4.0 %shard_map.88.refs_1_ = f32[16,1024]{1,0:T(8,128)S(1)} custom-call(s32[2,6]{1,0:T(2,128)S(1)} %get-tuple-element.24.lists, f32[16,1024]{1,0:T(8,128)S(1)} %get-tuple-element.36.refs_0_.refs_5_, f32[16,1024]{1,0:T(8,128)S(1)} %collective-permute-done.5.refs_1_, bf16[6,2,2,512,512]{4,3,2,1,0:T(8,128)(2,1)} %get-tuple-element.33.refs_2_), custom_call_target="tpu_custom_call" | custom-call | flops 100000000 | bytes 1048576 | tf_op jit(solution)/shard_map/pallas_call | solution.py:391
  62.9 0.0 collective-permute-done.4.refs_0_
  62.9 0.6 shard_map.89.refs_4_
  63.6 4.3 %all-to-all-done.2.refs_1_ = f32[32,16,128]{2,1,0:T(8,128)S(1)} async-done(((f32[32,16,128]{2,1,0:T(8,128)}), f32[32,16,128]{2,1,0:T(8,128)S(1)}, u32[]{:S(2)}, u32[]{:S(2)}) %all-to-all-start.2) | async-done | bytes 262176 | tf_op jit(solution)/shard_map/all_to_all | solution.py:133
  67.8 1.2 %shard_map.90 = (f32[16,1024]{1,0:T(8,128)S(1)}, f32[32,1,128]{2,1,0:T(1,128)S(1)}) custom-call(s32[2,16]{1,0:T(2,128)S(1)} %get-tuple-element.22.refs_0_, f32[32,16,128]{2,1,0:T(8,128)S(1)} %all-to-all-done.2.refs_1_, bf16[2,128,128]{2,1,0:T(8,128)(2,1)S(1)} %get-tuple-element.28.refs_2_, f32[2,64,512]{2,1,0:T(8,128)S(1)} %get-tuple-element.29.refs_3_, ...), custom_call_target="tpu_custom_call" | custom-call | flops 10000000 | bytes 1048576 | tf_op jit(solution)/shard_map/pallas_call | solution.py:491
  69.0 12.5 %all_to_all.20 = f32[32,1,128]{2,1,0:T(1,128)S(1)} all-to-all(f32[32,1,128]{2,1,0:T(1,128)S(1)} %get-tuple-element.38), channel_id=1, replica_groups=mesh['grp'=2,'leaf'=16] {'grp','leaf'}, dimensions={0} | all-to-all | bytes 32768 | tf_op jit(solution)/shard_map/all_to_all | solution.py:133
  81.6 0.1 reduce_sum.9
  81.6 0.7 broadcast_divide_fusion
  (1 shorter events, 0.0 us)
Async XLA Ops:
  2.8 20.4 %all-to-all-start = ((f32[32,24,128]{2,1,0:T(8,128)}), f32[32,24,128]{2,1,0:T(8,128)S(1)}, u32[]{:S(2)}, u32[]{:S(2)}) async-start(f32[32,24,128]{2,1,0:T(8,128)} %get-tuple-element.23), calls=%async_computation | async-start | bytes 786432 | tf_op jit(solution)/shard_map/all_to_all | solution.py:133
  10.1 3.9 %collective-permute-start.1 = (f32[24,1024]{1,0:T(8,128)S(1)}, f32[24,1024]{1,0:T(8,128)S(1)}, u32[]{:S(2)}, u32[]{:S(2)}) collective-permute-start(f32[24,1024]{1,0:T(8,128)S(1)} %get-tuple-element.25.own.refs_5_.refs_7_), channel_id=1, source_target_pairs={{1,2},{3,4},{5,6},{7,8},{9,10},{11,12},{13,14},{2,1},{4,3},{6,5},{... | collective-permute-start | bytes 294920 | tf_op jit(solution)/shard_map/ppermute | solution.py:403
  10.8 4.1 %collective-permute-start = (f32[24,1024]{1,0:T(8,128)S(1)}, f32[24,1024]{1,0:T(8,128)S(1)}, u32[]{:S(2)}, u32[]{:S(2)}) collective-permute-start(f32[24,1024]{1,0:T(8,128)S(1)} %get-tuple-element.25.own.refs_5_.refs_7_), channel_id=1, source_target_pairs={{0,1},{1,0},{2,3},{3,2},{4,5},{5,4},{6,7},{7,6},{8,9},{9,8},{10,11... | collective-permute-start | bytes 294920 | tf_op jit(solution)/shard_map/ppermute | solution.py:402
  26.3 23.3 %all-to-all-start.1 = ((f32[32,16,128]{2,1,0:T(8,128)}), f32[32,16,128]{2,1,0:T(8,128)S(1)}, u32[]{:S(2)}, u32[]{:S(2)}) async-start(f32[32,16,128]{2,1,0:T(8,128)} %get-tuple-element.31), calls=%async_computation.1 | async-start | bytes 524288 | tf_op jit(solution)/shard_map/all_to_all | solution.py:133
  39.4 1.3 %collective-permute-start.3 = (f32[16,1024]{1,0:T(8,128)S(1)}, f32[16,1024]{1,0:T(8,128)S(1)}, u32[]{:S(2)}, u32[]{:S(2)}) collective-permute-start(f32[16,1024]{1,0:T(8,128)S(1)} %get-tuple-element.32.refs_0_.refs_5_.refs_7_), channel_id=1, source_target_pairs={{0,1},{1,0},{2,3},{3,2},{4,5},{5,4},{6,7},{7,6},{8,9},{9,8},{10,11... | collective-permute-start | bytes 196616 | tf_op jit(solution)/shard_map/ppermute | solution.py:402
  39.7 5.0 %collective-permute-start.2 = (f32[16,1024]{1,0:T(8,128)S(1)}, f32[16,1024]{1,0:T(8,128)S(1)}, u32[]{:S(2)}, u32[]{:S(2)}) collective-permute-start(f32[16,1024]{1,0:T(8,128)S(1)} %get-tuple-element.32.refs_0_.refs_5_.refs_7_), channel_id=1, source_target_pairs={{1,2},{3,4},{5,6},{7,8},{9,10},{11,12},{13,14},{2,1},{4,3},{6,5},{... | collective-permute-start | bytes 196616 | tf_op jit(solution)/shard_map/ppermute | solution.py:403
  52.0 15.8 %all-to-all-start.2 = ((f32[32,16,128]{2,1,0:T(8,128)}), f32[32,16,128]{2,1,0:T(8,128)S(1)}, u32[]{:S(2)}, u32[]{:S(2)}) async-start(f32[32,16,128]{2,1,0:T(8,128)} %get-tuple-element.35), calls=%async_computation.2 | async-start | bytes 524288 | tf_op jit(solution)/shard_map/all_to_all | solution.py:133
  57.6 1.3 %collective-permute-start.5 = (f32[16,1024]{1,0:T(8,128)S(1)}, f32[16,1024]{1,0:T(8,128)S(1)}, u32[]{:S(2)}, u32[]{:S(2)}) collective-permute-start(f32[16,1024]{1,0:T(8,128)S(1)} %get-tuple-element.36.refs_0_.refs_5_), channel_id=1, source_target_pairs={{0,1},{1,0},{2,3},{3,2},{4,5},{5,4},{6,7},{7,6},{8,9},{9,8},{10,11... | collective-permute-start | bytes 196616 | tf_op jit(solution)/shard_map/ppermute | solution.py:402
  57.9 5.0 %collective-permute-start.4 = (f32[16,1024]{1,0:T(8,128)S(1)}, f32[16,1024]{1,0:T(8,128)S(1)}, u32[]{:S(2)}, u32[]{:S(2)}) collective-permute-start(f32[16,1024]{1,0:T(8,128)S(1)} %get-tuple-element.36.refs_0_.refs_5_), channel_id=1, source_target_pairs={{1,2},{3,4},{5,6},{7,8},{9,10},{11,12},{13,14},{2,1},{4,3},{6,5},{... | collective-permute-start | bytes 196616 | tf_op jit(solution)/shard_map/ppermute | solution.py:403

commit v4 on v3

--- a/solution.py
+++ b/solution.py
@@ -9,7 +9,6 @@
 log2_e = 1.4426950408889634
 centre = 0.05
 half_width = 0.05
-highest = lax.Precision.HIGHEST
 f32 = jnp.float32
 bf16 = jnp.bfloat16
 
@@ -33,14 +32,14 @@
     return both[:rows] + both[rows:] + jnp.dot(hi, right_lo, preferred_element_type=f32)
 
 
-def dot_nt(left, right):
-    return lax.dot_general(
-        left, right, (((1,), (1,)), ((), ())), precision=highest, preferred_element_type=f32
+def dot3_nt(left, right_hi, right_lo):
+    rows = left.shape[0]
+    hi, lo = split(left)
+    dot = lambda a, b: lax.dot_general(
+        a, b, (((1,), (1,)), ((), ())), preferred_element_type=f32
     )
-
-
-def dot_full(left, right):
-    return jnp.dot(left, right, precision=highest, preferred_element_type=f32)
+    both = dot(jnp.concatenate([hi, lo], axis=0), right_hi)
+    return both[:rows] + both[rows:] + dot(hi, right_lo)
 
 
 def three_parts(x):
@@ -152,32 +151,37 @@
             found = jnp.logical_or(found, lists[leaf, slot] == spot)
         return found
 
-    def coefficients(field, interp, transfer):
-        coeffs = jnp.concatenate(
-            [dot_nt(field[:, leaf_slice(j)], interp[j]) for j in range(per_dev)], axis=1
+    def coefficients(field, interp):
+        return jnp.concatenate(
+            [
+                dot3_nt(field[:, leaf_slice(j)], interp[0, j], interp[1, j])
+                for j in range(per_dev)
+            ],
+            axis=1,
         )
-        return coeffs, dot_full(coeffs, transfer[...])
-
-    def send_parts(copies, out, own, upward, group):
+
+    def send_all(copies, out, own, up, coeffs, transfer, group):
+        own[:vec] = coeffs
         for i in range(leaves):
             copies.start(("own", i), own, out.at[group * leaves + i])
+        up[:vec] = dot3(coeffs, transfer[0], transfer[1])
         for t in range(1, groups):
             first = lax.rem(group + t, groups) * leaves
             for i in range(leaves):
-                copies.start(("up", t, i), upward, out.at[first + i])
+                copies.start(("up", t, i), up, out.at[first + i])
 
     def start_body(
         field_in, points_in, skel_in, interp_in, transfer_in, coarse_in, near_lists_in, inter_lists_in,
         out, stacked, interp, transfer, coarse_points, near_lists, inter_lists,
-        points, skel, own, up, sems,
+        points, skel, whole_interp, whole_transfer, own, up, sems,
     ):
         field = stacked.at[pl.ds(0, vec)]
         copies = Copies(sems)
         copies.start("points", points_in, points)
         copies.start("skel", skel_in, skel)
         copies.start("field", field_in, field)
-        copies.start("interp", interp_in, interp)
-        copies.start("transfer", transfer_in, transfer)
+        copies.start("interp", interp_in, whole_interp)
+        copies.start("transfer", transfer_in, whole_transfer)
         copies.start("coarse", coarse_in, coarse_points)
         copies.start("near_lists", near_lists_in, near_lists)
         copies.start("inter_lists", inter_lists_in, inter_lists)
@@ -188,13 +192,20 @@
         stacked[vec : vec + 3] = points[...]
         for j in range(per_dev):
             places = lax.broadcasted_iota(jnp.int32, (leaf_size, rank), 0)
-            pick = (places == skel[j : j + 1, :]).astype(f32)
-            own[vec : vec + 3, j * rank : (j + 1) * rank] = dot_full(points[:, leaf_slice(j)], pick)
-        copies.wait("field", "interp", "transfer")
-        coeffs, upward = coefficients(field, interp, transfer)
-        own[:vec] = coeffs
-        up[:vec] = upward
-        send_parts(copies, out, own, up, whereabouts()[1])
+            pick = (places == skel[j : j + 1, :]).astype(f32).astype(bf16)
+            parts = jnp.concatenate(
+                three_parts(stacked[vec:, leaf_slice(j)]), axis=0
+            ).astype(bf16)
+            spots = jnp.dot(parts, pick, preferred_element_type=f32)
+            spots = spots[:SUB] + spots[SUB : 2 * SUB] + spots[2 * SUB :]
+            own[vec:, j * rank : (j + 1) * rank] = spots
+        copies.wait("interp", "field")
+        for j in range(per_dev):
+            interp[0, j], interp[1, j] = split(whole_interp[j])
+        coeffs = coefficients(field, interp)
+        copies.wait("transfer")
+        transfer[0], transfer[1] = split(whole_transfer[...])
+        send_all(copies, out, own, up, coeffs, transfer, whereabouts()[1])
         copies.finish()
 
     payload, stacked, interp, transfer, coarse_points, near_lists, inter_lists = call(
@@ -202,8 +213,8 @@
         (
             shape((devices, vec + SUB, cols), f32),
             shape((vec + SUB, width), f32),
-            shape(interp.shape, f32),
-            shape(transfer.shape, f32),
+            shape((2, *interp.shape), bf16),
+            shape((2, *transfer.shape), bf16),
             shape((3, groups, coarse), f32),
             shape(near_lists.shape, jnp.int32),
             shape(inter_lists.shape, jnp.int32),
@@ -213,6 +224,8 @@
         scratch=[
             pltpu.VMEM((3, width), f32),
             pltpu.VMEM((per_dev, rank), jnp.int32),
+            pltpu.VMEM(interp.shape, f32),
+            pltpu.VMEM(transfer.shape, f32),
             pltpu.VMEM((vec + SUB, cols), f32),
             pltpu.VMEM((vec + SUB, cols), f32),
             pltpu.SemaphoreType.DMA((8 + devices,)),
@@ -320,7 +333,7 @@
             far = coarse_points[:, lax.rem(group + t, groups)]
             kernel = matern(source_factors(coordinates(far, coarse_origin)), target)
             at = slice((t - 1) * coarse, t * coarse)
-            couple[0, at], couple[1, at] = split(dot_nt(kernel, transfer[...]))
+            couple[0, at], couple[1, at] = split(dot3_nt(kernel, transfer[0], transfer[1]))
         for leaf in range(per_dev):
             near[:, leaf_slice(leaf)] = total[leaf]
         last_even = jnp.where(ends_even, count - 1, count - 2)
@@ -423,37 +436,35 @@
                 far[0, at] = hi
                 far[1, at] = lo
 
-    far_shape = (2, far_rows, cols)
-
-    def post_body(step, lists, received, couple, interp, near, field, *rest):
-        rest = list(rest)
-        far, before = (None, None) if step == 1 else rest[:2]
-        rest = rest if step == 1 else rest[2:]
-        transfer = rest.pop(0) if step < 3 else None
-        out, send = rest[:2]
+    far_shape = (2, far_rows + couple_rows, cols)
+
+    def post_body(step, *refs):
+        refs = list(refs)
+        lists, couple = (refs.pop(0), refs.pop(0)) if step == 1 else (None, None)
+        received, interp, near, field = refs[:4]
+        refs = refs[4:]
+        far, before = (None, None) if step == 1 else (refs.pop(0), refs.pop(0))
+        transfer = refs.pop(0) if step < 3 else None
+        out, send = refs.pop(0), refs.pop(0)
         place = whereabouts()
         group = place[1]
         if step == 1:
-            far = rest[2]
+            far = refs.pop(0)
             origin = received[group * leaves + place[0], vec : vec + 3][:, :1]
             build_far(place, lists, received, origin, far)
-        coeffs = jnp.concatenate(
-            [received[group * leaves + i, :vec] for i in range(leaves)], axis=1
-        )
-        totals = []
+            far[:, far_rows:] = couple[...]
+        parts = [received[group * leaves + i, :vec] for i in range(leaves)]
         for t in range(1, groups):
             first = lax.rem(group + t, groups) * leaves
-            parts = [received[first + i, :vec] for i in range(leaves)]
-            while len(parts) > 1:
-                parts = [sum(parts[i : i + 2]) for i in range(0, len(parts), 2)]
-            totals.append(parts[0])
-        down = dot3(coeffs, far[0], far[1])
-        if totals:
-            down = down + dot3(jnp.concatenate(totals, axis=1), couple[0], couple[1])
+            sums = [received[first + i, :vec] for i in range(leaves)]
+            while len(sums) > 1:
+                sums = [sum(sums[i : i + 2]) for i in range(0, len(sums), 2)]
+            parts += sums
+        down = dot3(jnp.concatenate(parts, axis=1), far[0], far[1])
         news = []
         for j in range(per_dev):
             here = leaf_slice(j)
-            far_part = dot_full(down[:, j * rank : (j + 1) * rank], interp[j])
+            far_part = dot3(down[:, j * rank : (j + 1) * rank], interp[0, j], interp[1, j])
             applied = (near[:, here] + far_part) * (1.0 / (leaf_size * slots))
             term = (applied - centre * field[:vec, here]) * (1.0 / half_width)
             if step > 1:
@@ -461,13 +472,11 @@
             news.append(term)
             out[:, here] = term
         if step < 3:
-            coeffs, upward = coefficients(jnp.concatenate(news, axis=1), interp, transfer)
-            for i in range(leaves):
-                send[group * leaves + i] = coeffs
-            for t in range(1, groups):
-                first = lax.rem(group + t, groups) * leaves
-                for i in range(leaves):
-                    send[first + i] = upward
+            own, up, sems = refs
+            copies = Copies(sems)
+            coeffs = coefficients(jnp.concatenate(news, axis=1), interp)
+            send_all(copies, send, own, up, coeffs, transfer, group)
+            copies.finish()
         else:
             squares = None
             for term in news:
@@ -483,19 +492,32 @@
     def post(step, received, near, field, *rest):
         send_shape = (devices, vec, cols) if step < 3 else (devices, 1, 128)
         outs = [field_shape, shape(send_shape, f32)]
+        specs = [VMEM, HBM if step < 3 else VMEM]
+        args = [received, interp, near, field, *rest]
         if step == 1:
             outs.append(shape(far_shape, bf16))
-        args = [received, couple, interp, near, field, *rest]
+            specs.append(VMEM)
+            args = [inter_lists, couple, *args]
+        scratch = []
         if step < 3:
             args.append(transfer)
+            scratch = [
+                pltpu.VMEM((vec, cols), f32),
+                pltpu.VMEM((vec, cols), f32),
+                pltpu.SemaphoreType.DMA((devices,)),
+            ]
+        in_specs = [VMEM] * len(args)
+        if step == 1:
+            in_specs[0] = SMEM
         return call(
             lambda *refs: post_body(step, *refs),
             tuple(outs),
-            [SMEM] + [VMEM] * len(args),
-            (VMEM,) * len(outs),
+            in_specs,
+            tuple(specs),
+            scratch=scratch,
             flops=10**7,
             limit=limit,
-        )(inter_lists, *args)
+        )(*args)
 
     received = exchange(payload)
     pair, other = halo(stacked)

time: 82.9 us -> 81.5 us (0.983)
  Pallas kernels: 26 us -> 24.5 us
    pallas_call x3, Pallas kernels: 6.66 us -> 5.52 us  [post(): call(lambda *refs: post_body(step, *refs), tuple(outs), in_specs, tuple(s...]
where the time goes in v4:
time: 81.5 us; the launch traced here: 80.9 us
  starting transfers between devices  31.7 us (39%)
  Pallas kernels  24.5 us (30%)
  blocking collectives  12.5 us (15%)
  waiting for transfers between devices  11.2 us (14%)
    all_to_all x3, starting transfers between devices, on_device(): exchange = lambda x: lax.all_to_all(x, ('grp', 'leaf'), 0, 0, tiled=True)  25.9 us
    all_to_all x1, blocking collectives, on_device(): exchange = lambda x: lax.all_to_all(x, ('grp', 'leaf'), 0, 0, tiled=True)  12.5 us
    all_to_all x3, waiting for transfers between devices, on_device(): exchange = lambda x: lax.all_to_all(x, ('grp', 'leaf'), 0, 0, tiled=True)  9.59 us
    pallas_call x4, Pallas kernels, near_again(): call(body, field_shape, [SMEM] + [VMEM] * (len(kinds) + len(before)) + [H...  9.27 us
    pallas_call x1, Pallas kernels, near_first(): call(near_first_body, (field_shape, shape(blocks_shape, bf16), shape(coup...  7.26 us
    pallas_call x3, Pallas kernels, post(): call(lambda *refs: post_body(step, *refs), tuple(outs), in_specs, tuple(s...  5.52 us
    ppermute x3, starting transfers between devices, halo(): pair = lax.ppermute(field, 'leaf', inner)  3.82 us
    pallas_call x1, Pallas kernels, on_device(): call(start_body, (shape((devices, vec + SUB, cols), f32), shape((vec + SU...  2.49 us
  transfers between devices with their start and end apart: 9, of which 6 were waited for; matrix products, arithmetic and copies ran while one was open for 0% of the time, Pallas kernels for 20%

profile of v4, /device:TPU:0, one launch (start us, length us, event | category | flops | bytes accessed | tf_op | source)
XLA Modules:
  0.0 80.9 jit_solution(1766499385486839325)
XLA Ops:
  0.0 2.5 %shard_map.82 = (f32[32,24,128]{2,1,0:T(8,128)}, f32[24,1024]{1,0:T(8,128)S(1)}, bf16[2,2,64,512]{3,2,1,0:T(8,128)(2,1)S(1)}, bf16[2,128,128]{2,1,0:T(8,128)(2,1...) custom-call(f32[16,1024]{1,0:T(8,128)} %field_in.1, f32[3,1024]{1,0:T(4,128)} %points_in.1, ...), custom_call_target="tpu_custom_call" | custom-call | flops 10000000 | bytes 1048576 | tf_op jit(solution)/shard_map/pallas_call | solution.py:211
  2.5 7.3 %all-to-all-start = ((f32[32,24,128]{2,1,0:T(8,128)}), f32[32,24,128]{2,1,0:T(8,128)S(1)}, u32[]{:S(2)}, u32[]{:S(2)}) async-start(f32[32,24,128]{2,1,0:T(8,128)} %get-tuple-element.28), calls=%async_computation | async-start | bytes 786432 | tf_op jit(solution)/shard_map/all_to_all | solution.py:132
  9.8 0.7 collective-permute-start.1
  10.5 3.2 %collective-permute-start = (f32[24,1024]{1,0:T(8,128)S(1)}, f32[24,1024]{1,0:T(8,128)S(1)}, u32[]{:S(2)}, u32[]{:S(2)}) collective-permute-start(f32[24,1024]{1,0:T(8,128)S(1)} %get-tuple-element.24.own.refs_5_), channel_id=1, source_target_pairs={{0,1},{1,0},{2,3},{3,2},{4,5},{5,4},{6,7},{7,6},{8,9},{9,8},{10,11... | collective-permute-start | bytes 294920 | tf_op jit(solution)/shard_map/ppermute | solution.py:415
  13.7 0.0 collective-permute-done.1.other
  13.7 0.9 %collective-permute-done.pair = f32[24,1024]{1,0:T(8,128)S(1)} collective-permute-done((f32[24,1024]{1,0:T(8,128)S(1)}, f32[24,1024]{1,0:T(8,128)S(1)}, u32[]{:S(2)}, u32[]{:S(2)}) %collective-permute-start) | collective-permute-done | bytes 98336 | tf_op jit(solution)/shard_map/ppermute | solution.py:415
  14.6 7.3 %shard_map.83 = (f32[16,1024]{1,0:T(8,128)S(1)}, bf16[6,2,2,512,512]{4,3,2,1,0:T(8,128)(2,1)}, bf16[2,128,128]{2,1,0:T(8,128)(2,1)S(1)}) custom-call(s32[2,6]{1,0:T(2,128)S(1)} %get-tuple-element.23.lists, f32[24,1024]{1,0:T(8,128)S(1)} %get-tuple-element.24.own.refs_5_, f32[24,1024]{1,0:T(8,128)S(1)} %collective-permute-done.pair, ...), custom_call_target="tpu_custom_call" | custom-call | flops 1000000000 | bytes 1048576 | tf_op jit(solution)/shard_map/pallas_call | solution.py:348
  21.9 1.0 %all-to-all-done.refs_2_ = f32[32,24,128]{2,1,0:T(8,128)S(1)} async-done(((f32[32,24,128]{2,1,0:T(8,128)}), f32[32,24,128]{2,1,0:T(8,128)S(1)}, u32[]{:S(2)}, u32[]{:S(2)}) %all-to-all-start) | async-done | bytes 393248 | tf_op jit(solution)/shard_map/all_to_all | solution.py:132
  22.9 3.1 %shard_map.84 = (f32[16,1024]{1,0:T(8,128)S(1)}, f32[32,16,128]{2,1,0:T(8,128)}, bf16[2,2176,128]{2,1,0:T(8,128)(2,1)S(1)}) custom-call(s32[2,16]{1,0:T(2,128)S(1)} %get-tuple-element.22.refs_0_, bf16[2,128,128]{2,1,0:T(8,128)(2,1)S(1)} %get-tuple-element.27.refs_1_, f32[32,24,128]{2,1,0:T(8,128)S(1)} %all-to-all-done.refs_2_, ...), custom_call_target="tpu_custom_call" | custom-call | flops 10000000 | bytes 1048576 | tf_op jit(solution)/shard_map/pallas_call | solution.py:512
  26.0 13.1 %all-to-all-start.1 = ((f32[32,16,128]{2,1,0:T(8,128)}), f32[32,16,128]{2,1,0:T(8,128)S(1)}, u32[]{:S(2)}, u32[]{:S(2)}) async-start(f32[32,16,128]{2,1,0:T(8,128)} %get-tuple-element.31), calls=%async_computation.1 | async-start | bytes 524288 | tf_op jit(solution)/shard_map/all_to_all | solution.py:132
  39.1 0.3 collective-permute-start.3
  39.4 0.7 collective-permute-start.2
  40.1 0.3 collective-permute-done.3.refs_1_
  40.4 4.0 %shard_map.85.refs_1_ = f32[16,1024]{1,0:T(8,128)S(1)} custom-call(s32[2,6]{1,0:T(2,128)S(1)} %get-tuple-element.23.lists, f32[16,1024]{1,0:T(8,128)S(1)} %get-tuple-element.32.refs_0_.refs_3_.refs_5_, f32[16,1024]{1,0:T(8,128)S(1)} %collective-permute-done.3.refs_1_, bf16[6,2,2,512,512]{4,3,2,1,0:T(8,128)(2,1)} %get-tuple-element.33.refs_2_), custom_call_target="tpu_custom_call" | custom-call | flops 100000000 | bytes 1048576 | tf_op jit(solution)/shard_map/pallas_call | solution.py:404
  44.4 0.0 collective-permute-done.2.refs_0_
  44.5 0.6 shard_map.86.refs_2_
  45.1 4.3 %all-to-all-done.1.refs_0_ = f32[32,16,128]{2,1,0:T(8,128)S(1)} async-done(((f32[32,16,128]{2,1,0:T(8,128)}), f32[32,16,128]{2,1,0:T(8,128)S(1)}, u32[]{:S(2)}, u32[]{:S(2)}) %all-to-all-start.1) | async-done | bytes 262176 | tf_op jit(solution)/shard_map/all_to_all | solution.py:132
  49.4 1.8 %shard_map.87 = (f32[16,1024]{1,0:T(8,128)S(1)}, f32[32,16,128]{2,1,0:T(8,128)}) custom-call(f32[32,16,128]{2,1,0:T(8,128)S(1)} %all-to-all-done.1.refs_0_, bf16[2,2,64,512]{3,2,1,0:T(8,128)(2,1)S(1)} %get-tuple-element.29.refs_3_.refs_1_, f32[16,1024]{1,0:T(8,128)S(1)} %shard_map.86.refs_2_, f32[16,1024]{1,0:T(8,128)S(1)} %get-tuple-element.32.refs_0_.refs_3_.refs_5_, ...), custom_call_target="tpu_custom_call" | custom-call | flops 10000000 | bytes 1048576 | tf_op jit(solution)/shard_map/pallas_call | solution.py:512
  51.2 5.5 %all-to-all-start.2 = ((f32[32,16,128]{2,1,0:T(8,128)}), f32[32,16,128]{2,1,0:T(8,128)S(1)}, u32[]{:S(2)}, u32[]{:S(2)}) async-start(f32[32,16,128]{2,1,0:T(8,128)} %get-tuple-element.35), calls=%async_computation.2 | async-start | bytes 524288 | tf_op jit(solution)/shard_map/all_to_all | solution.py:132
  56.7 0.3 collective-permute-start.5
  57.1 0.7 collective-permute-start.4
  57.7 0.3 collective-permute-done.5.refs_1_
  58.1 4.0 %shard_map.88.refs_1_ = f32[16,1024]{1,0:T(8,128)S(1)} custom-call(s32[2,6]{1,0:T(2,128)S(1)} %get-tuple-element.23.lists, f32[16,1024]{1,0:T(8,128)S(1)} %get-tuple-element.36.refs_0_.refs_3_, f32[16,1024]{1,0:T(8,128)S(1)} %collective-permute-done.5.refs_1_, bf16[6,2,2,512,512]{4,3,2,1,0:T(8,128)(2,1)} %get-tuple-element.33.refs_2_), custom_call_target="tpu_custom_call" | custom-call | flops 100000000 | bytes 1048576 | tf_op jit(solution)/shard_map/pallas_call | solution.py:404
  62.1 0.0 collective-permute-done.4.refs_0_
  62.1 0.6 shard_map.89.refs_2_
  62.7 4.3 %all-to-all-done.2.refs_0_ = f32[32,16,128]{2,1,0:T(8,128)S(1)} async-done(((f32[32,16,128]{2,1,0:T(8,128)}), f32[32,16,128]{2,1,0:T(8,128)S(1)}, u32[]{:S(2)}, u32[]{:S(2)}) %all-to-all-start.2) | async-done | bytes 262176 | tf_op jit(solution)/shard_map/all_to_all | solution.py:132
  67.0 0.6 shard_map.90
  67.6 12.5 %all_to_all.20 = f32[32,1,128]{2,1,0:T(1,128)S(1)} all-to-all(f32[32,1,128]{2,1,0:T(1,128)S(1)} %get-tuple-element.38), channel_id=1, replica_groups=mesh['grp'=2,'leaf'=16] {'grp','leaf'}, dimensions={0} | all-to-all | bytes 32768 | tf_op jit(solution)/shard_map/all_to_all | solution.py:132
  80.2 0.1 reduce_sum.9
  80.2 0.7 broadcast_divide_fusion
  (1 shorter events, 0.0 us)
Async XLA Ops:
  2.5 20.4 %all-to-all-start = ((f32[32,24,128]{2,1,0:T(8,128)}), f32[32,24,128]{2,1,0:T(8,128)S(1)}, u32[]{:S(2)}, u32[]{:S(2)}) async-start(f32[32,24,128]{2,1,0:T(8,128)} %get-tuple-element.28), calls=%async_computation | async-start | bytes 786432 | tf_op jit(solution)/shard_map/all_to_all | solution.py:132
  9.8 3.9 %collective-permute-start.1 = (f32[24,1024]{1,0:T(8,128)S(1)}, f32[24,1024]{1,0:T(8,128)S(1)}, u32[]{:S(2)}, u32[]{:S(2)}) collective-permute-start(f32[24,1024]{1,0:T(8,128)S(1)} %get-tuple-element.24.own.refs_5_), channel_id=1, source_target_pairs={{1,2},{3,4},{5,6},{7,8},{9,10},{11,12},{13,14},{2,1},{4,3},{6,5},{... | collective-permute-start | bytes 294920 | tf_op jit(solution)/shard_map/ppermute | solution.py:416
  10.5 4.1 %collective-permute-start = (f32[24,1024]{1,0:T(8,128)S(1)}, f32[24,1024]{1,0:T(8,128)S(1)}, u32[]{:S(2)}, u32[]{:S(2)}) collective-permute-start(f32[24,1024]{1,0:T(8,128)S(1)} %get-tuple-element.24.own.refs_5_), channel_id=1, source_target_pairs={{0,1},{1,0},{2,3},{3,2},{4,5},{5,4},{6,7},{7,6},{8,9},{9,8},{10,11... | collective-permute-start | bytes 294920 | tf_op jit(solution)/shard_map/ppermute | solution.py:415
  26.0 23.3 %all-to-all-start.1 = ((f32[32,16,128]{2,1,0:T(8,128)}), f32[32,16,128]{2,1,0:T(8,128)S(1)}, u32[]{:S(2)}, u32[]{:S(2)}) async-start(f32[32,16,128]{2,1,0:T(8,128)} %get-tuple-element.31), calls=%async_computation.1 | async-start | bytes 524288 | tf_op jit(solution)/shard_map/all_to_all | solution.py:132
  39.1 1.3 %collective-permute-start.3 = (f32[16,1024]{1,0:T(8,128)S(1)}, f32[16,1024]{1,0:T(8,128)S(1)}, u32[]{:S(2)}, u32[]{:S(2)}) collective-permute-start(f32[16,1024]{1,0:T(8,128)S(1)} %get-tuple-element.32.refs_0_.refs_3_.refs_5_), channel_id=1, source_target_pairs={{0,1},{1,0},{2,3},{3,2},{4,5},{5,4},{6,7},{7,6},{8,9},{9,8},{10,11... | collective-permute-start | bytes 196616 | tf_op jit(solution)/shard_map/ppermute | solution.py:415
  39.4 5.0 %collective-permute-start.2 = (f32[16,1024]{1,0:T(8,128)S(1)}, f32[16,1024]{1,0:T(8,128)S(1)}, u32[]{:S(2)}, u32[]{:S(2)}) collective-permute-start(f32[16,1024]{1,0:T(8,128)S(1)} %get-tuple-element.32.refs_0_.refs_3_.refs_5_), channel_id=1, source_target_pairs={{1,2},{3,4},{5,6},{7,8},{9,10},{11,12},{13,14},{2,1},{4,3},{6,5},{... | collective-permute-start | bytes 196616 | tf_op jit(solution)/shard_map/ppermute | solution.py:416
  51.2 15.8 %all-to-all-start.2 = ((f32[32,16,128]{2,1,0:T(8,128)}), f32[32,16,128]{2,1,0:T(8,128)S(1)}, u32[]{:S(2)}, u32[]{:S(2)}) async-start(f32[32,16,128]{2,1,0:T(8,128)} %get-tuple-element.35), calls=%async_computation.2 | async-start | bytes 524288 | tf_op jit(solution)/shard_map/all_to_all | solution.py:132
  56.7 1.3 %collective-permute-start.5 = (f32[16,1024]{1,0:T(8,128)S(1)}, f32[16,1024]{1,0:T(8,128)S(1)}, u32[]{:S(2)}, u32[]{:S(2)}) collective-permute-start(f32[16,1024]{1,0:T(8,128)S(1)} %get-tuple-element.36.refs_0_.refs_3_), channel_id=1, source_target_pairs={{0,1},{1,0},{2,3},{3,2},{4,5},{5,4},{6,7},{7,6},{8,9},{9,8},{10,11... | collective-permute-start | bytes 196616 | tf_op jit(solution)/shard_map/ppermute | solution.py:415
  57.1 5.0 %collective-permute-start.4 = (f32[16,1024]{1,0:T(8,128)S(1)}, f32[16,1024]{1,0:T(8,128)S(1)}, u32[]{:S(2)}, u32[]{:S(2)}) collective-permute-start(f32[16,1024]{1,0:T(8,128)S(1)} %get-tuple-element.36.refs_0_.refs_3_), channel_id=1, source_target_pairs={{1,2},{3,4},{5,6},{7,8},{9,10},{11,12},{13,14},{2,1},{4,3},{6,5},{... | collective-permute-start | bytes 196616 | tf_op jit(solution)/shard_map/ppermute | solution.py:416

commit v5 on v4

--- a/solution.py
+++ b/solution.py
@@ -17,6 +17,7 @@
 SMEM = pl.BlockSpec(memory_space=pltpu.SMEM)
 SUB = 8
 NEAR_LIMIT = 54000
+INNER_LIMIT = 16000
 START_LIMIT = 6000
 
 
@@ -249,7 +250,7 @@
 
     def near_first_body(
         lists, own, pair, other, coarse_points, transfer,
-        near, blocks_out, couple,
+        near, blocks_out, other_out, couple,
         even, odd, factors, targets, fields, total, order, sems,
     ):
         place = whereabouts()
@@ -269,11 +270,35 @@
             order[count] = i
             count = count + hit(place, lists, kind, j, leaf).astype(jnp.int32)
 
-        def out_copy(i, buffer, side):
+        inner_entries = 2 * per_dev * per_dev
+
+        def out_start(i, buffer, side):
             entry = order[i]
-            return pltpu.make_async_copy(
-                buffer, blocks_out.at[entry // per_dev, lax.rem(entry, per_dev)], sems.at[side]
-            )
+            source, leaf = entry // per_dev, lax.rem(entry, per_dev)
+
+            @pl.when(entry < inner_entries)
+            def _():
+                pltpu.make_async_copy(buffer, blocks_out.at[source, leaf], sems.at[side]).start()
+
+            @pl.when(entry >= inner_entries)
+            def _():
+                pltpu.make_async_copy(
+                    buffer, other_out.at[source - 2 * per_dev, leaf], sems.at[side]
+                ).start()
+
+        def out_wait(i, buffer, side):
+            entry = order[i]
+            source, leaf = entry // per_dev, lax.rem(entry, per_dev)
+
+            @pl.when(entry < inner_entries)
+            def _():
+                pltpu.make_async_copy(buffer, blocks_out.at[source, leaf], sems.at[side]).wait()
+
+            @pl.when(entry >= inner_entries)
+            def _():
+                pltpu.make_async_copy(
+                    buffer, other_out.at[source - 2 * per_dev, leaf], sems.at[side]
+                ).wait()
 
         def make(i, buffer):
             entry = order[i]
@@ -294,16 +319,16 @@
             total[leaf] += both[:vec] + both[vec:] + rest
 
         make(0, even)
-        out_copy(0, even, 0).start()
+        out_start(0, even, 0)
 
         def turn(i, buffer, side, last):
             @pl.when(i >= 2)
             def _():
-                out_copy(i - 2, buffer, side).wait()
+                out_wait(i - 2, buffer, side)
 
             make(i, buffer)
             use(i - 1, last)
-            out_copy(i, buffer, side).start()
+            out_start(i, buffer, side)
 
         def two(t, _):
             turn(2 * t + 1, odd, 1, even)
@@ -337,19 +362,24 @@
         for leaf in range(per_dev):
             near[:, leaf_slice(leaf)] = total[leaf]
         last_even = jnp.where(ends_even, count - 1, count - 2)
-        out_copy(last_even, even, 0).wait()
+        out_wait(last_even, even, 0)
 
         @pl.when(count >= 2)
         def _():
-            out_copy(jnp.where(ends_even, count - 2, count - 1), odd, 1).wait()
+            out_wait(jnp.where(ends_even, count - 2, count - 1), odd, 1)
 
     def near_first(pair, other):
         block_shape = (2, leaf_size, leaf_size)
         return call(
             near_first_body,
-            (field_shape, shape(blocks_shape, bf16), shape(couple_shape, bf16)),
+            (
+                field_shape,
+                pltpu.HBM((2 * per_dev, *blocks_shape[1:]), bf16),
+                pltpu.HBM((per_dev, *blocks_shape[1:]), bf16),
+                shape(couple_shape, bf16),
+            ),
             [SMEM] + [VMEM] * 5,
-            (VMEM, HBM, VMEM),
+            (VMEM, HBM, HBM, VMEM),
             scratch=[
                 pltpu.VMEM(block_shape, bf16),
                 pltpu.VMEM(block_shape, bf16),
@@ -364,19 +394,14 @@
             limit=NEAR_LIMIT,
         )(near_lists, stacked, pair, other, coarse_points, transfer)
 
-    def near_again(kinds, windows, blocks, before=()):
-        chosen = [entry for entry in entries if entry[0] in kinds]
-        base = kinds[0] * per_dev
-        shape_here = (len(kinds) * per_dev, *blocks_shape[1:])
-
-        def body(lists, *refs):
-            windows = refs[: len(kinds)]
-            acc = refs[len(kinds) : len(kinds) + len(before)]
-            blocks_in, near, blocks, sems = refs[len(kinds) + len(before) :]
-
+    def near_inner(field, pair, blocks):
+        chosen = [entry for entry in entries if entry[0] < 2]
+        shape_here = (2 * per_dev, *blocks_shape[1:])
+
+        def body(lists, own, pair, blocks_in, near, blocks, sems):
             def in_copy(block, leaf):
                 return pltpu.make_async_copy(
-                    blocks_in.at[base + block, leaf], blocks.at[block, leaf],
+                    blocks_in.at[block, leaf], blocks.at[block, leaf],
                     sems.at[block * per_dev + leaf],
                 )
 
@@ -386,17 +411,17 @@
 
                 @pl.when(found)
                 def _():
-                    in_copy(kind * per_dev + j - base, leaf).start()
-
-            near[...] = acc[0][...] if acc else jnp.zeros_like(near)
+                    in_copy(kind * per_dev + j, leaf).start()
+
+            near[...] = jnp.zeros_like(near)
             for (kind, j, leaf), found in zip(chosen, hits, strict=True):
-                block = kind * per_dev + j - base
+                block = kind * per_dev + j
 
                 @pl.when(found)
                 def _():
                     in_copy(block, leaf).wait()
                     near[:, leaf_slice(leaf)] += dot3(
-                        windows[kind - kinds[0]][:, leaf_slice(j)],
+                        (own, pair)[kind][:, leaf_slice(j)],
                         blocks[block, leaf, 0],
                         blocks[block, leaf, 1],
                     )
@@ -404,12 +429,34 @@
         return call(
             body,
             field_shape,
-            [SMEM] + [VMEM] * (len(kinds) + len(before)) + [HBM],
+            [SMEM, VMEM, VMEM, HBM],
             VMEM,
             scratch=[pltpu.VMEM(shape_here, bf16), pltpu.SemaphoreType.DMA((len(chosen),))],
             flops=10**8,
-            limit=NEAR_LIMIT,
-        )(near_lists, *windows, *before, pltpu.with_memory_space_constraint(blocks, pltpu.HBM))
+            limit=INNER_LIMIT,
+        )(near_lists, field, pair, pltpu.with_memory_space_constraint(blocks, pltpu.HBM))
+
+    def near_outer(other, blocks, before):
+        def body(lists, other, blocks, before, near):
+            near[...] = before[...]
+            place = whereabouts()
+            for j in range(per_dev):
+                for leaf in range(per_dev):
+
+                    @pl.when(hit(place, lists, 2, j, leaf))
+                    def _():
+                        near[:, leaf_slice(leaf)] += dot3(
+                            other[:, leaf_slice(j)], blocks[j, leaf, 0], blocks[j, leaf, 1]
+                        )
+
+        return call(
+            body,
+            field_shape,
+            [SMEM, VMEM, VMEM, VMEM],
+            VMEM,
+            flops=10**8,
+            limit=limit,
+        )(near_lists, other, blocks, before)
 
     def halo(field):
         pair = lax.ppermute(field, "leaf", inner)
@@ -521,12 +568,12 @@
 
     received = exchange(payload)
     pair, other = halo(stacked)
-    near, blocks, couple = near_first(pair, other)
+    near, blocks, other_blocks, couple = near_first(pair, other)
 
     def again(field):
         pair, other = halo(field)
-        near = near_again((0, 1), (field, pair), blocks)
-        return near_again((2,), (other,), blocks, (near,))
+        near = near_inner(field, pair, blocks)
+        return near_outer(other, other_blocks, near)
 
     term_one, payload, far = post(1, received, near, stacked)
     received = exchange(payload)

time: 81.5 us -> 79.2 us (0.972)
  blocking collectives: 12.5 us -> 11.4 us
  starting transfers between devices: 31.7 us -> 30.8 us
    all_to_all x1, blocking collectives: 12.5 us -> 11.4 us  [on_device(): exchange = lambda x: lax.all_to_all(x, ('grp', 'leaf'), 0, 0, tiled=True)]
    all_to_all x3, starting transfers between devices: 25.9 us -> 24.8 us  [on_device(): exchange = lambda x: lax.all_to_all(x, ('grp', 'leaf'), 0, 0, tiled=True)]
  transfers between devices with their start and end apart: 9 -> 9, of which waited for: 6 -> 6; matrix products, arithmetic and copies ran while one was open for 0% -> 0% of each run, Pallas kernels for 20% -> 21%
where the time goes in v5:
time: 79.2 us; the launch traced here: 78.7 us
  starting transfers between devices  30.8 us (39%)
  Pallas kernels  24.8 us (31%)
  blocking collectives  11.4 us (14%)
  waiting for transfers between devices  10.8 us (14%)
    all_to_all x3, starting transfers between devices, on_device(): exchange = lambda x: lax.all_to_all(x, ('grp', 'leaf'), 0, 0, tiled=True)  24.8 us
    all_to_all x1, blocking collectives, on_device(): exchange = lambda x: lax.all_to_all(x, ('grp', 'leaf'), 0, 0, tiled=True)  11.4 us
    all_to_all x3, waiting for transfers between devices, on_device(): exchange = lambda x: lax.all_to_all(x, ('grp', 'leaf'), 0, 0, tiled=True)  9.26 us
    pallas_call x2, Pallas kernels, near_inner(): call(body, field_shape, [SMEM, VMEM, VMEM, HBM], VMEM, scratch=[pltpu.VME...  8.27 us
    pallas_call x1, Pallas kernels, near_first(): call(near_first_body, (field_shape, pltpu.HBM((2 * per_dev, *blocks_shape...  7.29 us
    pallas_call x3, Pallas kernels, post(): call(lambda *refs: post_body(step, *refs), tuple(outs), in_specs, tuple(s...  5.54 us
    ppermute x3, starting transfers between devices, halo(): pair = lax.ppermute(field, 'leaf', inner)  3.82 us
    pallas_call x1, Pallas kernels, on_device(): call(start_body, (shape((devices, vec + SUB, cols), f32), shape((vec + SU...  2.48 us
  transfers between devices with their start and end apart: 9, of which 6 were waited for; matrix products, arithmetic and copies ran while one was open for 0% of the time, Pallas kernels for 21%

profile of v5, /device:TPU:0, one launch (start us, length us, event | category | flops | bytes accessed | tf_op | source)
XLA Modules:
  0.0 78.7 jit_solution(16845015907338564100)
XLA Ops:
  0.0 2.5 %shard_map.82 = (f32[32,24,128]{2,1,0:T(8,128)}, f32[24,1024]{1,0:T(8,128)S(1)}, bf16[2,2,64,512]{3,2,1,0:T(8,128)(2,1)S(1)}, bf16[2,128,128]{2,1,0:T(8,128)(2,1...) custom-call(f32[16,1024]{1,0:T(8,128)} %field_in.1, f32[3,1024]{1,0:T(4,128)} %points_in.1, ...), custom_call_target="tpu_custom_call" | custom-call | flops 10000000 | bytes 1048576 | tf_op jit(solution)/shard_map/pallas_call | solution.py:212
  2.5 7.3 %all-to-all-start = ((f32[32,24,128]{2,1,0:T(8,128)}), f32[32,24,128]{2,1,0:T(8,128)S(1)}, u32[]{:S(2)}, u32[]{:S(2)}) async-start(f32[32,24,128]{2,1,0:T(8,128)} %get-tuple-element.29), calls=%async_computation | async-start | bytes 786432 | tf_op jit(solution)/shard_map/all_to_all | solution.py:133
  9.8 0.7 collective-permute-start.1
  10.5 3.2 %collective-permute-start = (f32[24,1024]{1,0:T(8,128)S(1)}, f32[24,1024]{1,0:T(8,128)S(1)}, u32[]{:S(2)}, u32[]{:S(2)}) collective-permute-start(f32[24,1024]{1,0:T(8,128)S(1)} %get-tuple-element.25.own.refs_5_), channel_id=1, source_target_pairs={{0,1},{1,0},{2,3},{3,2},{4,5},{5,4},{6,7},{7,6},{8,9},{9,8},{10,11... | collective-permute-start | bytes 294920 | tf_op jit(solution)/shard_map/ppermute | solution.py:462
  13.7 0.0 collective-permute-done.1.other
  13.7 0.9 %collective-permute-done.pair = f32[24,1024]{1,0:T(8,128)S(1)} collective-permute-done((f32[24,1024]{1,0:T(8,128)S(1)}, f32[24,1024]{1,0:T(8,128)S(1)}, u32[]{:S(2)}, u32[]{:S(2)}) %collective-permute-start) | collective-permute-done | bytes 98336 | tf_op jit(solution)/shard_map/ppermute | solution.py:462
  14.6 7.3 %shard_map.83 = (f32[16,1024]{1,0:T(8,128)S(1)}, bf16[4,2,2,512,512]{4,3,2,1,0:T(8,128)(2,1)}, bf16[2,2,2,512,512]{4,3,2,1,0:T(8,128)(2,1)}, bf16[2,128,128]{2,1,0:T(8,128)(2,1)S(1)}) custom-call(s32[2,6]{1,0:T(2,128)S(1)} %get-tuple-element.24.lists, f32[24,1024]{1,0:T(8,128)S(1)} %get-tuple-element.25.own.refs_5_, ...), custom_call_target="tpu_custom_call" | custom-call | flops 1000000000 | bytes 1048576 | tf_op jit(solution)/shard_map/pallas_call | solution.py:373
  21.9 1.0 %all-to-all-done.refs_2_ = f32[32,24,128]{2,1,0:T(8,128)S(1)} async-done(((f32[32,24,128]{2,1,0:T(8,128)}), f32[32,24,128]{2,1,0:T(8,128)S(1)}, u32[]{:S(2)}, u32[]{:S(2)}) %all-to-all-start) | async-done | bytes 393248 | tf_op jit(solution)/shard_map/all_to_all | solution.py:133
  22.9 3.1 %shard_map.84 = (f32[16,1024]{1,0:T(8,128)S(1)}, f32[32,16,128]{2,1,0:T(8,128)}, bf16[2,2176,128]{2,1,0:T(8,128)(2,1)S(1)}) custom-call(s32[2,16]{1,0:T(2,128)S(1)} %get-tuple-element.23.refs_0_, bf16[2,128,128]{2,1,0:T(8,128)(2,1)S(1)} %get-tuple-element.28.refs_1_, f32[32,24,128]{2,1,0:T(8,128)S(1)} %all-to-all-done.refs_2_, ...), custom_call_target="tpu_custom_call" | custom-call | flops 10000000 | bytes 1048576 | tf_op jit(solution)/shard_map/pallas_call | solution.py:559
  26.1 13.1 %all-to-all-start.1 = ((f32[32,16,128]{2,1,0:T(8,128)}), f32[32,16,128]{2,1,0:T(8,128)S(1)}, u32[]{:S(2)}, u32[]{:S(2)}) async-start(f32[32,16,128]{2,1,0:T(8,128)} %get-tuple-element.32), calls=%async_computation.1 | async-start | bytes 524288 | tf_op jit(solution)/shard_map/all_to_all | solution.py:133
  39.1 0.3 collective-permute-start.3
  39.5 0.7 collective-permute-start.2
  40.1 0.3 collective-permute-done.3.pair
  40.5 0.0 copy-start
  40.5 4.3 %shard_map.85.before = f32[16,1024]{1,0:T(8,128)S(1)} custom-call(s32[2,6]{1,0:T(2,128)S(1)} %get-tuple-element.24.lists, f32[16,1024]{1,0:T(8,128)S(1)} %get-tuple-element.33.own.refs_3_.refs_5_, f32[16,1024]{1,0:T(8,128)S(1)} %collective-permute-done.3.pair, bf16[4,2,2,512,512]{4,3,2,1,0:T(8,128)(2,1)} %get-tuple-element.35.blocks_in), custom_call_target="tpu_custom_call" | custom-call | flops 100000000 | bytes 1048576 | tf_op jit(solution)/shard_map/pallas_call | solution.py:429
  44.7 0.0 collective-permute-done.2.other
  44.7 0.1 copy-done
  44.8 0.6 shard_map.86.refs_2_
  45.4 4.0 %all-to-all-done.1.refs_0_ = f32[32,16,128]{2,1,0:T(8,128)S(1)} async-done(((f32[32,16,128]{2,1,0:T(8,128)}), f32[32,16,128]{2,1,0:T(8,128)S(1)}, u32[]{:S(2)}, u32[]{:S(2)}) %all-to-all-start.1) | async-done | bytes 262176 | tf_op jit(solution)/shard_map/all_to_all | solution.py:133
  49.4 1.8 %shard_map.87 = (f32[16,1024]{1,0:T(8,128)S(1)}, f32[32,16,128]{2,1,0:T(8,128)}) custom-call(f32[32,16,128]{2,1,0:T(8,128)S(1)} %all-to-all-done.1.refs_0_, bf16[2,2,64,512]{3,2,1,0:T(8,128)(2,1)S(1)} %get-tuple-element.30.refs_3_.refs_1_, f32[16,1024]{1,0:T(8,128)S(1)} %shard_map.86.refs_2_, f32[16,1024]{1,0:T(8,128)S(1)} %get-tuple-element.33.own.refs_3_.refs_5_, ...), custom_call_target="tpu_custom_call" | custom-call | flops 10000000 | bytes 1048576 | tf_op jit(solution)/shard_map/pallas_call | solution.py:559
  51.2 4.4 %all-to-all-start.2 = ((f32[32,16,128]{2,1,0:T(8,128)}), f32[32,16,128]{2,1,0:T(8,128)S(1)}, u32[]{:S(2)}, u32[]{:S(2)}) async-start(f32[32,16,128]{2,1,0:T(8,128)} %get-tuple-element.37), calls=%async_computation.2 | async-start | bytes 524288 | tf_op jit(solution)/shard_map/all_to_all | solution.py:133
  55.7 0.0 copy-start.1
  55.7 0.3 collective-permute-start.5
  56.0 0.8 collective-permute-start.4
  56.8 0.2 collective-permute-done.5.pair
  57.0 4.0 %shard_map.88.before = f32[16,1024]{1,0:T(8,128)S(1)} custom-call(s32[2,6]{1,0:T(2,128)S(1)} %get-tuple-element.24.lists, f32[16,1024]{1,0:T(8,128)S(1)} %get-tuple-element.38.own.refs_3_, f32[16,1024]{1,0:T(8,128)S(1)} %collective-permute-done.5.pair, bf16[4,2,2,512,512]{4,3,2,1,0:T(8,128)(2,1)} %get-tuple-element.35.blocks_in), custom_call_target="tpu_custom_call" | custom-call | flops 100000000 | bytes 1048576 | tf_op jit(solution)/shard_map/pallas_call | solution.py:429
  61.0 0.0 collective-permute-done.4.other
  61.0 0.0 copy-done.1
  61.0 0.6 shard_map.89.refs_2_
  61.7 4.3 %all-to-all-done.2.refs_0_ = f32[32,16,128]{2,1,0:T(8,128)S(1)} async-done(((f32[32,16,128]{2,1,0:T(8,128)}), f32[32,16,128]{2,1,0:T(8,128)S(1)}, u32[]{:S(2)}, u32[]{:S(2)}) %all-to-all-start.2) | async-done | bytes 262176 | tf_op jit(solution)/shard_map/all_to_all | solution.py:133
  66.0 0.6 shard_map.90
  66.5 11.4 %all_to_all.20 = f32[32,1,128]{2,1,0:T(1,128)S(1)} all-to-all(f32[32,1,128]{2,1,0:T(1,128)S(1)} %get-tuple-element.40), channel_id=1, replica_groups=mesh['grp'=2,'leaf'=16] {'grp','leaf'}, dimensions={0} | all-to-all | bytes 32768 | tf_op jit(solution)/shard_map/all_to_all | solution.py:133
  77.9 0.1 reduce_sum.9
  78.0 0.7 broadcast_divide_fusion
  (1 shorter events, 0.0 us)
Async XLA Ops:
  2.5 20.4 %all-to-all-start = ((f32[32,24,128]{2,1,0:T(8,128)}), f32[32,24,128]{2,1,0:T(8,128)S(1)}, u32[]{:S(2)}, u32[]{:S(2)}) async-start(f32[32,24,128]{2,1,0:T(8,128)} %get-tuple-element.29), calls=%async_computation | async-start | bytes 786432 | tf_op jit(solution)/shard_map/all_to_all | solution.py:133
  9.8 3.9 %collective-permute-start.1 = (f32[24,1024]{1,0:T(8,128)S(1)}, f32[24,1024]{1,0:T(8,128)S(1)}, u32[]{:S(2)}, u32[]{:S(2)}) collective-permute-start(f32[24,1024]{1,0:T(8,128)S(1)} %get-tuple-element.25.own.refs_5_), channel_id=1, source_target_pairs={{1,2},{3,4},{5,6},{7,8},{9,10},{11,12},{13,14},{2,1},{4,3},{6,5},{... | collective-permute-start | bytes 294920 | tf_op jit(solution)/shard_map/ppermute | solution.py:463
  10.5 4.1 %collective-permute-start = (f32[24,1024]{1,0:T(8,128)S(1)}, f32[24,1024]{1,0:T(8,128)S(1)}, u32[]{:S(2)}, u32[]{:S(2)}) collective-permute-start(f32[24,1024]{1,0:T(8,128)S(1)} %get-tuple-element.25.own.refs_5_), channel_id=1, source_target_pairs={{0,1},{1,0},{2,3},{3,2},{4,5},{5,4},{6,7},{7,6},{8,9},{9,8},{10,11... | collective-permute-start | bytes 294920 | tf_op jit(solution)/shard_map/ppermute | solution.py:462
  26.1 23.4 %all-to-all-start.1 = ((f32[32,16,128]{2,1,0:T(8,128)}), f32[32,16,128]{2,1,0:T(8,128)S(1)}, u32[]{:S(2)}, u32[]{:S(2)}) async-start(f32[32,16,128]{2,1,0:T(8,128)} %get-tuple-element.32), calls=%async_computation.1 | async-start | bytes 524288 | tf_op jit(solution)/shard_map/all_to_all | solution.py:133
  39.1 1.3 %collective-permute-start.3 = (f32[16,1024]{1,0:T(8,128)S(1)}, f32[16,1024]{1,0:T(8,128)S(1)}, u32[]{:S(2)}, u32[]{:S(2)}) collective-permute-start(f32[16,1024]{1,0:T(8,128)S(1)} %get-tuple-element.33.own.refs_3_.refs_5_), channel_id=1, source_target_pairs={{0,1},{1,0},{2,3},{3,2},{4,5},{5,4},{6,7},{7,6},{8,9},{9,8},{10,11... | collective-permute-start | bytes 196616 | tf_op jit(solution)/shard_map/ppermute | solution.py:462
  39.5 5.3 %collective-permute-start.2 = (f32[16,1024]{1,0:T(8,128)S(1)}, f32[16,1024]{1,0:T(8,128)S(1)}, u32[]{:S(2)}, u32[]{:S(2)}) collective-permute-start(f32[16,1024]{1,0:T(8,128)S(1)} %get-tuple-element.33.own.refs_3_.refs_5_), channel_id=1, source_target_pairs={{1,2},{3,4},{5,6},{7,8},{9,10},{11,12},{13,14},{2,1},{4,3},{6,5},{... | collective-permute-start | bytes 196616 | tf_op jit(solution)/shard_map/ppermute | solution.py:463
  40.5 4.4 %copy-start = (bf16[2,2,2,512,512]{4,3,2,1,0:T(8,128)(2,1)S(1)}, bf16[2,2,2,512,512]{4,3,2,1,0:T(8,128)(2,1)}, u32[]{:S(2)}) copy-start(bf16[2,2,2,512,512]{4,3,2,1,0:T(8,128)(2,1)} %get-tuple-element.34.blocks) | copy-start | bytes 12582916
  51.2 14.7 %all-to-all-start.2 = ((f32[32,16,128]{2,1,0:T(8,128)}), f32[32,16,128]{2,1,0:T(8,128)S(1)}, u32[]{:S(2)}, u32[]{:S(2)}) async-start(f32[32,16,128]{2,1,0:T(8,128)} %get-tuple-element.37), calls=%async_computation.2 | async-start | bytes 524288 | tf_op jit(solution)/shard_map/all_to_all | solution.py:133
  55.7 5.4 %copy-start.1 = (bf16[2,2,2,512,512]{4,3,2,1,0:T(8,128)(2,1)S(1)}, bf16[2,2,2,512,512]{4,3,2,1,0:T(8,128)(2,1)}, u32[]{:S(2)}) copy-start(bf16[2,2,2,512,512]{4,3,2,1,0:T(8,128)(2,1)} %get-tuple-element.34.blocks) | copy-start | bytes 12582916
  55.7 1.3 %collective-permute-start.5 = (f32[16,1024]{1,0:T(8,128)S(1)}, f32[16,1024]{1,0:T(8,128)S(1)}, u32[]{:S(2)}, u32[]{:S(2)}) collective-permute-start(f32[16,1024]{1,0:T(8,128)S(1)} %get-tuple-element.38.own.refs_3_), channel_id=1, source_target_pairs={{0,1},{1,0},{2,3},{3,2},{4,5},{5,4},{6,7},{7,6},{8,9},{9,8},{10,11... | collective-permute-start | bytes 196616 | tf_op jit(solution)/shard_map/ppermute | solution.py:462
  56.0 5.0 %collective-permute-start.4 = (f32[16,1024]{1,0:T(8,128)S(1)}, f32[16,1024]{1,0:T(8,128)S(1)}, u32[]{:S(2)}, u32[]{:S(2)}) collective-permute-start(f32[16,1024]{1,0:T(8,128)S(1)} %get-tuple-element.38.own.refs_3_), channel_id=1, source_target_pairs={{1,2},{3,4},{5,6},{7,8},{9,10},{11,12},{13,14},{2,1},{4,3},{6,5},{... | collective-permute-start | bytes 196616 | tf_op jit(solution)/shard_map/ppermute | solution.py:463

commit v6 on v5

--- a/solution.py
+++ b/solution.py
@@ -69,7 +69,7 @@
 
 
 def source_factors(points):
-    return distance_factors(points)[0].T.astype(bf16)
+    return distance_factors(points)[0].astype(bf16).T
 
 
 def target_factors(points):
@@ -249,8 +249,8 @@
     couple_shape = (2, couple_rows, cols)
 
     def near_first_body(
-        lists, own, pair, other, coarse_points, transfer,
-        near, blocks_out, other_out, couple,
+        lists, inter_lists, own, pair, other, coarse_points, transfer,
+        near, blocks_out, other_out, couple, marks,
         even, odd, factors, targets, fields, total, order, sems,
     ):
         place = whereabouts()
@@ -359,6 +359,14 @@
             kernel = matern(source_factors(coordinates(far, coarse_origin)), target)
             at = slice((t - 1) * coarse, t * coarse)
             couple[0, at], couple[1, at] = split(dot3_nt(kernel, transfer[0], transfer[1]))
+        lane_leaf = lax.broadcasted_iota(jnp.int32, marks.shape, 1) // rank
+        row_leaf = lax.broadcasted_iota(jnp.int32, marks.shape, 0)
+        mark = jnp.zeros(marks.shape, f32)
+        for j in range(per_dev):
+            for s in range(listed):
+                chosen = jnp.logical_and(row_leaf == inter_lists[j, s], lane_leaf == j)
+                mark = jnp.where(chosen, 1.0, mark)
+        marks[...] = mark
         for leaf in range(per_dev):
             near[:, leaf_slice(leaf)] = total[leaf]
         last_even = jnp.where(ends_even, count - 1, count - 2)
@@ -377,9 +385,10 @@
                 pltpu.HBM((2 * per_dev, *blocks_shape[1:]), bf16),
                 pltpu.HBM((per_dev, *blocks_shape[1:]), bf16),
                 shape(couple_shape, bf16),
+                shape((leaves * per_dev, cols), f32),
             ),
-            [SMEM] + [VMEM] * 5,
-            (VMEM, HBM, HBM, VMEM),
+            [SMEM, SMEM] + [VMEM] * 5,
+            (VMEM, HBM, HBM, VMEM, VMEM),
             scratch=[
                 pltpu.VMEM(block_shape, bf16),
                 pltpu.VMEM(block_shape, bf16),
@@ -392,7 +401,7 @@
             ],
             flops=10**9,
             limit=NEAR_LIMIT,
-        )(near_lists, stacked, pair, other, coarse_points, transfer)
+        )(near_lists, inter_lists, stacked, pair, other, coarse_points, transfer)
 
     def near_inner(field, pair, blocks):
         chosen = [entry for entry in entries if entry[0] < 2]
@@ -463,23 +472,16 @@
         other = lax.ppermute(field, "leaf", outer)
         return pair, other
 
-    def build_far(place, lists, received, origin, far):
+    def build_far(place, marks, received, origin, far):
         group, leaf = place[1], place[0]
         target = target_factors(coordinates(received[group * leaves + leaf, vec : vec + 3], origin))
-        lane_leaf = lax.broadcasted_iota(jnp.int32, (leaves * per_dev, cols), 1) // rank
-        row_leaf = lax.broadcasted_iota(jnp.int32, (leaves * per_dev, cols), 0)
-        mark = jnp.zeros((leaves * per_dev, cols), f32)
-        for j in range(per_dev):
-            for s in range(listed):
-                here = jnp.logical_and(row_leaf == lists[j, s], lane_leaf == j)
-                mark = jnp.where(here, 1.0, mark)
         for i in range(leaves):
             spots = received[group * leaves + i, vec : vec + 3]
             kernel = matern(source_factors(coordinates(spots, origin)), target)
             for h in range(per_dev):
                 m = i * per_dev + h
                 at = slice(m * rank, (m + 1) * rank)
-                hi, lo = split(kernel[h * rank : (h + 1) * rank] * mark[m : m + 1])
+                hi, lo = split(kernel[h * rank : (h + 1) * rank] * marks[m : m + 1])
                 far[0, at] = hi
                 far[1, at] = lo
 
@@ -487,7 +489,7 @@
 
     def post_body(step, *refs):
         refs = list(refs)
-        lists, couple = (refs.pop(0), refs.pop(0)) if step == 1 else (None, None)
+        marks, couple = (refs.pop(0), refs.pop(0)) if step == 1 else (None, None)
         received, interp, near, field = refs[:4]
         refs = refs[4:]
         far, before = (None, None) if step == 1 else (refs.pop(0), refs.pop(0))
@@ -498,7 +500,7 @@
         if step == 1:
             far = refs.pop(0)
             origin = received[group * leaves + place[0], vec : vec + 3][:, :1]
-            build_far(place, lists, received, origin, far)
+            build_far(place, marks, received, origin, far)
             far[:, far_rows:] = couple[...]
         parts = [received[group * leaves + i, :vec] for i in range(leaves)]
         for t in range(1, groups):
@@ -544,7 +546,7 @@
         if step == 1:
             outs.append(shape(far_shape, bf16))
             specs.append(VMEM)
-            args = [inter_lists, couple, *args]
+            args = [marks, couple, *args]
         scratch = []
         if step < 3:
             args.append(transfer)
@@ -553,13 +555,10 @@
                 pltpu.VMEM((vec, cols), f32),
                 pltpu.SemaphoreType.DMA((devices,)),
             ]
-        in_specs = [VMEM] * len(args)
-        if step == 1:
-            in_specs[0] = SMEM
         return call(
             lambda *refs: post_body(step, *refs),
             tuple(outs),
-            in_specs,
+            [VMEM] * len(args),
             tuple(specs),
             scratch=scratch,
             flops=10**7,
@@ -568,7 +567,7 @@
 
     received = exchange(payload)
     pair, other = halo(stacked)
-    near, blocks, other_blocks, couple = near_first(pair, other)
+    near, blocks, other_blocks, couple, marks = near_first(pair, other)
 
     def again(field):
         pair, other = halo(field)

time: 79.2 us -> 78.6 us (level)
  no operation moved by 1% of the time
where the time goes in v6:
time: 78.6 us; the launch traced here: 78.1 us
  starting transfers between devices  30.8 us (39%)
  Pallas kernels  24.2 us (31%)
  blocking collectives  11.4 us (15%)
  waiting for transfers between devices  10.8 us (14%)
    all_to_all x3, starting transfers between devices, on_device(): exchange = lambda x: lax.all_to_all(x, ('grp', 'leaf'), 0, 0, tiled=True)  24.9 us
    all_to_all x1, blocking collectives, on_device(): exchange = lambda x: lax.all_to_all(x, ('grp', 'leaf'), 0, 0, tiled=True)  11.4 us
    all_to_all x3, waiting for transfers between devices, on_device(): exchange = lambda x: lax.all_to_all(x, ('grp', 'leaf'), 0, 0, tiled=True)  9.26 us
    pallas_call x2, Pallas kernels, near_inner(): call(body, field_shape, [SMEM, VMEM, VMEM, HBM], VMEM, scratch=[pltpu.VME...  8.27 us
    pallas_call x1, Pallas kernels, near_first(): call(near_first_body, (field_shape, pltpu.HBM((2 * per_dev, *blocks_shape...  7.29 us
    pallas_call x3, Pallas kernels, post(): call(lambda *refs: post_body(step, *refs), tuple(outs), [VMEM] * len(args...  4.91 us
    ppermute x3, starting transfers between devices, halo(): pair = lax.ppermute(field, 'leaf', inner)  3.82 us
    pallas_call x1, Pallas kernels, on_device(): call(start_body, (shape((devices, vec + SUB, cols), f32), shape((vec + SU...  2.48 us
  transfers between devices with their start and end apart: 9, of which 6 were waited for; matrix products, arithmetic and copies ran while one was open for 0% of the time, Pallas kernels for 21%

profile of v6, /device:TPU:0, one launch (start us, length us, event | category | flops | bytes accessed | tf_op | source)
XLA Modules:
  0.0 78.1 jit_solution(14106764448617818497)
XLA Ops:
  0.0 2.5 %shard_map.82 = (f32[32,24,128]{2,1,0:T(8,128)}, f32[24,1024]{1,0:T(8,128)S(1)}, bf16[2,2,64,512]{3,2,1,0:T(8,128)(2,1)S(1)}, bf16[2,128,128]{2,1,0:T(8,128)(2,1...) custom-call(f32[16,1024]{1,0:T(8,128)} %field_in.1, f32[3,1024]{1,0:T(4,128)} %points_in.1, ...), custom_call_target="tpu_custom_call" | custom-call | flops 10000000 | bytes 1048576 | tf_op jit(solution)/shard_map/pallas_call | solution.py:212
  2.5 7.3 %all-to-all-start = ((f32[32,24,128]{2,1,0:T(8,128)}), f32[32,24,128]{2,1,0:T(8,128)S(1)}, u32[]{:S(2)}, u32[]{:S(2)}) async-start(f32[32,24,128]{2,1,0:T(8,128)} %get-tuple-element.31), calls=%async_computation | async-start | bytes 786432 | tf_op jit(solution)/shard_map/all_to_all | solution.py:133
  9.8 0.7 collective-permute-start.1
  10.5 3.2 %collective-permute-start = (f32[24,1024]{1,0:T(8,128)S(1)}, f32[24,1024]{1,0:T(8,128)S(1)}, u32[]{:S(2)}, u32[]{:S(2)}) collective-permute-start(f32[24,1024]{1,0:T(8,128)S(1)} %get-tuple-element.26.own.refs_5_), channel_id=1, source_target_pairs={{0,1},{1,0},{2,3},{3,2},{4,5},{5,4},{6,7},{7,6},{8,9},{9,8},{10,11... | collective-permute-start | bytes 294920 | tf_op jit(solution)/shard_map/ppermute | solution.py:471
  13.7 0.0 collective-permute-done.1.other
  13.7 0.9 %collective-permute-done.pair = f32[24,1024]{1,0:T(8,128)S(1)} collective-permute-done((f32[24,1024]{1,0:T(8,128)S(1)}, f32[24,1024]{1,0:T(8,128)S(1)}, u32[]{:S(2)}, u32[]{:S(2)}) %collective-permute-start) | collective-permute-done | bytes 98336 | tf_op jit(solution)/shard_map/ppermute | solution.py:471
  14.6 7.3 %shard_map.83 = (f32[16,1024]{1,0:T(8,128)S(1)}, bf16[4,2,2,512,512]{4,3,2,1,0:T(8,128)(2,1)}, bf16[2,2,2,512,512]{4,3,2,1,0:T(8,128)(2,1)}, bf16[2,128,128]{2,1,0:T(8,128)(2,1)S(1)}, f32[32,128]{1,0:T(8,128)S(1)}) custom-call(s32[2,6]{1,0:T(2,128)S(1)} %get-tuple-element.24.lists, s32[2,16]{1,0:T(2,128)S(1)} %get-tuple-element.25.inter_lists, ...), custom_call_target="tpu_custom_call" | custom-call | flops 1000000000 | bytes 1048576 | tf_op jit(solution)/shard_map/pallas_call | solution.py:381
  21.9 1.0 %all-to-all-done.refs_2_ = f32[32,24,128]{2,1,0:T(8,128)S(1)} async-done(((f32[32,24,128]{2,1,0:T(8,128)}), f32[32,24,128]{2,1,0:T(8,128)S(1)}, u32[]{:S(2)}, u32[]{:S(2)}) %all-to-all-start) | async-done | bytes 393248 | tf_op jit(solution)/shard_map/all_to_all | solution.py:133
  22.9 2.5 %shard_map.84 = (f32[16,1024]{1,0:T(8,128)S(1)}, f32[32,16,128]{2,1,0:T(8,128)}, bf16[2,2176,128]{2,1,0:T(8,128)(2,1)S(1)}) custom-call(f32[32,128]{1,0:T(8,128)S(1)} %get-tuple-element.29.refs_0_, bf16[2,128,128]{2,1,0:T(8,128)(2,1)S(1)} %get-tuple-element.30.refs_1_, f32[32,24,128]{2,1,0:T(8,128)S(1)} %all-to-all-done.refs_2_, ...), custom_call_target="tpu_custom_call" | custom-call | flops 10000000 | bytes 1048576 | tf_op jit(solution)/shard_map/pallas_call | solution.py:558
  25.4 13.1 %all-to-all-start.1 = ((f32[32,16,128]{2,1,0:T(8,128)}), f32[32,16,128]{2,1,0:T(8,128)S(1)}, u32[]{:S(2)}, u32[]{:S(2)}) async-start(f32[32,16,128]{2,1,0:T(8,128)} %get-tuple-element.34), calls=%async_computation.1 | async-start | bytes 524288 | tf_op jit(solution)/shard_map/all_to_all | solution.py:133
  38.5 0.3 collective-permute-start.3
  38.8 0.7 collective-permute-start.2
  39.5 0.3 collective-permute-done.3.pair
  39.9 0.0 copy-start
  39.9 4.3 %shard_map.85.before = f32[16,1024]{1,0:T(8,128)S(1)} custom-call(s32[2,6]{1,0:T(2,128)S(1)} %get-tuple-element.24.lists, f32[16,1024]{1,0:T(8,128)S(1)} %get-tuple-element.35.own.refs_3_.refs_5_, f32[16,1024]{1,0:T(8,128)S(1)} %collective-permute-done.3.pair, bf16[4,2,2,512,512]{4,3,2,1,0:T(8,128)(2,1)} %get-tuple-element.37.blocks_in), custom_call_target="tpu_custom_call" | custom-call | flops 100000000 | bytes 1048576 | tf_op jit(solution)/shard_map/pallas_call | solution.py:438
  44.1 0.0 collective-permute-done.2.other
  44.1 0.1 copy-done
  44.2 0.6 shard_map.86.refs_2_
  44.8 4.0 %all-to-all-done.1.refs_0_ = f32[32,16,128]{2,1,0:T(8,128)S(1)} async-done(((f32[32,16,128]{2,1,0:T(8,128)}), f32[32,16,128]{2,1,0:T(8,128)S(1)}, u32[]{:S(2)}, u32[]{:S(2)}) %all-to-all-start.1) | async-done | bytes 262176 | tf_op jit(solution)/shard_map/all_to_all | solution.py:133
  48.8 1.8 %shard_map.87 = (f32[16,1024]{1,0:T(8,128)S(1)}, f32[32,16,128]{2,1,0:T(8,128)}) custom-call(f32[32,16,128]{2,1,0:T(8,128)S(1)} %all-to-all-done.1.refs_0_, bf16[2,2,64,512]{3,2,1,0:T(8,128)(2,1)S(1)} %get-tuple-element.32.refs_3_.refs_1_, f32[16,1024]{1,0:T(8,128)S(1)} %shard_map.86.refs_2_, f32[16,1024]{1,0:T(8,128)S(1)} %get-tuple-element.35.own.refs_3_.refs_5_, ...), custom_call_target="tpu_custom_call" | custom-call | flops 10000000 | bytes 1048576 | tf_op jit(solution)/shard_map/pallas_call | solution.py:558
  50.6 4.4 %all-to-all-start.2 = ((f32[32,16,128]{2,1,0:T(8,128)}), f32[32,16,128]{2,1,0:T(8,128)S(1)}, u32[]{:S(2)}, u32[]{:S(2)}) async-start(f32[32,16,128]{2,1,0:T(8,128)} %get-tuple-element.39), calls=%async_computation.2 | async-start | bytes 524288 | tf_op jit(solution)/shard_map/all_to_all | solution.py:133
  55.1 0.0 copy-start.1
  55.1 0.3 collective-permute-start.5
  55.4 0.8 %collective-permute-start.4 = (f32[16,1024]{1,0:T(8,128)S(1)}, f32[16,1024]{1,0:T(8,128)S(1)}, u32[]{:S(2)}, u32[]{:S(2)}) collective-permute-start(f32[16,1024]{1,0:T(8,128)S(1)} %get-tuple-element.40.own.refs_3_), channel_id=1, source_target_pairs={{1,2},{3,4},{5,6},{7,8},{9,10},{11,12},{13,14},{2,1},{4,3},{6,5},{... | collective-permute-start | bytes 196616 | tf_op jit(solution)/shard_map/ppermute | solution.py:472
  56.2 0.2 collective-permute-done.5.pair
  56.4 4.0 %shard_map.88.before = f32[16,1024]{1,0:T(8,128)S(1)} custom-call(s32[2,6]{1,0:T(2,128)S(1)} %get-tuple-element.24.lists, f32[16,1024]{1,0:T(8,128)S(1)} %get-tuple-element.40.own.refs_3_, f32[16,1024]{1,0:T(8,128)S(1)} %collective-permute-done.5.pair, bf16[4,2,2,512,512]{4,3,2,1,0:T(8,128)(2,1)} %get-tuple-element.37.blocks_in), custom_call_target="tpu_custom_call" | custom-call | flops 100000000 | bytes 1048576 | tf_op jit(solution)/shard_map/pallas_call | solution.py:438
  60.4 0.0 collective-permute-done.4.other
  60.4 0.0 copy-done.1
  60.4 0.6 shard_map.89.refs_2_
  61.1 4.3 %all-to-all-done.2.refs_0_ = f32[32,16,128]{2,1,0:T(8,128)S(1)} async-done(((f32[32,16,128]{2,1,0:T(8,128)}), f32[32,16,128]{2,1,0:T(8,128)S(1)}, u32[]{:S(2)}, u32[]{:S(2)}) %all-to-all-start.2) | async-done | bytes 262176 | tf_op jit(solution)/shard_map/all_to_all | solution.py:133
  65.3 0.6 shard_map.90
  65.9 11.4 %all_to_all.20 = f32[32,1,128]{2,1,0:T(1,128)S(1)} all-to-all(f32[32,1,128]{2,1,0:T(1,128)S(1)} %get-tuple-element.42), channel_id=1, replica_groups=mesh['grp'=2,'leaf'=16] {'grp','leaf'}, dimensions={0} | all-to-all | bytes 32768 | tf_op jit(solution)/shard_map/all_to_all | solution.py:133
  77.3 0.1 reduce_sum.9
  77.4 0.7 broadcast_divide_fusion
  (1 shorter events, 0.0 us)
Async XLA Ops:
  2.5 20.4 %all-to-all-start = ((f32[32,24,128]{2,1,0:T(8,128)}), f32[32,24,128]{2,1,0:T(8,128)S(1)}, u32[]{:S(2)}, u32[]{:S(2)}) async-start(f32[32,24,128]{2,1,0:T(8,128)} %get-tuple-element.31), calls=%async_computation | async-start | bytes 786432 | tf_op jit(solution)/shard_map/all_to_all | solution.py:133
  9.8 3.9 %collective-permute-start.1 = (f32[24,1024]{1,0:T(8,128)S(1)}, f32[24,1024]{1,0:T(8,128)S(1)}, u32[]{:S(2)}, u32[]{:S(2)}) collective-permute-start(f32[24,1024]{1,0:T(8,128)S(1)} %get-tuple-element.26.own.refs_5_), channel_id=1, source_target_pairs={{1,2},{3,4},{5,6},{7,8},{9,10},{11,12},{13,14},{2,1},{4,3},{6,5},{... | collective-permute-start | bytes 294920 | tf_op jit(solution)/shard_map/ppermute | solution.py:472
  10.5 4.1 %collective-permute-start = (f32[24,1024]{1,0:T(8,128)S(1)}, f32[24,1024]{1,0:T(8,128)S(1)}, u32[]{:S(2)}, u32[]{:S(2)}) collective-permute-start(f32[24,1024]{1,0:T(8,128)S(1)} %get-tuple-element.26.own.refs_5_), channel_id=1, source_target_pairs={{0,1},{1,0},{2,3},{3,2},{4,5},{5,4},{6,7},{7,6},{8,9},{9,8},{10,11... | collective-permute-start | bytes 294920 | tf_op jit(solution)/shard_map/ppermute | solution.py:471
  25.4 23.4 %all-to-all-start.1 = ((f32[32,16,128]{2,1,0:T(8,128)}), f32[32,16,128]{2,1,0:T(8,128)S(1)}, u32[]{:S(2)}, u32[]{:S(2)}) async-start(f32[32,16,128]{2,1,0:T(8,128)} %get-tuple-element.34), calls=%async_computation.1 | async-start | bytes 524288 | tf_op jit(solution)/shard_map/all_to_all | solution.py:133
  38.5 1.3 %collective-permute-start.3 = (f32[16,1024]{1,0:T(8,128)S(1)}, f32[16,1024]{1,0:T(8,128)S(1)}, u32[]{:S(2)}, u32[]{:S(2)}) collective-permute-start(f32[16,1024]{1,0:T(8,128)S(1)} %get-tuple-element.35.own.refs_3_.refs_5_), channel_id=1, source_target_pairs={{0,1},{1,0},{2,3},{3,2},{4,5},{5,4},{6,7},{7,6},{8,9},{9,8},{10,11... | collective-permute-start | bytes 196616 | tf_op jit(solution)/shard_map/ppermute | solution.py:471
  38.8 5.3 %collective-permute-start.2 = (f32[16,1024]{1,0:T(8,128)S(1)}, f32[16,1024]{1,0:T(8,128)S(1)}, u32[]{:S(2)}, u32[]{:S(2)}) collective-permute-start(f32[16,1024]{1,0:T(8,128)S(1)} %get-tuple-element.35.own.refs_3_.refs_5_), channel_id=1, source_target_pairs={{1,2},{3,4},{5,6},{7,8},{9,10},{11,12},{13,14},{2,1},{4,3},{6,5},{... | collective-permute-start | bytes 196616 | tf_op jit(solution)/shard_map/ppermute | solution.py:472
  39.9 4.4 %copy-start = (bf16[2,2,2,512,512]{4,3,2,1,0:T(8,128)(2,1)S(1)}, bf16[2,2,2,512,512]{4,3,2,1,0:T(8,128)(2,1)}, u32[]{:S(2)}) copy-start(bf16[2,2,2,512,512]{4,3,2,1,0:T(8,128)(2,1)} %get-tuple-element.36.blocks) | copy-start | bytes 12582916
  50.6 14.7 %all-to-all-start.2 = ((f32[32,16,128]{2,1,0:T(8,128)}), f32[32,16,128]{2,1,0:T(8,128)S(1)}, u32[]{:S(2)}, u32[]{:S(2)}) async-start(f32[32,16,128]{2,1,0:T(8,128)} %get-tuple-element.39), calls=%async_computation.2 | async-start | bytes 524288 | tf_op jit(solution)/shard_map/all_to_all | solution.py:133
  55.1 5.4 %copy-start.1 = (bf16[2,2,2,512,512]{4,3,2,1,0:T(8,128)(2,1)S(1)}, bf16[2,2,2,512,512]{4,3,2,1,0:T(8,128)(2,1)}, u32[]{:S(2)}) copy-start(bf16[2,2,2,512,512]{4,3,2,1,0:T(8,128)(2,1)} %get-tuple-element.36.blocks) | copy-start | bytes 12582916
  55.1 1.3 %collective-permute-start.5 = (f32[16,1024]{1,0:T(8,128)S(1)}, f32[16,1024]{1,0:T(8,128)S(1)}, u32[]{:S(2)}, u32[]{:S(2)}) collective-permute-start(f32[16,1024]{1,0:T(8,128)S(1)} %get-tuple-element.40.own.refs_3_), channel_id=1, source_target_pairs={{0,1},{1,0},{2,3},{3,2},{4,5},{5,4},{6,7},{7,6},{8,9},{9,8},{10,11... | collective-permute-start | bytes 196616 | tf_op jit(solution)/shard_map/ppermute | solution.py:471
  55.4 5.0 %collective-permute-start.4 = (f32[16,1024]{1,0:T(8,128)S(1)}, f32[16,1024]{1,0:T(8,128)S(1)}, u32[]{:S(2)}, u32[]{:S(2)}) collective-permute-start(f32[16,1024]{1,0:T(8,128)S(1)} %get-tuple-element.40.own.refs_3_), channel_id=1, source_target_pairs={{1,2},{3,4},{5,6},{7,8},{9,10},{11,12},{13,14},{2,1},{4,3},{6,5},{... | collective-permute-start | bytes 196616 | tf_op jit(solution)/shard_map/ppermute | solution.py:472

commit v7 on v6

--- a/solution.py
+++ b/solution.py
@@ -135,6 +135,9 @@
     field_shape = shape((vec, width), f32)
     couple_rows = (groups - 1) * coarse
     far_rows = leaves * cols
+    pieces = vec // 2
+    wide = (pieces + 2) * cols
+    piece = lambda k: slice(k * cols, (k + 1) * cols)
     limit = max(6000, far_rows * 3 // 2)
     leaf_slice = lambda j: slice(j * leaf_size, (j + 1) * leaf_size)
 
@@ -161,11 +164,18 @@
             axis=1,
         )
 
+    def put_rows(block, values):
+        if block.shape[0] == vec:
+            block[...] = values
+        else:
+            for k in range(pieces):
+                block[:, piece(k)] = values[2 * k : 2 * k + 2]
+
     def send_all(copies, out, own, up, coeffs, transfer, group):
-        own[:vec] = coeffs
+        put_rows(own, coeffs)
         for i in range(leaves):
             copies.start(("own", i), own, out.at[group * leaves + i])
-        up[:vec] = dot3(coeffs, transfer[0], transfer[1])
+        put_rows(up, dot3(coeffs, transfer[0], transfer[1]))
         for t in range(1, groups):
             first = lax.rem(group + t, groups) * leaves
             for i in range(leaves):
@@ -186,11 +196,12 @@
         copies.start("coarse", coarse_in, coarse_points)
         copies.start("near_lists", near_lists_in, near_lists)
         copies.start("inter_lists", inter_lists_in, inter_lists)
-        own[vec:] = jnp.zeros((SUB, cols), f32)
-        up[vec:] = jnp.zeros((SUB, cols), f32)
+        up[:, piece(pieces)] = jnp.zeros((2, cols), f32)
+        up[:, piece(pieces + 1)] = jnp.zeros((2, cols), f32)
         copies.wait("points", "skel")
         stacked[vec:] = jnp.zeros((SUB, width), f32)
         stacked[vec : vec + 3] = points[...]
+        all_spots = []
         for j in range(per_dev):
             places = lax.broadcasted_iota(jnp.int32, (leaf_size, rank), 0)
             pick = (places == skel[j : j + 1, :]).astype(f32).astype(bf16)
@@ -199,7 +210,10 @@
             ).astype(bf16)
             spots = jnp.dot(parts, pick, preferred_element_type=f32)
             spots = spots[:SUB] + spots[SUB : 2 * SUB] + spots[2 * SUB :]
-            own[vec:, j * rank : (j + 1) * rank] = spots
+            all_spots.append(spots)
+        all_spots = jnp.concatenate(all_spots, axis=1)
+        own[:, piece(pieces)] = all_spots[:2]
+        own[:, piece(pieces + 1)] = all_spots[2:4]
         copies.wait("interp", "field")
         for j in range(per_dev):
             interp[0, j], interp[1, j] = split(whole_interp[j])
@@ -212,7 +226,7 @@
     payload, stacked, interp, transfer, coarse_points, near_lists, inter_lists = call(
         start_body,
         (
-            shape((devices, vec + SUB, cols), f32),
+            shape((devices, 2, wide), f32),
             shape((vec + SUB, width), f32),
             shape((2, *interp.shape), bf16),
             shape((2, *transfer.shape), bf16),
@@ -227,8 +241,8 @@
             pltpu.VMEM((per_dev, rank), jnp.int32),
             pltpu.VMEM(interp.shape, f32),
             pltpu.VMEM(transfer.shape, f32),
-            pltpu.VMEM((vec + SUB, cols), f32),
-            pltpu.VMEM((vec + SUB, cols), f32),
+            pltpu.VMEM((2, wide), f32),
+            pltpu.VMEM((2, wide), f32),
             pltpu.SemaphoreType.DMA((8 + devices,)),
         ],
         flops=10**7,
@@ -248,6 +262,11 @@
     blocks_shape = (3 * per_dev, per_dev, 2, leaf_size, leaf_size)
     couple_shape = (2, couple_rows, cols)
 
+    mirrored, mirror = (0, 1, 0), (0, 0, 1)
+
+    def both_ways(place, lists):
+        return jnp.logical_and(hit(place, lists, *mirrored), hit(place, lists, *mirror))
+
     def near_first_body(
         lists, inter_lists, own, pair, other, coarse_points, transfer,
         near, blocks_out, other_out, couple, marks,
@@ -258,17 +277,21 @@
         for leaf in range(per_dev):
             targets[leaf] = target_factors(coordinates(own[vec : vec + 3, leaf_slice(leaf)], origin))
             total[leaf] = jnp.zeros((vec, leaf_size), f32)
-        count = jnp.int32(0)
-        for i, (kind, j, leaf) in enumerate(entries):
-            window = (own, pair, other)[kind]
-            if leaf == 0:
+        for kind, window in enumerate((own, pair, other)):
+            for j in range(per_dev):
                 source = kind * per_dev + j
                 factors[source] = source_factors(
                     coordinates(window[vec : vec + 3, leaf_slice(j)], origin)
                 )
                 fields[source] = jnp.concatenate(split(window[:vec, leaf_slice(j)]), axis=0)
-            order[count] = i
-            count = count + hit(place, lists, kind, j, leaf).astype(jnp.int32)
+        twice = both_ways(place, lists)
+        count = jnp.int32(0)
+        for entry in [mirror] + [entry for entry in entries if entry != mirror]:
+            found = hit(place, lists, *entry)
+            if entry == mirrored:
+                found = jnp.logical_and(found, jnp.logical_not(twice))
+            order[count] = entries.index(entry)
+            count = count + found.astype(jnp.int32)
 
         inner_entries = 2 * per_dev * per_dev
 
@@ -317,38 +340,6 @@
             both = jnp.dot(field, buffer[0], preferred_element_type=f32)
             rest = jnp.dot(field[:vec], buffer[1], preferred_element_type=f32)
             total[leaf] += both[:vec] + both[vec:] + rest
-
-        make(0, even)
-        out_start(0, even, 0)
-
-        def turn(i, buffer, side, last):
-            @pl.when(i >= 2)
-            def _():
-                out_wait(i - 2, buffer, side)
-
-            make(i, buffer)
-            use(i - 1, last)
-            out_start(i, buffer, side)
-
-        def two(t, _):
-            turn(2 * t + 1, odd, 1, even)
-
-            @pl.when(2 * t + 2 < count)
-            def _():
-                turn(2 * t + 2, even, 0, odd)
-
-            return 0
-
-        lax.fori_loop(0, count // 2, two, 0)
-        ends_even = lax.rem(count, 2) == 1
-
-        @pl.when(ends_even)
-        def _():
-            use(count - 1, even)
-
-        @pl.when(jnp.logical_not(ends_even))
-        def _():
-            use(count - 1, odd)
 
         group = place[1]
         mine = coarse_points[:, group]
@@ -367,6 +358,47 @@
                 chosen = jnp.logical_and(row_leaf == inter_lists[j, s], lane_leaf == j)
                 mark = jnp.where(chosen, 1.0, mark)
         marks[...] = mark
+        make(0, even)
+        out_start(0, even, 0)
+
+        @pl.when(twice)
+        def _():
+            across = lambda a, b: lax.dot_general(
+                a, b, (((1,), (1,)), ((), ())), preferred_element_type=f32
+            )
+            both = across(fields[1], even[0])
+            total[0] += both[:vec] + both[vec:] + across(fields[1, :vec], even[1])
+
+
+        def turn(i, buffer, side, last):
+            @pl.when(i >= 2)
+            def _():
+                out_wait(i - 2, buffer, side)
+
+            make(i, buffer)
+            use(i - 1, last)
+            out_start(i, buffer, side)
+
+        def two(t, _):
+            turn(2 * t + 1, odd, 1, even)
+
+            @pl.when(2 * t + 2 < count)
+            def _():
+                turn(2 * t + 2, even, 0, odd)
+
+            return 0
+
+        lax.fori_loop(0, count // 2, two, 0)
+        ends_even = lax.rem(count, 2) == 1
+
+        @pl.when(ends_even)
+        def _():
+            use(count - 1, even)
+
+        @pl.when(jnp.logical_not(ends_even))
+        def _():
+            use(count - 1, odd)
+
         for leaf in range(per_dev):
             near[:, leaf_slice(leaf)] = total[leaf]
         last_even = jnp.where(ends_even, count - 1, count - 2)
@@ -416,6 +448,9 @@
 
             place = whereabouts()
             hits = [hit(place, lists, *entry) for entry in chosen]
+            twice = both_ways(place, lists)
+            at = chosen.index(mirrored)
+            hits[at] = jnp.logical_and(hits[at], jnp.logical_not(twice))
             for (kind, j, leaf), found in zip(chosen, hits, strict=True):
 
                 @pl.when(found)
@@ -434,6 +469,14 @@
                         blocks[block, leaf, 0],
                         blocks[block, leaf, 1],
                     )
+
+                if (kind, j, leaf) == mirrored:
+
+                    @pl.when(twice)
+                    def _():
+                        near[:, leaf_slice(0)] += dot3_nt(
+                            own[:, leaf_slice(1)], blocks[0, 1, 0], blocks[0, 1, 1]
+                        )
 
         return call(
             body,
@@ -472,12 +515,22 @@
         other = lax.ppermute(field, "leaf", outer)
         return pair, other
 
-    def build_far(place, marks, received, origin, far):
+    def build_far(place, marks, received, far):
         group, leaf = place[1], place[0]
-        target = target_factors(coordinates(received[group * leaves + leaf, vec : vec + 3], origin))
+
+        def spots_of(i):
+            at = group * leaves + i
+            first = received[at, :, piece(pieces)]
+            return [first[0:1], first[1:2], received[at, :, piece(pieces + 1)][0:1]]
+
+        mine = spots_of(leaf)
+        origin = [x[:, :1] for x in mine]
+        scaled = lambda spots: [
+            (x - o) * kappa_scale for x, o in zip(spots, origin, strict=True)
+        ]
+        target = target_factors(scaled(mine))
         for i in range(leaves):
-            spots = received[group * leaves + i, vec : vec + 3]
-            kernel = matern(source_factors(coordinates(spots, origin)), target)
+            kernel = matern(source_factors(scaled(spots_of(i))), target)
             for h in range(per_dev):
                 m = i * per_dev + h
                 at = slice(m * rank, (m + 1) * rank)
@@ -498,17 +551,27 @@
         place = whereabouts()
         group = place[1]
         if step == 1:
-            far = refs.pop(0)
-            origin = received[group * leaves + place[0], vec : vec + 3][:, :1]
-            build_far(place, marks, received, origin, far)
+            far, rows = refs.pop(0), refs.pop()
+            build_far(place, marks, received, far)
             far[:, far_rows:] = couple[...]
-        parts = [received[group * leaves + i, :vec] for i in range(leaves)]
+            for i in range(leaves):
+                for k in range(pieces):
+                    rows[i, 2 * k : 2 * k + 2] = received[group * leaves + i, :, piece(k)]
+        else:
+            rows = received
+        first = 0 if step == 1 else group * leaves
+        parts = [rows[first + i] for i in range(leaves)]
         for t in range(1, groups):
             first = lax.rem(group + t, groups) * leaves
-            sums = [received[first + i, :vec] for i in range(leaves)]
+            sums = [received[first + i] for i in range(leaves)]
             while len(sums) > 1:
                 sums = [sum(sums[i : i + 2]) for i in range(0, len(sums), 2)]
-            parts += sums
+            if step == 1:
+                for k in range(pieces):
+                    rows[leaves, 2 * k : 2 * k + 2] = sums[0][:, piece(k)]
+                parts.append(rows[leaves])
+            else:
+                parts += sums
         down = dot3(jnp.concatenate(parts, axis=1), far[0], far[1])
         news = []
         for j in range(per_dev):
@@ -555,6 +618,8 @@
                 pltpu.VMEM((vec, cols), f32),
                 pltpu.SemaphoreType.DMA((devices,)),
             ]
+            if step == 1:
+                scratch.append(pltpu.VMEM((leaves + 1, vec, cols), f32))
         return call(
             lambda *refs: post_body(step, *refs),
             tuple(outs),

time: 78.6 us -> 76.4 us (0.972)
  Pallas kernels: 24.2 us -> 23.4 us
where the time goes in v7:
time: 76.4 us; the launch traced here: 75.8 us
  starting transfers between devices  30.1 us (39%)
  Pallas kernels  23.4 us (31%)
  blocking collectives  11.2 us (15%)
  waiting for transfers between devices  10.2 us (13%)
  other arithmetic  0.78 us (1%)
    all_to_all x3, starting transfers between devices, on_device(): exchange = lambda x: lax.all_to_all(x, ('grp', 'leaf'), 0, 0, tiled=True)  24.1 us
    all_to_all x1, blocking collectives, on_device(): exchange = lambda x: lax.all_to_all(x, ('grp', 'leaf'), 0, 0, tiled=True)  11.2 us
    all_to_all x3, waiting for transfers between devices, on_device(): exchange = lambda x: lax.all_to_all(x, ('grp', 'leaf'), 0, 0, tiled=True)  8.66 us
    pallas_call x2, Pallas kernels, near_inner(): call(body, field_shape, [SMEM, VMEM, VMEM, HBM], VMEM, scratch=[pltpu.VME...  8.08 us
    pallas_call x1, Pallas kernels, near_first(): call(near_first_body, (field_shape, pltpu.HBM((2 * per_dev, *blocks_shape...  6.72 us
    pallas_call x3, Pallas kernels, post(): call(lambda *refs: post_body(step, *refs), tuple(outs), [VMEM] * len(args...  4.92 us
    ppermute x3, starting transfers between devices, halo(): pair = lax.ppermute(field, 'leaf', inner)  3.82 us
    pallas_call x1, Pallas kernels, on_device(): call(start_body, (shape((devices, 2, wide), f32), shape((vec + SUB, width...  2.47 us
  transfers between devices with their start and end apart: 9, of which 6 were waited for; matrix products, arithmetic and copies ran while one was open for 0% of the time, Pallas kernels for 21%

profile of v7, /device:TPU:0, one launch (start us, length us, event | category | flops | bytes accessed | tf_op | source)
XLA Modules:
  0.0 75.8 jit_solution(16892316359546293094)
XLA Ops:
  0.0 2.5 %shard_map.82 = (f32[32,2,1280]{2,1,0:T(2,128)}, f32[24,1024]{1,0:T(8,128)S(1)}, bf16[2,2,64,512]{3,2,1,0:T(8,128)(2,1)S(1)}, bf16[2,128,128]{2,1,0:T(8,128)(2,1...) custom-call(f32[16,1024]{1,0:T(8,128)} %field_in.1, f32[3,1024]{1,0:T(4,128)} %points_in.1, ...), custom_call_target="tpu_custom_call" | custom-call | flops 10000000 | bytes 1048576 | tf_op jit(solution)/shard_map/pallas_call | solution.py:226
  2.5 7.3 %all-to-all-start = ((f32[32,2,1280]{2,1,0:T(2,128)}), f32[32,2,1280]{2,1,0:T(2,128)S(1)}, u32[]{:S(2)}, u32[]{:S(2)}) async-start(f32[32,2,1280]{2,1,0:T(2,128)} %get-tuple-element.31), calls=%async_computation | async-start | bytes 655360 | tf_op jit(solution)/shard_map/all_to_all | solution.py:133
  9.8 0.7 collective-permute-start.1
  10.5 3.2 %collective-permute-start = (f32[24,1024]{1,0:T(8,128)S(1)}, f32[24,1024]{1,0:T(8,128)S(1)}, u32[]{:S(2)}, u32[]{:S(2)}) collective-permute-start(f32[24,1024]{1,0:T(8,128)S(1)} %get-tuple-element.26.own.refs_5_), channel_id=1, source_target_pairs={{0,1},{1,0},{2,3},{3,2},{4,5},{5,4},{6,7},{7,6},{8,9},{9,8},{10,11... | collective-permute-start | bytes 294920 | tf_op jit(solution)/shard_map/ppermute | solution.py:514
  13.7 0.0 collective-permute-done.1.other
  13.7 0.9 %collective-permute-done.pair = f32[24,1024]{1,0:T(8,128)S(1)} collective-permute-done((f32[24,1024]{1,0:T(8,128)S(1)}, f32[24,1024]{1,0:T(8,128)S(1)}, u32[]{:S(2)}, u32[]{:S(2)}) %collective-permute-start) | collective-permute-done | bytes 98336 | tf_op jit(solution)/shard_map/ppermute | solution.py:514
  14.6 6.7 %shard_map.83 = (f32[16,1024]{1,0:T(8,128)S(1)}, bf16[4,2,2,512,512]{4,3,2,1,0:T(8,128)(2,1)}, bf16[2,2,2,512,512]{4,3,2,1,0:T(8,128)(2,1)}, bf16[2,128,128]{2,1,0:T(8,128)(2,1)S(1)}, f32[32,128]{1,0:T(8,128)S(1)}) custom-call(s32[2,6]{1,0:T(2,128)S(1)} %get-tuple-element.24.lists, s32[2,16]{1,0:T(2,128)S(1)} %get-tuple-element.25.inter_lists, ...), custom_call_target="tpu_custom_call" | custom-call | flops 1000000000 | bytes 1048576 | tf_op jit(solution)/shard_map/pallas_call | solution.py:413
  21.3 0.1 all-to-all-done.refs_2_
  21.5 2.5 %shard_map.84 = (f32[16,1024]{1,0:T(8,128)S(1)}, f32[32,16,128]{2,1,0:T(8,128)}, bf16[2,2176,128]{2,1,0:T(8,128)(2,1)S(1)}) custom-call(f32[32,128]{1,0:T(8,128)S(1)} %get-tuple-element.29.refs_0_, bf16[2,128,128]{2,1,0:T(8,128)(2,1)S(1)} %get-tuple-element.30.refs_1_, f32[32,2,1280]{2,1,0:T(2,128)S(1)} %all-to-all-done.refs_2_, ...), custom_call_target="tpu_custom_call" | custom-call | flops 10000000 | bytes 1048576 | tf_op jit(solution)/shard_map/pallas_call | solution.py:623
  24.0 12.5 %all-to-all-start.1 = ((f32[32,16,128]{2,1,0:T(8,128)}), f32[32,16,128]{2,1,0:T(8,128)S(1)}, u32[]{:S(2)}, u32[]{:S(2)}) async-start(f32[32,16,128]{2,1,0:T(8,128)} %get-tuple-element.34), calls=%async_computation.1 | async-start | bytes 524288 | tf_op jit(solution)/shard_map/all_to_all | solution.py:133
  36.6 0.3 collective-permute-start.3
  36.9 0.7 collective-permute-start.2
  37.5 0.3 collective-permute-done.3.pair
  37.9 0.0 copy-start
  37.9 4.2 %shard_map.85.before = f32[16,1024]{1,0:T(8,128)S(1)} custom-call(s32[2,6]{1,0:T(2,128)S(1)} %get-tuple-element.24.lists, f32[16,1024]{1,0:T(8,128)S(1)} %get-tuple-element.35.own.refs_3_.refs_5_, f32[16,1024]{1,0:T(8,128)S(1)} %collective-permute-done.3.pair, bf16[4,2,2,512,512]{4,3,2,1,0:T(8,128)(2,1)} %get-tuple-element.37.blocks_in), custom_call_target="tpu_custom_call" | custom-call | flops 100000000 | bytes 1048576 | tf_op jit(solution)/shard_map/pallas_call | solution.py:481
  42.1 0.0 collective-permute-done.2.other
  42.1 0.0 copy-done
  42.1 0.6 shard_map.86.refs_2_
  42.7 4.1 %all-to-all-done.1.refs_0_ = f32[32,16,128]{2,1,0:T(8,128)S(1)} async-done(((f32[32,16,128]{2,1,0:T(8,128)}), f32[32,16,128]{2,1,0:T(8,128)S(1)}, u32[]{:S(2)}, u32[]{:S(2)}) %all-to-all-start.1) | async-done | bytes 262176 | tf_op jit(solution)/shard_map/all_to_all | solution.py:133
  46.8 1.8 %shard_map.87 = (f32[16,1024]{1,0:T(8,128)S(1)}, f32[32,16,128]{2,1,0:T(8,128)}) custom-call(f32[32,16,128]{2,1,0:T(8,128)S(1)} %all-to-all-done.1.refs_0_, bf16[2,2,64,512]{3,2,1,0:T(8,128)(2,1)S(1)} %get-tuple-element.32.refs_3_.refs_1_, f32[16,1024]{1,0:T(8,128)S(1)} %shard_map.86.refs_2_, f32[16,1024]{1,0:T(8,128)S(1)} %get-tuple-element.35.own.refs_3_.refs_5_, ...), custom_call_target="tpu_custom_call" | custom-call | flops 10000000 | bytes 1048576 | tf_op jit(solution)/shard_map/pallas_call | solution.py:623
  48.7 4.3 %all-to-all-start.2 = ((f32[32,16,128]{2,1,0:T(8,128)}), f32[32,16,128]{2,1,0:T(8,128)S(1)}, u32[]{:S(2)}, u32[]{:S(2)}) async-start(f32[32,16,128]{2,1,0:T(8,128)} %get-tuple-element.39), calls=%async_computation.2 | async-start | bytes 524288 | tf_op jit(solution)/shard_map/all_to_all | solution.py:133
  52.9 0.0 copy-start.1
  53.0 0.3 collective-permute-start.5
  53.3 0.8 %collective-permute-start.4 = (f32[16,1024]{1,0:T(8,128)S(1)}, f32[16,1024]{1,0:T(8,128)S(1)}, u32[]{:S(2)}, u32[]{:S(2)}) collective-permute-start(f32[16,1024]{1,0:T(8,128)S(1)} %get-tuple-element.40.own.refs_3_), channel_id=1, source_target_pairs={{1,2},{3,4},{5,6},{7,8},{9,10},{11,12},{13,14},{2,1},{4,3},{6,5},{... | collective-permute-start | bytes 196616 | tf_op jit(solution)/shard_map/ppermute | solution.py:515
  54.1 0.2 collective-permute-done.5.pair
  54.3 3.9 %shard_map.88.before = f32[16,1024]{1,0:T(8,128)S(1)} custom-call(s32[2,6]{1,0:T(2,128)S(1)} %get-tuple-element.24.lists, f32[16,1024]{1,0:T(8,128)S(1)} %get-tuple-element.40.own.refs_3_, f32[16,1024]{1,0:T(8,128)S(1)} %collective-permute-done.5.pair, bf16[4,2,2,512,512]{4,3,2,1,0:T(8,128)(2,1)} %get-tuple-element.37.blocks_in), custom_call_target="tpu_custom_call" | custom-call | flops 100000000 | bytes 1048576 | tf_op jit(solution)/shard_map/pallas_call | solution.py:481
  58.2 0.0 collective-permute-done.4.other
  58.2 0.0 copy-done.1
  58.2 0.6 shard_map.89.refs_2_
  58.8 4.4 %all-to-all-done.2.refs_0_ = f32[32,16,128]{2,1,0:T(8,128)S(1)} async-done(((f32[32,16,128]{2,1,0:T(8,128)}), f32[32,16,128]{2,1,0:T(8,128)S(1)}, u32[]{:S(2)}, u32[]{:S(2)}) %all-to-all-start.2) | async-done | bytes 262176 | tf_op jit(solution)/shard_map/all_to_all | solution.py:133
  63.2 0.6 shard_map.90
  63.8 11.2 %all_to_all.20 = f32[32,1,128]{2,1,0:T(1,128)S(1)} all-to-all(f32[32,1,128]{2,1,0:T(1,128)S(1)} %get-tuple-element.42), channel_id=1, replica_groups=mesh['grp'=2,'leaf'=16] {'grp','leaf'}, dimensions={0} | all-to-all | bytes 32768 | tf_op jit(solution)/shard_map/all_to_all | solution.py:133
  75.1 0.1 reduce_sum.9
  75.1 0.7 broadcast_divide_fusion
  (1 shorter events, 0.0 us)
Async XLA Ops:
  2.5 19.0 %all-to-all-start = ((f32[32,2,1280]{2,1,0:T(2,128)}), f32[32,2,1280]{2,1,0:T(2,128)S(1)}, u32[]{:S(2)}, u32[]{:S(2)}) async-start(f32[32,2,1280]{2,1,0:T(2,128)} %get-tuple-element.31), calls=%async_computation | async-start | bytes 655360 | tf_op jit(solution)/shard_map/all_to_all | solution.py:133
  9.8 3.9 %collective-permute-start.1 = (f32[24,1024]{1,0:T(8,128)S(1)}, f32[24,1024]{1,0:T(8,128)S(1)}, u32[]{:S(2)}, u32[]{:S(2)}) collective-permute-start(f32[24,1024]{1,0:T(8,128)S(1)} %get-tuple-element.26.own.refs_5_), channel_id=1, source_target_pairs={{1,2},{3,4},{5,6},{7,8},{9,10},{11,12},{13,14},{2,1},{4,3},{6,5},{... | collective-permute-start | bytes 294920 | tf_op jit(solution)/shard_map/ppermute | solution.py:515
  10.5 4.1 %collective-permute-start = (f32[24,1024]{1,0:T(8,128)S(1)}, f32[24,1024]{1,0:T(8,128)S(1)}, u32[]{:S(2)}, u32[]{:S(2)}) collective-permute-start(f32[24,1024]{1,0:T(8,128)S(1)} %get-tuple-element.26.own.refs_5_), channel_id=1, source_target_pairs={{0,1},{1,0},{2,3},{3,2},{4,5},{5,4},{6,7},{7,6},{8,9},{9,8},{10,11... | collective-permute-start | bytes 294920 | tf_op jit(solution)/shard_map/ppermute | solution.py:514
  24.0 22.8 %all-to-all-start.1 = ((f32[32,16,128]{2,1,0:T(8,128)}), f32[32,16,128]{2,1,0:T(8,128)S(1)}, u32[]{:S(2)}, u32[]{:S(2)}) async-start(f32[32,16,128]{2,1,0:T(8,128)} %get-tuple-element.34), calls=%async_computation.1 | async-start | bytes 524288 | tf_op jit(solution)/shard_map/all_to_all | solution.py:133
  36.6 1.3 %collective-permute-start.3 = (f32[16,1024]{1,0:T(8,128)S(1)}, f32[16,1024]{1,0:T(8,128)S(1)}, u32[]{:S(2)}, u32[]{:S(2)}) collective-permute-start(f32[16,1024]{1,0:T(8,128)S(1)} %get-tuple-element.35.own.refs_3_.refs_5_), channel_id=1, source_target_pairs={{0,1},{1,0},{2,3},{3,2},{4,5},{5,4},{6,7},{7,6},{8,9},{9,8},{10,11... | collective-permute-start | bytes 196616 | tf_op jit(solution)/shard_map/ppermute | solution.py:514
  36.9 5.2 %collective-permute-start.2 = (f32[16,1024]{1,0:T(8,128)S(1)}, f32[16,1024]{1,0:T(8,128)S(1)}, u32[]{:S(2)}, u32[]{:S(2)}) collective-permute-start(f32[16,1024]{1,0:T(8,128)S(1)} %get-tuple-element.35.own.refs_3_.refs_5_), channel_id=1, source_target_pairs={{1,2},{3,4},{5,6},{7,8},{9,10},{11,12},{13,14},{2,1},{4,3},{6,5},{... | collective-permute-start | bytes 196616 | tf_op jit(solution)/shard_map/ppermute | solution.py:515
  37.9 4.2 %copy-start = (bf16[2,2,2,512,512]{4,3,2,1,0:T(8,128)(2,1)S(1)}, bf16[2,2,2,512,512]{4,3,2,1,0:T(8,128)(2,1)}, u32[]{:S(2)}) copy-start(bf16[2,2,2,512,512]{4,3,2,1,0:T(8,128)(2,1)} %get-tuple-element.36.blocks) | copy-start | bytes 12582916
  48.7 14.6 %all-to-all-start.2 = ((f32[32,16,128]{2,1,0:T(8,128)}), f32[32,16,128]{2,1,0:T(8,128)S(1)}, u32[]{:S(2)}, u32[]{:S(2)}) async-start(f32[32,16,128]{2,1,0:T(8,128)} %get-tuple-element.39), calls=%async_computation.2 | async-start | bytes 524288 | tf_op jit(solution)/shard_map/all_to_all | solution.py:133
  52.9 5.3 %copy-start.1 = (bf16[2,2,2,512,512]{4,3,2,1,0:T(8,128)(2,1)S(1)}, bf16[2,2,2,512,512]{4,3,2,1,0:T(8,128)(2,1)}, u32[]{:S(2)}) copy-start(bf16[2,2,2,512,512]{4,3,2,1,0:T(8,128)(2,1)} %get-tuple-element.36.blocks) | copy-start | bytes 12582916
  53.0 1.3 %collective-permute-start.5 = (f32[16,1024]{1,0:T(8,128)S(1)}, f32[16,1024]{1,0:T(8,128)S(1)}, u32[]{:S(2)}, u32[]{:S(2)}) collective-permute-start(f32[16,1024]{1,0:T(8,128)S(1)} %get-tuple-element.40.own.refs_3_), channel_id=1, source_target_pairs={{0,1},{1,0},{2,3},{3,2},{4,5},{5,4},{6,7},{7,6},{8,9},{9,8},{10,11... | collective-permute-start | bytes 196616 | tf_op jit(solution)/shard_map/ppermute | solution.py:514
  53.3 4.9 %collective-permute-start.4 = (f32[16,1024]{1,0:T(8,128)S(1)}, f32[16,1024]{1,0:T(8,128)S(1)}, u32[]{:S(2)}, u32[]{:S(2)}) collective-permute-start(f32[16,1024]{1,0:T(8,128)S(1)} %get-tuple-element.40.own.refs_3_), channel_id=1, source_target_pairs={{1,2},{3,4},{5,6},{7,8},{9,10},{11,12},{13,14},{2,1},{4,3},{6,5},{... | collective-permute-start | bytes 196616 | tf_op jit(solution)/shard_map/ppermute | solution.py:515
